TPU v7x, 32 devices: a whole 2x2x4 slice. The times are simulated.
32 devices in a mesh: dp: 2 (over x), row: 4 (over z), col: 4 (over y, core).
Axes of the slice: x: 2, y: 2, z: 4, core: 2. Of those that a mesh axis runs over, the one named last changes fastest.
Arguments:
- tokens: bfloat16 [16, 768, 1024], P(('dp', 'row'), 'col'), may hold values from -6 to 6
- memory: bfloat16 [16, 20, 768], P(('dp', 'row'), None, 'col'), may hold values from -6 to 6
- block_ids: int32 [16, 1024], P(('dp', 'row')), may hold values from 0 to 7, never falling along the last dimension, each value on 1 to 256 neighbouring positions
- valid: int32 [16], replicated, may hold values from 512 to 1024
- teacher: bfloat16 [16, 768, 1024], P(('dp', 'row'), 'col'), may hold values from -6 to 6
- w_qkv: bfloat16 [12, 147456], P('row', 'col'), may hold values from -0.21875 to 0.21875
- bias_qv: float32 [12, 128], P('row'), may hold values from -3 to 3
- w_out: bfloat16 [768, 768], P('row', 'col'), may hold values from -0.875 to 0.875
- bias_out: float32 [768], P('col'), may hold values from -2 to 2
- ln1_gain: float32 [768], P('col'), may hold values from 0.1 to 1.9
- ln1_bias: float32 [768], P('col'), may hold values from -2 to 2
- w_up: bfloat16 [768, 3072], P('col', 'row'), may hold values from -0.21875 to 0.21875
- bias_up: float32 [3072], P('row'), may hold values from -3 to 3
- w_down: bfloat16 [768, 3072], P('col', 'row'), may hold values from -0.109375 to 0.109375
- bias_down: float32 [768], P('col'), may hold values from -2 to 2
- ln2_gain: float32 [768], P('col'), may hold values from 0.1 to 1.9
- ln2_bias: float32 [768], P('col'), may hold values from -2 to 2
Outputs:
- layer_out: bfloat16 [16, 1044, 768], P(('dp', 'row'), None, 'col')
- grad_tokens: float32 [16, 1024, 768], P(('dp', 'row'), None, 'col')
- grad_memory: float32 [16, 20, 768], P(('dp', 'row'), None, 'col')
- grad_w_qkv: float32 [12, 147456], P('row', 'col')
- grad_bias_qv: float32 [12, 128], P('row')
- grad_w_out: float32 [768, 768], P('row', 'col')
- grad_bias_out: float32 [768], P('col')
- grad_ln1_gain: float32 [768], P('col')
- grad_ln1_bias: float32 [768], P('col')
- grad_w_up: float32 [768, 3072], P('col', 'row')
- grad_bias_up: float32 [3072], P('row')
- grad_w_down: float32 [768, 3072], P('col', 'row')
- grad_bias_down: float32 [768], P('col')
- grad_ln2_gain: float32 [768], P('col')
- grad_ln2_bias: float32 [768], P('col')
Inputs may be any that keep to these rules, and one draw needn't show every extreme that they name: `block_ids`: along each sequence the numbers never fall; each of the 8 numbers covers 1 to 256 consecutive tokens.
All inputs are finite; a program needn't handle non-finite values.
Results may differ from a plain program's by a relative error of at most 0.015.
Values may be sent and summed in bfloat16 or wider, within the bound.
A program may use at most 192 MiB of HBM per device.

v0:
```python
from functools import partial

import jax
import jax.numpy as jnp
from jax import lax
from jax.sharding import PartitionSpec as P

EPSILON = 1e-12
NEGATIVE = -1e30


def gather_feats(shard):
    return lax.all_gather(shard, "col", axis=1, tiled=True)


def back_gather(shard):
    return lax.all_gather(shard, "col", axis=1, tiled=True)


def forward_reduce(partial_rows):
    return lax.psum_scatter(
        partial_rows.astype(jnp.bfloat16), "col", scatter_dimension=1, tiled=True
    ).astype(jnp.float32)


def backward_reduce(partial_rows):
    return lax.psum_scatter(
        partial_rows.astype(jnp.bfloat16), "col", scatter_dimension=1, tiled=True
    ).astype(jnp.float32)


def against(piece_rows, matrix):
    return lax.dot_general(
        piece_rows, matrix, (((1,), (1,)), ((), ())), preferred_element_type=jnp.float32
    )


def column_total(piece_rows):
    unit_row = jnp.ones((1, piece_rows.shape[0]), jnp.bfloat16)
    return jnp.dot(unit_row, piece_rows, preferred_element_type=jnp.float32)[0]


def outer_sum(left_rows, right_rows):
    return lax.dot_general(
        left_rows, right_rows, (((0,), (0,)), ((), ())), preferred_element_type=jnp.float32
    )


def assemble(stacked, row_size, col_size):
    shape = stacked.shape
    grid = stacked.reshape((row_size, col_size) + shape[1:])
    moved = jnp.swapaxes(grid, 1, 2)
    return moved.reshape((row_size * shape[1], col_size * shape[2]) + shape[3:])


def norm_forward(summed, gain, shift, feat_total):
    sum_plain, sum_square = lax.psum(
        (jnp.sum(summed, axis=1), jnp.sum(summed * summed, axis=1)), "col"
    )
    average = sum_plain / feat_total
    inverse = lax.rsqrt(sum_square / feat_total - average * average + EPSILON)
    scaled = (summed - average[:, None]) * inverse[:, None]
    return (scaled * gain + shift, scaled, inverse)


def norm_backward(cotangent, scaled, inverse, gain, feat_total):
    weighted = cotangent * gain
    sum_plain, sum_cross = lax.psum(
        (jnp.sum(weighted, axis=1), jnp.sum(weighted * scaled, axis=1)), "col"
    )
    inner = weighted - sum_plain[:, None] / feat_total - scaled * (sum_cross[:, None] / feat_total)
    return (
        inverse[:, None] * inner,
        jnp.sum(cotangent * scaled, axis=0),
        jnp.sum(cotangent, axis=0),
    )


def visible_rows(token_ids, seq_rows):
    length = token_ids.shape[0]
    memory_rows = (seq_rows - length) // 2
    row_ids = jnp.concatenate(
        [
            jnp.full((memory_rows,), -1, jnp.int32),
            token_ids,
            jnp.full((memory_rows,), length, jnp.int32),
        ]
    )
    return row_ids[None, :] <= row_ids[:, None]


def masked_scores(queries, key_rows, token_ids):
    inv_root = queries.shape[-1] ** (-0.5)
    scores = (
        jnp.einsum("qhe,khe->hqk", queries, key_rows, preferred_element_type=jnp.float32) * inv_root
    )
    visible = visible_rows(token_ids, queries.shape[0])
    return jnp.where(visible[None], scores, NEGATIVE)


def attend(packed):
    queries, key_rows, values, token_ids = packed
    masked = masked_scores(queries, key_rows, token_ids)
    highest = jnp.max(masked, axis=-1, keepdims=True)
    exponent = jnp.exp(masked - highest)
    summed = jnp.sum(exponent, axis=-1, keepdims=True)
    attn_weights = (exponent / summed).astype(jnp.bfloat16)
    mixed_out = jnp.einsum("hqk,khe->qhe", attn_weights, values, preferred_element_type=jnp.float32)
    return (mixed_out.astype(jnp.bfloat16), (highest + jnp.log(summed))[..., 0])


def attend_back(packed):
    queries, key_rows, values, token_ids, log_totals, grad_mixed = packed
    inv_root = queries.shape[-1] ** (-0.5)
    masked = masked_scores(queries, key_rows, token_ids)
    probs_full = jnp.exp(masked - log_totals[..., None])
    attn_weights = probs_full.astype(jnp.bfloat16)
    grad_probs = jnp.einsum("qhe,khe->hqk", grad_mixed, values, preferred_element_type=jnp.float32)
    row_inner = jnp.sum(probs_full * grad_probs, axis=-1, keepdims=True)
    grad_scores = (probs_full * (grad_probs - row_inner)).astype(jnp.bfloat16)
    grad_queries = (
        jnp.einsum("hqk,khe->qhe", grad_scores, key_rows, preferred_element_type=jnp.float32)
        * inv_root
    )
    grad_keys = (
        jnp.einsum("hqk,qhe->khe", grad_scores, queries, preferred_element_type=jnp.float32)
        * inv_root
    )
    grad_values = jnp.einsum(
        "hqk,qhe->khe", attn_weights, grad_mixed, preferred_element_type=jnp.float32
    )
    return (
        grad_queries.astype(jnp.bfloat16),
        grad_keys.astype(jnp.bfloat16),
        grad_values.astype(jnp.bfloat16),
    )


def per_device(
    tokens,
    memory,
    block_ids,
    valid,
    teacher,
    w_qkv,
    bias_qv,
    w_out,
    bias_out,
    ln1_gain,
    ln1_bias,
    w_up,
    bias_up,
    w_down,
    bias_down,
    ln2_gain,
    ln2_bias,
):
    seq_count, feat_cols, length = tokens.shape
    memory_rows = memory.shape[1] // 2
    seq_rows = length + 2 * memory_rows
    row_count = seq_count * seq_rows
    row_size = lax.axis_size("row")
    col_size = lax.axis_size("col")
    row_place = lax.axis_index("row")
    col_place = lax.axis_index("col")
    head_rows = w_qkv.shape[0]
    head_size = bias_qv.shape[1] // 2
    feat_total = feat_cols * col_size
    head_local = head_rows * row_size // col_size
    unit_total = bias_up.shape[0] * row_size
    unit_local = unit_total // col_size
    qkv_blocks = w_qkv.reshape(head_rows, feat_cols, 3 * head_size)
    up_blocks = jnp.transpose(w_up)
    down_blocks = jnp.transpose(w_down)
    whole = (
        lax.all_gather(qkv_blocks[None], ("row", "col"), axis=0, tiled=True),
        lax.all_gather(w_out[None], ("row", "col"), axis=0, tiled=True),
        lax.all_gather(up_blocks[None], ("row", "col"), axis=0, tiled=True),
        lax.all_gather(down_blocks[None], ("row", "col"), axis=0, tiled=True),
    )
    full_qkv = assemble(whole[0], row_size, col_size)
    full_out = assemble(whole[1], row_size, col_size)
    full_up = assemble(whole[2], row_size, col_size)
    full_down = assemble(whole[3], row_size, col_size)
    qkv_heads = lax.dynamic_slice_in_dim(full_qkv, col_place * head_local, head_local, 0)
    out_rows = lax.dynamic_slice_in_dim(
        full_out, col_place * (head_local * head_size), head_local * head_size, 0
    )
    up_rows = lax.dynamic_slice_in_dim(full_up, col_place * unit_local, unit_local, 0)
    down_rows = lax.dynamic_slice_in_dim(full_down, col_place * unit_local, unit_local, 0)
    bias_heads_all, bias_units_all = (
        lax.all_gather(bias_qv, "row", axis=0, tiled=True),
        lax.all_gather(bias_up, "row", axis=0, tiled=True),
    )
    bias_heads = lax.dynamic_slice_in_dim(bias_heads_all, col_place * head_local, head_local, 0)
    bias_units = lax.dynamic_slice_in_dim(bias_units_all, col_place * unit_local, unit_local, 0)
    flat_qkv = jnp.transpose(qkv_heads, (1, 0, 2)).reshape(feat_total, head_local * 3 * head_size)
    token_rows = jnp.swapaxes(tokens, 1, 2)
    inputs = jnp.concatenate(
        [memory[:, :memory_rows], token_rows, memory[:, memory_rows:]], axis=1
    ).reshape(row_count, feat_cols)
    full_in = gather_feats(inputs)
    projected = jnp.dot(full_in, flat_qkv, preferred_element_type=jnp.float32).reshape(
        seq_count, seq_rows, head_local, 3 * head_size
    )
    queries = (projected[..., :head_size] + bias_heads[:, :head_size]).astype(jnp.bfloat16)
    key_rows = projected[..., head_size : 2 * head_size].astype(jnp.bfloat16)
    values = (projected[..., 2 * head_size :] + bias_heads[:, head_size:]).astype(jnp.bfloat16)
    mixed_out, log_totals = lax.map(attend, (queries, key_rows, values, block_ids))
    mixed_rows = mixed_out.reshape(row_count, head_local * head_size)
    attn_out = (
        forward_reduce(jnp.dot(mixed_rows, out_rows, preferred_element_type=jnp.float32)) + bias_out
    )
    norm_one, scaled_one, inverse_one = norm_forward(
        inputs.astype(jnp.float32) + attn_out, ln1_gain, ln1_bias, feat_total
    )
    norm_low = norm_one.astype(jnp.bfloat16)
    full_norm = gather_feats(norm_low)
    gate_pre = against(full_norm, up_rows) + bias_units
    hidden = jax.nn.gelu(gate_pre, approximate=False).astype(jnp.bfloat16)
    branch = (
        forward_reduce(jnp.dot(hidden, down_rows, preferred_element_type=jnp.float32)) + bias_down
    )
    output_rows, scaled_two, inverse_two = norm_forward(
        norm_one + branch, ln2_gain, ln2_bias, feat_total
    )
    output_seq = output_rows.reshape(seq_count, seq_rows, feat_cols)
    offset = lax.axis_index(("dp", "row")) * seq_count
    counts = lax.dynamic_slice_in_dim(valid, offset, seq_count, 0)
    loss_scale = valid.shape[0] * length / jnp.sum(valid).astype(jnp.float32)
    kept_rows = (jnp.arange(length, dtype=jnp.int32)[None, :] < counts[:, None])[..., None]
    mismatch = output_seq[:, memory_rows : memory_rows + length] - jnp.swapaxes(
        teacher, 1, 2
    ).astype(jnp.float32)
    grad_tok = jnp.where(kept_rows, loss_scale * mismatch, 0.0)
    grad_out = jnp.pad(grad_tok, ((0, 0), (memory_rows, memory_rows), (0, 0))).reshape(
        row_count, feat_cols
    )
    grad_two, gain_two, shift_two = norm_backward(
        grad_out, scaled_two, inverse_two, ln2_gain, feat_total
    )
    grad_branch = grad_two.astype(jnp.bfloat16)
    full_branch = back_gather(grad_branch)
    grad_down_rows = outer_sum(hidden, full_branch)
    grad_bias_down = column_total(grad_branch)
    grad_hidden = against(full_branch, down_rows)
    gelu_pull = jax.vjp(partial(jax.nn.gelu, approximate=False), gate_pre)[1]
    grad_gate = gelu_pull(grad_hidden)[0].astype(jnp.bfloat16)
    grad_up_rows = outer_sum(grad_gate, full_norm)
    grad_bias_units = column_total(grad_gate)
    grad_first = grad_two + backward_reduce(
        jnp.dot(grad_gate, up_rows, preferred_element_type=jnp.float32)
    )
    grad_one, gain_one, shift_one = norm_backward(
        grad_first, scaled_one, inverse_one, ln1_gain, feat_total
    )
    grad_attn = grad_one.astype(jnp.bfloat16)
    full_attn = back_gather(grad_attn)
    grad_out_rows = outer_sum(mixed_rows, full_attn)
    grad_bias_out = column_total(grad_attn)
    grad_mixed = against(full_attn, out_rows).astype(jnp.bfloat16)
    grad_mixed = grad_mixed.reshape(seq_count, seq_rows, head_local, head_size)
    grad_queries, grad_keys, grad_values = lax.map(
        attend_back, (queries, key_rows, values, block_ids, log_totals, grad_mixed)
    )
    grad_proj = jnp.concatenate([grad_queries, grad_keys, grad_values], axis=-1).reshape(
        row_count, head_local * 3 * head_size
    )
    grad_flat = outer_sum(full_in, grad_proj).reshape(feat_total, head_local, 3 * head_size)
    grad_heads = jnp.transpose(grad_flat, (1, 0, 2))
    proj_total = column_total(grad_proj).reshape(head_local, 3 * head_size)
    grad_bias_heads = jnp.concatenate(
        [proj_total[:, :head_size], proj_total[:, 2 * head_size :]], axis=1
    )
    grad_in = grad_one + backward_reduce(against(grad_proj, flat_qkv))
    relayed = (
        lax.all_to_all(
            grad_heads.astype(jnp.bfloat16), "col", split_axis=1, concat_axis=0, tiled=True
        ).astype(grad_heads.dtype),
        lax.all_to_all(
            grad_out_rows.astype(jnp.bfloat16), "col", split_axis=1, concat_axis=0, tiled=True
        ).astype(grad_out_rows.dtype),
        lax.all_to_all(
            grad_up_rows.astype(jnp.bfloat16), "col", split_axis=1, concat_axis=0, tiled=True
        ).astype(grad_up_rows.dtype),
        lax.all_to_all(
            grad_down_rows.astype(jnp.bfloat16), "col", split_axis=1, concat_axis=0, tiled=True
        ).astype(grad_down_rows.dtype),
    )
    grid_parts = (
        lax.psum_scatter(
            relayed[0].astype(jnp.bfloat16), "row", scatter_dimension=0, tiled=True
        ).astype(jnp.float32),
        lax.psum_scatter(
            relayed[1].astype(jnp.bfloat16), "row", scatter_dimension=0, tiled=True
        ).astype(jnp.float32),
        lax.psum_scatter(
            relayed[2].astype(jnp.bfloat16), "row", scatter_dimension=0, tiled=True
        ).astype(jnp.float32),
        lax.psum_scatter(
            relayed[3].astype(jnp.bfloat16), "row", scatter_dimension=0, tiled=True
        ).astype(jnp.float32),
    )
    weight_totals = (
        lax.psum(grid_parts[0].astype(jnp.bfloat16), "dp").astype(jnp.float32),
        lax.psum(grid_parts[1].astype(jnp.bfloat16), "dp").astype(jnp.float32),
        lax.psum(grid_parts[2].astype(jnp.bfloat16), "dp").astype(jnp.float32),
        lax.psum(grid_parts[3].astype(jnp.bfloat16), "dp").astype(jnp.float32),
    )
    grad_w_qkv = weight_totals[0].reshape(head_rows, feat_cols * 3 * head_size)
    grad_w_out = weight_totals[1]
    grad_w_up = jnp.transpose(weight_totals[2])
    grad_w_down = jnp.transpose(weight_totals[3])
    heads_pad = lax.dynamic_update_slice_in_dim(
        jnp.zeros((head_local * col_size, 2 * head_size), jnp.float32),
        grad_bias_heads,
        col_place * head_local,
        0,
    )
    units_pad = lax.dynamic_update_slice_in_dim(
        jnp.zeros((unit_total,), jnp.float32), grad_bias_units, col_place * unit_local, 0
    )
    feat_stack = jnp.stack(
        [gain_one, shift_one, gain_two, shift_two, grad_bias_out, grad_bias_down]
    )
    feat_pad = lax.dynamic_update_slice_in_dim(
        jnp.zeros((6, feat_total), jnp.float32), feat_stack, col_place * feat_cols, 1
    )
    small_totals = lax.psum((heads_pad, units_pad, feat_pad), ("dp", "row", "col"))
    grad_bias_qv = lax.dynamic_slice_in_dim(small_totals[0], row_place * head_rows, head_rows, 0)
    grad_bias_up = lax.dynamic_slice_in_dim(
        small_totals[1], row_place * bias_up.shape[0], bias_up.shape[0], 0
    )
    feat_totals = lax.dynamic_slice_in_dim(small_totals[2], col_place * feat_cols, feat_cols, 1)
    grad_seq = grad_in.reshape(seq_count, seq_rows, feat_cols)
    grad_tokens = grad_seq[:, memory_rows : memory_rows + length]
    grad_memory = jnp.concatenate(
        [grad_seq[:, :memory_rows], grad_seq[:, memory_rows + length :]], axis=1
    )
    return (
        output_seq.astype(jnp.bfloat16),
        grad_tokens,
        grad_memory,
        grad_w_qkv,
        grad_bias_qv,
        grad_w_out,
        feat_totals[4],
        feat_totals[0],
        feat_totals[1],
        grad_w_up,
        grad_bias_up,
        grad_w_down,
        feat_totals[5],
        feat_totals[2],
        feat_totals[3],
    )


def solution(mesh):
    in_specs = (
        P(("dp", "row"), "col", None),
        P(("dp", "row"), None, "col"),
        P(("dp", "row"), None),
        P(),
        P(("dp", "row"), "col", None),
        P("row", "col"),
        P("row", None),
        P("row", "col"),
        P("col"),
        P("col"),
        P("col"),
        P("col", "row"),
        P("row"),
        P("col", "row"),
        P("col"),
        P("col"),
        P("col"),
    )
    out_specs = (
        P(("dp", "row"), None, "col"),
        P(("dp", "row"), None, "col"),
        P(("dp", "row"), None, "col"),
        P("row", "col"),
        P("row", None),
        P("row", "col"),
        P("col"),
        P("col"),
        P("col"),
        P("col", "row"),
        P("row"),
        P("col", "row"),
        P("col"),
        P("col"),
        P("col"),
    )
    return jax.shard_map(
        per_device, mesh=mesh, in_specs=in_specs, out_specs=out_specs, check_vma=False
    )
```

profile of v0, /device:TPU:0, one launch (start us, length us, event | category | flops | bytes accessed | tf_op | source)
XLA Modules:
  0.0 976.6 jit_solution(16924794278916850676)
XLA Ops:
  14.5 13.6 %all-gather.3 = f32[4,3,128]{2,1,0:T(4,128)S(1)} all-gather(f32[1,3,128]{2,1,0:T(4,128)S(1)} %bitcast.266), channel_id=1, replica_groups=mesh['dp'=2,'row'=4,'col'=4] {'row'}, dimensions={0}, use_global_device_ids=true | all-gather | bytes 7680 | tf_op jit(solution)/shard_map/all_gather | solution.py:192
  28.2 24.4 %all-gather.24.cloned.1.call-done = bf16[3072,192]{1,0:T(8,128)(2,1)} async-done(((bf16[192,192]{1,0:T(8,128)(2,1)}), bf16[3072,192]{1,0:T(8,128)(2,1)}) %all-gather.24.cloned.1.call-update) | async-done | bytes 1179664 | tf_op jit(solution)/shard_map/all_gather | solution.py:177
  57.5 25.1 %all-gather.14.cloned.1.call-done = bf16[2088,768]{0,1:T(8,128)(2,1)} async-done(((bf16[2088,192]{0,1:T(8,128)(2,1)}), bf16[2088,768]{0,1:T(8,128)(2,1)}) %all-gather.14.cloned.1.call-update) | async-done | bytes 3207184 | tf_op jit(solution)/shard_map/all_gather | solution.py:13
  82.5 8.7 reshape.275
  91.2 47.3 %all-gather.16.cloned.1.call-done = bf16[16,3,192,192]{3,2,1,0:T(8,128)(2,1)} async-done(((bf16[1,3,192,192]{3,2,1,0:T(8,128)(2,1)}), bf16[16,3,192,192]{3,2,1,0:T(8,128)(2,1)}) %all-gather.16.cloned.1.call-update) | async-done | bytes 3538960 | tf_op jit(solution)/shard_map/all_gather | solution.py:176
  138.5 9.7 copy.108
  148.2 7.7 reshape.238
  155.9 4.6 fusion.60
  161.4 51.5 %while.26 = (s32[]{:T(128)}, bf16[2,1044,3,64]{1,3,2,0:T(8,128)(2,1)S(1)}, f32[2,3,1044]{2,1,0:T(4,128)}, bf16[2,1044,3,64]{1,3,2,0:T(8,128)(2,1)S(1)}, s32[2,10...) while((s32[]{:T(128)}, ...), condition=%wide.region_3.4_spmd, body=%wide.region_0.3_spmd.sunk | while | flops 864516608 | bytes 43690424 | solution.py:209
  163.9 8.0 fusion.151
  171.9 7.1 fusion.152
  179.0 7.8 fusion.153
  189.4 8.0 fusion.151
  197.4 7.1 fusion.152
  204.5 7.8 fusion.153
  218.0 4.0 convolution_convert_fusion.3
  223.5 36.4 %reduce-scatter.9.cloned.1.call-done = bf16[2088,192]{0,1:T(8,128)(2,1)} async-done(((bf16[2088,768]{0,1:T(8,128)(2,1)}), bf16[2088,192]{0,1:T(8,128)(2,1)}) %reduce-scatter.9.cloned.1.call-update) | async-done | bytes 801808 | tf_op jit(solution)/shard_map/reduce_scatter | solution.py:21
  261.6 10.3 %all-reduce.5 = (f32[2088]{0:T(1024)S(1)}, f32[2088]{0:T(1024)S(1)}) all-reduce(f32[2088]{0:T(1024)S(1)} %get-tuple-element.158, f32[2088]{0:T(1024)S(1)} %get-tuple-element.157), channel_id=1, replica_groups=mesh['dp'=2,'row'=4,'col'=4] {'col'}, use_global_device_ids=true, to_apply=%region_8.9 | all-reduce | flops 4176 | bytes 33408 | tf_op jit(solution)/shard_map/psum | solution.py:57
  274.6 13.3 %all-gather.4 = f32[4,1,768]{2,1,0:T(1,128)S(1)} all-gather(f32[1,1,768]{2,1,0:T(1,128)S(1)} %reshape.262), channel_id=1, replica_groups=mesh['dp'=2,'row'=4,'col'=4] {'row'}, dimensions={0}, use_global_device_ids=true | all-gather | bytes 15360 | tf_op jit(solution)/shard_map/all_gather | solution.py:193
  288.0 27.5 %all-gather.26.cloned.1.call-done = bf16[12288,192]{0,1:T(8,128)(2,1)} async-done(((bf16[768,192]{0,1:T(8,128)(2,1)}), bf16[12288,192]{0,1:T(8,128)(2,1)}) %all-gather.26.cloned.1.call-update) | async-done | bytes 4718608 | tf_op jit(solution)/shard_map/all_gather | solution.py:178
  315.5 8.2 reshape.243
  323.7 4.3 copy.111
  328.0 3.2 copy.143
  331.2 38.2 %all-gather.28.cloned.1.call-done = bf16[12288,192]{0,1:T(8,128)(2,1)} async-done(((bf16[768,192]{0,1:T(8,128)(2,1)}), bf16[12288,192]{0,1:T(8,128)(2,1)}) %all-gather.28.cloned.1.call-update) | async-done | bytes 4718608 | tf_op jit(solution)/shard_map/all_gather | solution.py:179
  369.4 8.3 reshape.245
  377.7 4.7 copy.112
  385.5 14.0 %all-gather.18.cloned.1.call-done = bf16[2088,768]{0,1:T(8,128)(2,1)} async-done(((bf16[2088,192]{0,1:T(8,128)(2,1)}), bf16[2088,768]{0,1:T(8,128)(2,1)}) %all-gather.18.cloned.1.call-update) | async-done | bytes 3207184 | tf_op jit(solution)/shard_map/all_gather | solution.py:13
  399.5 20.0 %multiply_convert_fusion.1 = (bf16[2088,768]{1,0:T(8,128)(2,1)S(1)}, f32[2088,768]{1,0:T(8,128)}, f32[2088,768]{1,0:T(8,128)}) fusion(f32[768]{0:T(1024)S(1)} %dynamic_slice.67, bf16[2088,768]{0,1:T(8,128)(2,1)} %all-gather.18.cloned.1.call-done, bf16[3072,768]{0,1:T(8,128)(2,1)} %bitcast.237, s32[]{:T(128)S(6)} %select_n.38), kind=kOutput, calls=%fused_computation.65 | convolution fusion | flops 2568941568 | bytes 20560900 | tf_op jit(solution)/shard_map/dot_general | solution.py:33
  421.2 5.9 convolution_convert_fusion.2
  429.2 37.2 %reduce-scatter.11.cloned.1.call-done = bf16[2088,192]{0,1:T(8,128)(2,1)} async-done(((bf16[2088,768]{0,1:T(8,128)(2,1)}), bf16[2088,192]{0,1:T(8,128)(2,1)}) %reduce-scatter.11.cloned.1.call-update) | async-done | bytes 801808 | tf_op jit(solution)/shard_map/reduce_scatter | solution.py:21
  468.7 10.6 %all-reduce.4 = (f32[2088]{0:T(1024)S(1)}, f32[2088]{0:T(1024)S(1)}) all-reduce(f32[2088]{0:T(1024)S(1)} %get-tuple-element.161, f32[2088]{0:T(1024)S(1)} %get-tuple-element.160), channel_id=1, replica_groups=mesh['dp'=2,'row'=4,'col'=4] {'col'}, use_global_device_ids=true, to_apply=%region_13.14 | all-reduce | flops 4176 | bytes 33408 | tf_op jit(solution)/shard_map/psum | solution.py:57
  480.9 3.5 reshape.247
  490.3 4.5 pad.4.clone
  494.8 3.2 reshape.248
  500.5 10.3 %all-reduce.3 = (f32[2088]{0:T(1024)S(1)}, f32[2088]{0:T(1024)S(1)}) all-reduce(f32[2088]{0:T(1024)S(1)} %get-tuple-element.155, f32[2088]{0:T(1024)S(1)} %reduce_sum.143), channel_id=1, replica_groups=mesh['dp'=2,'row'=4,'col'=4] {'col'}, use_global_device_ids=true, to_apply=%region_18.19 | all-reduce | flops 4176 | bytes 33408 | tf_op jit(solution)/shard_map/psum | solution.py:68
  514.1 29.9 %all-gather.20.cloned.1.call-done = bf16[2088,768]{0,1:T(8,128)(2,1)} async-done(((bf16[2088,192]{0,1:T(8,128)(2,1)}), bf16[2088,768]{0,1:T(8,128)(2,1)}) %all-gather.20.cloned.1.call-update) | async-done | bytes 3207184 | tf_op jit(solution)/shard_map/all_gather | solution.py:17
  544.0 10.5 %add_convert_fusion = bf16[2088,768]{1,0:T(8,128)(2,1)S(1)} fusion(f32[2088,768]{1,0:T(8,128)} %get-tuple-element.216, f32[2088,768]{1,0:T(8,128)} %get-tuple-element.241, bf16[2088,768]{0,1:T(8,128)(2,1)} %all-gather.20.cloned.1.call-done, bf16[3072,768]{0,1:T(8,128)(2,1)} %bitcast.240, s32[]{:T(128)S(6)} %select_n.38), kind=kOutput, calls=%fused_computation.64 | convolution fusion | flops 2485555200 | bytes 20557828 | tf_op jit(solution)/shard_map/dot_general | solution.py:33
  556.2 6.0 convolution_convert_fusion.1
  562.3 39.2 %reduce-scatter.13.cloned.1.call-done = bf16[2088,192]{0,1:T(8,128)(2,1)} async-done(((bf16[2088,768]{0,1:T(8,128)(2,1)}), bf16[2088,192]{0,1:T(8,128)(2,1)}) %reduce-scatter.13.cloned.1.call-update) | async-done | bytes 801808 | tf_op jit(solution)/shard_map/reduce_scatter | solution.py:27
  601.5 5.0 multiply_reduce_fusion.3
  606.5 10.3 %all-reduce.2 = (f32[2088]{0:T(1024)S(1)}, f32[2088]{0:T(1024)S(1)}) all-reduce(f32[2088]{0:T(1024)S(1)} %get-tuple-element.153, f32[2088]{0:T(1024)S(1)} %get-tuple-element.156), channel_id=1, replica_groups=mesh['dp'=2,'row'=4,'col'=4] {'col'}, use_global_device_ids=true, to_apply=%region_23.24 | all-reduce | flops 4176 | bytes 33408 | tf_op jit(solution)/shard_map/psum | solution.py:68
  620.3 30.1 %all-gather.22.cloned.1.call-done = bf16[2088,768]{0,1:T(8,128)(2,1)} async-done(((bf16[2088,192]{0,1:T(8,128)(2,1)}), bf16[2088,768]{0,1:T(8,128)(2,1)}) %all-gather.22.cloned.1.call-update) | async-done | bytes 3207184 | tf_op jit(solution)/shard_map/all_gather | solution.py:17
  650.4 3.7 convolution_convert_fusion.4
  660.9 68.2 %while.27 = (s32[]{:T(128)}, bf16[2,1044,3,64]{1,3,2,0:T(8,128)(2,1)}, bf16[2,1044,3,64]{1,3,2,0:T(8,128)(2,1)}, bf16[2,1044,3,64]{1,3,2,0:T(8,128)(2,1)}, bf16[...) while((s32[]{:T(128)}, ...), condition=%wide.region_26.27_spmd, body=%wide.region_24.26_spmd.sunk | while | flops 2124194560 | bytes 151329200 | solution.py:263
  661.8 3.4 fusion.162
  665.2 8.2 multiply_reduce_fusion.10
  673.5 8.6 multiply_convert_fusion.3
  682.1 8.3 fusion.165
  695.8 3.4 fusion.162
  699.2 8.2 multiply_reduce_fusion.10
  707.5 8.6 multiply_convert_fusion.3
  716.0 8.3 fusion.165
  736.8 5.0 fusion.72
  742.7 22.5 %all_to_all.75 = bf16[3,768,192]{2,0,1:T(4,128)(2,1)S(1)} all-to-all(bf16[3,768,192]{2,0,1:T(4,128)(2,1)S(1)} %copy.121), channel_id=1, replica_groups=mesh['dp'=2,'row'=4,'col'=4] {'col'}, dimensions={1} | all-to-all | bytes 1769472 | tf_op jit(solution)/shard_map/all_to_all | solution.py:277
  767.6 4.8 convolution_convert_fusion.5
  772.4 18.5 %all_to_all.76 = bf16[768,4,192]{0,2,1:T(8,128)(2,1)S(1)} all-to-all(bf16[768,4,192]{0,2,1:T(8,128)(2,1)S(1)} %bitcast.250), channel_id=1, replica_groups=mesh['dp'=2,'row'=4,'col'=4] {'col'}, dimensions={1} | all-to-all | bytes 2359296 | tf_op jit(solution)/shard_map/all_to_all | solution.py:286
  792.2 4.9 convolution_convert_fusion.6
  797.1 18.4 %all_to_all.77 = bf16[768,4,192]{0,2,1:T(8,128)(2,1)S(1)} all-to-all(bf16[768,4,192]{0,2,1:T(8,128)(2,1)S(1)} %bitcast.251), channel_id=1, replica_groups=mesh['dp'=2,'row'=4,'col'=4] {'col'}, dimensions={1} | all-to-all | bytes 2359296 | tf_op jit(solution)/shard_map/all_to_all | solution.py:283
  820.7 10.6 %all_to_all.78 = bf16[192,4,192]{2,0,1:T(8,128)(2,1)} all-to-all(bf16[192,4,192]{2,0,1:T(8,128)(2,1)S(1)} %copy.124), channel_id=1, replica_groups=mesh['dp'=2,'row'=4,'col'=4] {'col'}, dimensions={1} | all-to-all | bytes 589824 | tf_op jit(solution)/shard_map/all_to_all | solution.py:280
  833.5 22.8 %reduce-scatter.21.cloned.1.call-done = bf16[768,192]{0,1:T(8,128)(2,1)} async-done(((bf16[3072,192]{0,1:T(8,128)(2,1)}), bf16[768,192]{0,1:T(8,128)(2,1)}) %reduce-scatter.21.cloned.1.call-update) | async-done | bytes 294928 | tf_op jit(solution)/shard_map/reduce_scatter | solution.py:297
  856.3 21.5 %reduce-scatter.19.cloned.1.call-done = bf16[192,192]{1,0:T(8,128)(2,1)} async-done(((bf16[768,192]{1,0:T(8,128)(2,1)}), bf16[192,192]{1,0:T(8,128)(2,1)}) %reduce-scatter.19.cloned.1.call-update) | async-done | bytes 73744 | tf_op jit(solution)/shard_map/reduce_scatter | solution.py:294
  877.9 5.8 convolution_convert_fusion
  893.4 39.6 %all-reduce.1 = (f32[12,128]{1,0:T(8,128)S(1)}, f32[6,768]{1,0:T(8,128)S(1)}, f32[3072]{0:T(1024)S(1)}) all-reduce(f32[12,128]{1,0:T(8,128)S(1)} %dynamic_update_slice.26, f32[6,768]{1,0:T(8,128)S(1)} %dynamic_update_slice.27, f32[3072]{0:T(1024)S(1)} %dynamic_update_slice.28), channel_id=1, replica_groups=mesh['dp'=2,'row'=4,'col'=4] {'dp','row','col'}, use_global_device_ids=true, to_apply=%region_30.31 | all-reduce | flops 9216 | bytes 73728 | tf_op jit(solution)/shard_map/psum | solution.py:329
  942.1 17.5 %reduce-scatter.15.cloned.1.call-done = bf16[2088,192]{0,1:T(8,128)(2,1)} async-done(((bf16[2088,768]{0,1:T(8,128)(2,1)}), bf16[2088,192]{0,1:T(8,128)(2,1)}) %reduce-scatter.15.cloned.1.call-update) | async-done | bytes 801808 | tf_op jit(solution)/shard_map/reduce_scatter | solution.py:27
  (285 shorter events, 122.0 us)
Async XLA Ops:
  7.2 45.4 %all-gather.24.cloned.1.call-start = ((), (), s32[]{:S(2)}) async-start(), calls=%async_computation.25 | async-start | bytes 1671168 | tf_op jit(solution)/shard_map/all_gather | solution.py:177
  7.9 74.6 %all-gather.14.cloned.1.call-start = ((), (), s32[]{:S(2)}) async-start(), calls=%async_computation.12 | async-start | bytes 4177920 | tf_op jit(solution)/shard_map/all_gather | solution.py:13
  8.7 4.6 copy-start.30
  9.0 5.5 copy-start.51
  13.3 125.2 %all-gather.16.cloned.1.call-start = ((), (), s32[]{:S(2)}) async-start(), calls=%async_computation.13 | async-start | bytes 5013504 | tf_op jit(solution)/shard_map/all_gather | solution.py:176
  14.4 245.5 %reduce-scatter.9.cloned.1.call-start = ((), (), s32[]{:S(2)}) async-start(), calls=%async_computation.14 | async-start | bytes 4177920 | tf_op jit(solution)/shard_map/reduce_scatter | solution.py:21
  155.9 4.7 copy-start.24
  179.0 7.8 copy-start.31
  179.0 8.4 copy-start.35
  204.5 7.8 copy-start.31
  204.5 8.4 copy-start.35
  212.9 5.1 copy-start.3
  212.9 9.1 copy-start.5
  222.0 37.9 %copy-start.1 = (bf16[2088,192]{0,1:T(8,128)(2,1)S(1)}, bf16[2088,192]{0,1:T(8,128)(2,1)}, u32[]{:S(2)}) copy-start(bf16[2088,192]{0,1:T(8,128)(2,1)} %reshape.236) | copy-start | bytes 2405380
  222.0 37.9 %copy-start.40 = (f32[192]{0:T(256)S(1)}, f32[192]{0:T(256)}, u32[]{:S(2)}) copy-start(f32[192]{0:T(256)} %param.29) | copy-start | bytes 2308
  222.1 49.8 %copy-start.43 = (f32[192]{0:T(256)S(1)}, f32[192]{0:T(256)}, u32[]{:S(2)}) copy-start(f32[192]{0:T(256)} %param.30) | copy-start | bytes 2308
  222.1 49.8 %copy-start.45 = (f32[192]{0:T(256)S(1)}, f32[192]{0:T(256)}, u32[]{:S(2)}) copy-start(f32[192]{0:T(256)} %param.31) | copy-start | bytes 2308
  222.1 52.5 %copy-start.49 = (f32[768]{0:T(1024)S(1)}, f32[768]{0:T(1024)}, u32[]{:S(2)}) copy-start(f32[768]{0:T(1024)} %param.33) | copy-start | bytes 9220
  222.1 93.4 %all-gather.26.cloned.1.call-start = ((), (), s32[]{:S(2)}) async-start(), calls=%async_computation.26 | async-start | bytes 5013504 | tf_op jit(solution)/shard_map/all_gather | solution.py:178
  222.7 146.7 %all-gather.28.cloned.1.call-start = ((), (), s32[]{:S(2)}) async-start(), calls=%async_computation.27 | async-start | bytes 5013504 | tf_op jit(solution)/shard_map/all_gather | solution.py:179
  223.3 176.3 %all-gather.18.cloned.1.call-start = ((), (), s32[]{:S(2)}) async-start(), calls=%async_computation.15 | async-start | bytes 4177920 | tf_op jit(solution)/shard_map/all_gather | solution.py:13
  271.9 345.0 %copy-start.26 = (f32[2088]{0:T(1024)}, f32[2088]{0:T(1024)S(1)}, u32[]{:S(2)}) copy-start(f32[2088]{0:T(1024)S(1)} %get-tuple-element.235) | copy-start | bytes 25060
  271.9 345.0 %copy-start.28 = (f32[2088]{0:T(1024)}, f32[2088]{0:T(1024)S(1)}, u32[]{:S(2)}) copy-start(f32[2088]{0:T(1024)S(1)} %get-tuple-element.236) | copy-start | bytes 25060
  274.6 191.9 %reduce-scatter.11.cloned.1.call-start = ((), (), s32[]{:S(2)}) async-start(), calls=%async_computation.16 | async-start | bytes 4177920 | tf_op jit(solution)/shard_map/reduce_scatter | solution.py:21
  427.1 39.3 %copy-start.8 = (bf16[2088,192]{0,1:T(8,128)(2,1)S(1)}, bf16[2088,192]{0,1:T(8,128)(2,1)}, u32[]{:S(2)}) copy-start(bf16[2088,192]{0,1:T(8,128)(2,1)} %reduce-scatter.9.cloned.1.call-done) | copy-start | bytes 2405380
  427.1 39.3 %copy-start.52 = (f32[192]{0:T(256)S(1)}, f32[192]{0:T(256)}, u32[]{:S(2)}) copy-start(f32[192]{0:T(256)} %param.35) | copy-start | bytes 2308
  427.1 52.2 %copy-start.42 = (f32[192]{0:T(256)S(1)}, f32[192]{0:T(256)}, u32[]{:S(2)}) copy-start(f32[192]{0:T(256)} %param.36) | copy-start | bytes 2308
  427.1 52.2 %copy-start.53 = (f32[192]{0:T(256)S(1)}, f32[192]{0:T(256)}, u32[]{:S(2)}) copy-start(f32[192]{0:T(256)} %param.37) | copy-start | bytes 2308
  427.2 116.8 %all-gather.20.cloned.1.call-start = ((), (), s32[]{:S(2)}) async-start(), calls=%async_computation.17 | async-start | bytes 4177920 | tf_op jit(solution)/shard_map/all_gather | solution.py:17
  513.6 87.9 %reduce-scatter.13.cloned.1.call-start = ((), (), s32[]{:S(2)}) async-start(), calls=%async_computation.18 | async-start | bytes 4177920 | tf_op jit(solution)/shard_map/reduce_scatter | solution.py:27
  562.2 88.1 %all-gather.22.cloned.1.call-start = ((), (), s32[]{:S(2)}) async-start(), calls=%async_computation.19 | async-start | bytes 4177920 | tf_op jit(solution)/shard_map/all_gather | solution.py:17
  616.8 37.3 %copy-start.36 = (f32[2088]{0:T(1024)}, f32[2088]{0:T(1024)S(1)}, u32[]{:S(2)}) copy-start(f32[2088]{0:T(1024)S(1)} %broadcast_multiply_fusion) | copy-start | bytes 25060
  616.8 37.3 %copy-start.38 = (f32[2088]{0:T(1024)}, f32[2088]{0:T(1024)S(1)}, u32[]{:S(2)}) copy-start(f32[2088]{0:T(1024)S(1)} %broadcast_multiply_fusion.1) | copy-start | bytes 25060
  620.0 211.4 %reduce-scatter.17.cloned.1.call-start = ((), (), s32[]{:S(2)}) async-start(), calls=%async_computation.21 | async-start | bytes 1474560 | tf_op jit(solution)/shard_map/reduce_scatter | solution.py:291
  654.1 6.8 copy-start.4
  654.1 6.8 copy-start.6
  654.1 6.8 copy-start.33
  673.5 8.6 copy-start.7
  682.0 8.3 copy-start
  682.0 8.3 copy-start.17
  707.5 8.6 copy-start.7
  716.0 8.3 copy-start
  716.0 8.3 copy-start.17
  766.5 67.0 %reduce-scatter.23.cloned.1.call-start = ((), (), s32[]{:S(2)}) async-start(), calls=%async_computation.24 | async-start | bytes 1474560 | tf_op jit(solution)/shard_map/reduce_scatter | solution.py:300
  772.4 19.8 %copy-start.22 = (bf16[2088,768]{1,0:T(8,128)(2,1)S(1)}, bf16[2088,768]{1,0:T(8,128)(2,1)}, u32[]{:S(2)}) copy-start(bf16[2088,768]{1,0:T(8,128)(2,1)} %copy-done.21) | copy-start | bytes 9621508
  792.2 64.2 %reduce-scatter.21.cloned.1.call-start = ((), (), s32[]{:S(2)}) async-start(), calls=%async_computation.23 | async-start | bytes 1474560 | tf_op jit(solution)/shard_map/reduce_scatter | solution.py:297
  797.1 20.1 %copy-start.13 = (bf16[2088,192]{0,1:T(8,128)(2,1)S(1)}, bf16[2088,192]{0,1:T(8,128)(2,1)}, u32[]{:S(2)}) copy-start(bf16[2088,192]{0,1:T(8,128)(2,1)} %copy-done.12) | copy-start | bytes 2405380
  816.7 61.1 %reduce-scatter.19.cloned.1.call-start = ((), (), s32[]{:S(2)}) async-start(), calls=%async_computation.22 | async-start | bytes 491520 | tf_op jit(solution)/shard_map/reduce_scatter | solution.py:294
  820.3 57.6 %copy-start.15 = (bf16[2088,576]{0,1:T(8,128)(2,1)S(1)}, bf16[2088,576]{0,1:T(8,128)(2,1)}, u32[]{:S(2)}) copy-start(bf16[2088,576]{0,1:T(8,128)(2,1)} %reshape.250) | copy-start | bytes 7216132
  831.4 103.6 %all-reduce.9.cloned.1.call-start = ((), (), s32[]{:S(2)}) async-start(), calls=%async_computation.28 | async-start | bytes 1966080 | tf_op jit(solution)/shard_map/psum | solution.py:305
  877.9 81.7 %reduce-scatter.15.cloned.1.call-start = ((), (), s32[]{:S(2)}) async-start(), calls=%async_computation.20 | async-start | bytes 4177920 | tf_op jit(solution)/shard_map/reduce_scatter | solution.py:27
  885.5 4.8 copy-start.46
  885.5 4.8 copy-start.47
  885.5 4.9 copy-start.48
  885.5 4.9 copy-start.50
  888.6 70.9 %copy-start.2 = (bf16[2088,192]{0,1:T(8,128)(2,1)S(1)}, bf16[2088,192]{0,1:T(8,128)(2,1)}, u32[]{:S(2)}) copy-start(bf16[2088,192]{0,1:T(8,128)(2,1)} %reshape.236) | copy-start | bytes 2405380
  888.6 70.9 %copy-start.9 = (bf16[2088,192]{0,1:T(8,128)(2,1)S(1)}, bf16[2088,192]{0,1:T(8,128)(2,1)}, u32[]{:S(2)}) copy-start(bf16[2088,192]{0,1:T(8,128)(2,1)} %reduce-scatter.9.cloned.1.call-done) | copy-start | bytes 2405380
  888.6 70.9 %copy-start.11 = (f32[2088,192]{0,1:T(8,128)S(1)}, f32[2088,192]{0,1:T(8,128)}, u32[]{:S(2)}) copy-start(f32[2088,192]{0,1:T(8,128)} %get-tuple-element.213) | copy-start | bytes 4810756
  888.6 70.9 %copy-start.27 = (f32[2088]{0:T(1024)S(1)}, f32[2088]{0:T(1024)}, u32[]{:S(2)}) copy-start(f32[2088]{0:T(1024)} %copy-done.26) | copy-start | bytes 25060
  888.6 70.9 %copy-start.29 = (f32[2088]{0:T(1024)S(1)}, f32[2088]{0:T(1024)}, u32[]{:S(2)}) copy-start(f32[2088]{0:T(1024)} %copy-done.28) | copy-start | bytes 25060
  888.6 70.9 %copy-start.37 = (f32[2088]{0:T(1024)S(1)}, f32[2088]{0:T(1024)}, u32[]{:S(2)}) copy-start(f32[2088]{0:T(1024)} %copy-done.36) | copy-start | bytes 25060
  888.7 70.9 %copy-start.39 = (f32[2088]{0:T(1024)S(1)}, f32[2088]{0:T(1024)}, u32[]{:S(2)}) copy-start(f32[2088]{0:T(1024)} %copy-done.38) | copy-start | bytes 25060
  888.7 70.9 %copy-start.41 = (f32[192]{0:T(256)S(1)}, f32[192]{0:T(256)}, u32[]{:S(2)}) copy-start(f32[192]{0:T(256)} %param.29) | copy-start | bytes 2308
  888.7 70.9 %copy-start.44 = (f32[192]{0:T(256)S(1)}, f32[192]{0:T(256)}, u32[]{:S(2)}) copy-start(f32[192]{0:T(256)} %param.30) | copy-start | bytes 2308
  (19 other events, 30.9 us)
Sparse Core Ops, SparseCore 0:
  10.3 42.2 all-gather.23
  54.2 28.3 all-gather.13
  85.4 53.1 all-gather.15
  222.2 37.6 reduce-scatter.8
  262.0 53.4 all-gather.25
  317.6 51.7 all-gather.27
  371.5 27.9 all-gather.17
  427.3 39.0 reduce-scatter.10
  513.7 30.2 all-gather.19
  562.3 39.1 reduce-scatter.12
  620.2 30.1 all-gather.21
  766.6 29.3 reduce-scatter.16
  798.3 27.9 reduce-scatter.22
  828.4 27.9 reduce-scatter.20
  858.5 19.3 reduce-scatter.18
  880.8 37.2 all-reduce.8
  920.5 39.0 reduce-scatter.14
where the time goes:
time: 987 us; the launch traced here: 977 us
  waiting for transfers between devices  413 us (42%)
  blocking collectives  178 us (18%)
  matrix products  162 us (16%)
  local copies, waits for them, and re-layouts  134 us (14%)
  other arithmetic  71.6 us (7%)
  between operations  15.7 us (2%)
    reduce_scatter x2, waiting for transfers between devices, forward_reduce(): lax.psum_scatter(partial_rows.astype(jnp.bfloat16), 'col', scatter_dimens...  73.6 us
    all_gather x2, waiting for transfers between devices, back_gather(): return lax.all_gather(shard, 'col', axis=1, tiled=True)  60 us
    reduce_scatter x2, waiting for transfers between devices, backward_reduce(): lax.psum_scatter(partial_rows.astype(jnp.bfloat16), 'col', scatter_dimens...  56.7 us
    all_gather x1, waiting for transfers between devices, per_device(): lax.all_gather(qkv_blocks[None], ('row', 'col'), axis=0, tiled=True)  47.3 us
    dot_general x4, matrix products, against(): lax.dot_general(piece_rows, matrix, (((1,), (1,)), ((), ())), preferred_e...  40 us
    psum x1, blocking collectives, per_device(): lax.psum((heads_pad, units_pad, feat_pad), ('dp', 'row', 'col'))  39.6 us
    all_gather x2, waiting for transfers between devices, gather_feats(): return lax.all_gather(shard, 'col', axis=1, tiled=True)  39.1 us
    all_gather x1, waiting for transfers between devices, per_device(): lax.all_gather(down_blocks[None], ('row', 'col'), axis=0, tiled=True)  38.2 us
  transfers between devices with their start and end apart: 17, of which 14 were waited for; matrix products, arithmetic and copies ran while one was open for 10% of the time, Pallas kernels for 0%

commit v1 on v0

v1 whole, which is shorter than its diff:
```python
import jax
import jax.numpy as jnp
from jax import lax
from jax.experimental import pallas as pl
from jax.experimental.pallas import tpu as pltpu
from jax.sharding import PartitionSpec as P
BF=jnp.bfloat16; F32=jnp.float32
EPSILON=1e-12
CH=48

def nn(a,b): return lax.dot_general(a,b,(((1,),(0,)),((),())),preferred_element_type=F32)
def nt(a,b): return lax.dot_general(a,b,(((1,),(1,)),((),())),preferred_element_type=F32)

def gelu_pair(v):
    t = pl.reciprocal(1.0 + (0.3275911 * 0.7071067811865476) * jnp.abs(v))
    poly = t * (0.5*0.254829592 + t * (-0.5*0.284496736 + t * (0.5*1.421413741 + t * (-0.5*1.453152027 + t * (0.5*1.061405429)))))
    e = jnp.exp(-0.5 * v * v)
    half = poly * e
    cdf = jnp.where(v >= 0.0, 1.0 - half, half)
    return v * cdf, cdf + v * (e * 0.3989422804014327)

def group_sum(v):
    rows = v.shape[0]
    return jnp.sum(v.reshape(rows // 8, 8, v.shape[1]), axis=0)

def mlp_kernel(half_ref, valid_ref, mixed, x, teach, vec, bup, wa_hbm, wu_hbm, wd_hbm,
               out, g_one, g_attn, vgrad, bupgrad, gu_hbm, gd_hbm,
               tr, wraw, wt, wu, wd, h1, h2, rs1, low, lowt, brt, br, hid, dgl, gg, gu, gd, sem):
    rows, feats = x.shape
    zs = wu.shape[0]
    nb = feats // 256
    copies_a = [pltpu.make_async_copy(wa_hbm.at[z, :, pl.ds(512, 256)], wraw.at[z], sem.at[z]) for z in range(zs)]
    copies_u = [pltpu.make_async_copy(wu_hbm.at[z], wu.at[z], sem.at[zs + z]) for z in range(zs)]
    copies_d = [pltpu.make_async_copy(wd_hbm.at[z], wd.at[z], sem.at[2 * zs + z]) for z in range(zs)]
    for c in copies_a + copies_u + copies_d:
        c.start()
    for c in copies_a:
        c.wait()
    main = teach.shape[1]
    for i in range(main // 128):
        tr[pl.ds(128 * i, 128), :] = teach[:, pl.ds(128 * i, 128)].T
    tr[pl.ds(main, rows - main), :] = jnp.zeros((rows - main, feats), BF)
    low_lane = lax.broadcasted_iota(jnp.int32, (feats, 128), 1) < 64
    for k in range(zs // 2):
        z0, z1 = 2 * k, 2 * k + 1
        wt[:, pl.ds(384 * k, 128)] = wraw[z0, :, pl.ds(128, 128)]
        wt[:, pl.ds(384 * k + 128, 128)] = wraw[z1, :, pl.ds(128, 128)]
        t0 = pltpu.roll(wraw[z0, :, pl.ds(0, 128)].astype(F32), 64, 1)
        t1 = wraw[z1, :, pl.ds(0, 128)].astype(F32)
        wt[:, pl.ds(384 * k + 256, 128)] = jnp.where(low_lane, t0, t1).astype(BF)
    for n in range(nb):
        f = pl.ds(256 * n, 256)
        h1[:, f] = nt(mixed[...], wt[f, :]) + x[:, f].astype(F32) + vec[0:1, f]
    inv = 1.0 / feats

    vgrad[...] = jnp.zeros_like(vgrad)
    bupgrad[...] = jnp.zeros_like(bupgrad)

    def norm1(i, _):
        r = pl.ds(pl.multiple_of(i * CH, 16), CH)
        h = h1[r, :]
        m = jnp.sum(h, axis=1, keepdims=True) * inv
        s = jnp.sum(h * h, axis=1, keepdims=True) * inv
        rstd = lax.rsqrt(s - m * m + EPSILON)
        xhat = (h - m) * rstd
        h1[r, :] = xhat
        rs1[r, :] = jnp.broadcast_to(rstd, (CH, 128))
        low[r, :] = (xhat * vec[1:2, :] + vec[2:3, :]).astype(BF)
        return 0
    lax.fori_loop(0, rows // CH, norm1, 0)
    lowt[...] = low[...].T
    for c in copies_u:
        c.wait()

    def gate(i, _):
        z = i // nb
        f = pl.ds(pl.multiple_of((i % nb) * 256, 256), 256)
        v = nn(low[...], wu[z, :, f]) + bup[z, :, f]
        a, b = gelu_pair(v)
        hid[z, :, f] = a.astype(BF)
        dgl[z, :, f] = b
        return 0
    lax.fori_loop(0, zs * nb, gate, 0)
    for c in copies_d:
        c.wait()

    def down(n, _):
        f = pl.ds(pl.multiple_of(n * 256, 256), 256)
        acc = nt(hid[0], wd[0, f, :])
        for z in range(1, zs):
            acc = acc + nt(hid[z], wd[z, f, :])
        h2[:, f] = acc
        return 0
    lax.fori_loop(0, nb, down, 0)
    scale = vec[6:7, 0:1]
    first = half_ref[0] * main

    def norm2(i, _):
        r = pl.ds(pl.multiple_of(i * CH, 16), CH)
        h = h2[r, :] + (h1[r, :] * vec[1:2, :] + vec[2:3, :]) + vec[3:4, :]
        m = jnp.sum(h, axis=1, keepdims=True) * inv
        s = jnp.sum(h * h, axis=1, keepdims=True) * inv
        rstd = lax.rsqrt(s - m * m + EPSILON)
        xhat = (h - m) * rstd
        o = xhat * vec[4:5, :] + vec[5:6, :]
        out[r, :] = o.astype(BF)
        place = lax.broadcasted_iota(jnp.int32, (CH, 1), 0) + i * CH
        place = jnp.where(place < main, place + first, valid_ref[0])
        go = jnp.where(place < valid_ref[0], scale * (o - tr[r, :].astype(F32)), 0.0)
        a = go * vec[4:5, :]
        m1 = jnp.sum(a, axis=1, keepdims=True) * inv
        m2 = jnp.sum(a * xhat, axis=1, keepdims=True) * inv
        g2 = rstd * (a - m1 - xhat * m2)
        h2[r, :] = g2
        b = g2.astype(BF)
        br[r, :] = b
        vgrad[0] += group_sum(go * xhat)
        vgrad[1] += group_sum(go)
        vgrad[2] += group_sum(b.astype(F32))
        return 0
    lax.fori_loop(0, rows // CH, norm2, 0)
    brt[...] = br[...].T

    def back(i, _):
        z = i // nb
        f = pl.ds(pl.multiple_of((i % nb) * 256, 256), 256)
        gh = nn(br[...], wd[z, :, f])
        g = (gh * dgl[z, :, f]).astype(BF)
        gg[z, :, f] = g
        bupgrad[z, :, f] += group_sum(g.astype(F32))
        gd[z, :, f] = nn(brt[...], hid[z, :, f]).astype(BF)
        gu[z, :, f] = nn(lowt[...], g).astype(BF)
        return 0
    lax.fori_loop(0, zs * nb, back, 0)
    outs = [pltpu.make_async_copy(gd, gd_hbm, sem.at[0]), pltpu.make_async_copy(gu, gu_hbm, sem.at[1])]
    for c in outs:
        c.start()

    def first_grad(n, _):
        f = pl.ds(pl.multiple_of(n * 256, 256), 256)
        acc = h2[:, f]
        for z in range(zs):
            acc = acc + nt(gg[z], wu[z, f, :])
        h2[:, f] = acc
        return 0
    lax.fori_loop(0, nb, first_grad, 0)

    def norm1_back(i, _):
        r = pl.ds(pl.multiple_of(i * CH, 16), CH)
        g = h2[r, :]
        xhat = h1[r, :]
        a = g * vec[1:2, :]
        m1 = jnp.sum(a, axis=1, keepdims=True) * inv
        m2 = jnp.sum(a * xhat, axis=1, keepdims=True) * inv
        g1 = rs1[r, 0:1] * (a - m1 - xhat * m2)
        g_one[r, :] = g1
        b = g1.astype(BF)
        g_attn[r, :] = b
        vgrad[3] += group_sum(g * xhat)
        vgrad[4] += group_sum(g)
        vgrad[5] += group_sum(b.astype(F32))
        return 0
    lax.fori_loop(0, rows // CH, norm1_back, 0)
    for c in outs:
        c.wait()

def mlp(half, valid, mixed, x, teach, vec, bup, wa, wu, wd):
    rows, feats = x.shape; zs = wu.shape[0]
    V = lambda *s, d=BF: pltpu.VMEM(s, d)
    vm = pl.BlockSpec(memory_space=pltpu.VMEM); sm = pl.BlockSpec(memory_space=pltpu.SMEM); an = pl.BlockSpec(memory_space=pl.ANY)
    S = jax.ShapeDtypeStruct
    return pl.pallas_call(mlp_kernel,
        out_shape=(S((rows,feats),BF),S((rows,feats),F32),S((rows,feats),BF),S((6,8,feats),F32),S((zs,8,feats),F32),S(wu.shape,BF),S(wd.shape,BF)),
        in_specs=[sm,sm,vm,vm,vm,vm,vm,an,an,an],
        out_specs=(vm,vm,vm,vm,vm,an,an),
        scratch_shapes=[V(rows,feats),V(zs,feats,256),V(feats,feats),V(*wu.shape),V(*wd.shape),V(rows,feats,d=F32),V(rows,feats,d=F32),V(rows,128,d=F32),V(rows,feats),
            V(feats,rows),V(feats,rows),V(rows,feats),V(zs,rows,feats),V(zs,rows,feats,d=F32),V(zs,rows,feats),V(*wu.shape),V(*wd.shape),pltpu.SemaphoreType.DMA((3*zs,))],
        compiler_params=pltpu.CompilerParams(vmem_limit_bytes=63*2**20),
    )(half,valid,mixed,x,teach,vec,bup,wa,wu,wd)
NEG=-1e30
def tn_lanes(): return lax.broadcasted_iota(jnp.int32,(1,128),1)

def assemble_pairs(w, wp, feats):
    lo = lax.broadcasted_iota(jnp.int32, (feats, 128), 1) < 64
    wp[0] = w[0, :, pl.ds(0, 384)]
    wp[1] = w[1, :, pl.ds(0, 384)]
    a0, a1 = w[0, :, pl.ds(384, 128)].astype(F32), w[1, :, pl.ds(384, 128)].astype(F32)
    wp[2, :, pl.ds(0, 128)] = jnp.where(lo, a0, pltpu.roll(a1, 64, 1)).astype(BF)
    wp[2, :, pl.ds(128, 128)] = jnp.where(lo, pltpu.roll(a0, 64, 1), a1).astype(BF)
    b0, b1 = w[0, :, pl.ds(512, 128)].astype(F32), w[1, :, pl.ds(512, 128)].astype(F32)
    wp[2, :, pl.ds(256, 128)] = jnp.where(lo, b0, pltpu.roll(b1, 64, 1)).astype(BF)

def tiles(rows, length):
    mem = (length, rows - length, True)
    out = []
    for a in range(0, length, 256):
        spans = []
        if a:
            spans.append((0, a, False))
        spans.append((a, min(512, length - a), True))
        out.append((a, 256, spans + [mem]))
    out.append((length, rows - length, [(0, length, True), mem]))
    return out

def scores_of(kt, qm, idk, idq, p, spans):
    out = []
    for k0, kn, masked in spans:
        s = nt(kt[p, pl.ds(k0, kn), :], qm)
        if masked:
            s = jnp.where(idk[pl.ds(k0, kn), 0:1] <= idq, s, NEG)
        out.append(s)
    return out

def attn_fwd_kernel(xt, wa_hbm, bias, idk, idq, x, qt, kt, vt, mixed, lse, w, wp, vtt, ot, sem):
    feats = xt.shape[0]; rows = x.shape[0]; length = xt.shape[1] - 128
    c = pltpu.make_async_copy(wa_hbm, w, sem); c.start()
    for i in range(length // 128):
        x[pl.ds(128 * i, 128), :] = xt[:, pl.ds(128 * i, 128)].T
    x[pl.ds(length, rows - length), :] = xt[:, pl.ds(length, 128)].T[: rows - length, :]
    c.wait()
    assemble_pairs(w, wp, feats)
    rc = rows // 3

    def project(i, _):
        p = i // 3
        r = pl.ds(pl.multiple_of((i % 3) * rc, 16), rc)
        v = nn(x[r, :], wp[p]) + bias[p]
        qt[p, r, :] = (v[:, :128].astype(BF).astype(F32) * 0.125).astype(BF)
        kt[p, r, :] = v[:, 128:256].astype(BF)
        vt[p, r, :] = v[:, 256:].astype(BF)
        return 0
    lax.fori_loop(0, 9, project, 0)

    def pair(p, _):
        vtt[...] = vt[p].T
        for e in range(2):
            lanes = (tn_lanes() < 64) if e == 0 else (tn_lanes() >= 64)
            for q0, qn, spans in tiles(rows, length):
                q = qt[p, pl.ds(q0, qn), :]
                qm = jnp.where(lanes, q, jnp.zeros_like(q))
                ss = scores_of(kt, qm, idk, idq[0:1, pl.ds(q0, qn)], p, spans)
                m = jnp.max(ss[0], axis=0, keepdims=True)
                for s in ss[1:]:
                    m = jnp.maximum(m, jnp.max(s, axis=0, keepdims=True))
                tot, acc = None, None
                for s, (k0, kn, _) in zip(ss, spans):
                    ex = jnp.exp(s - m)
                    t = jnp.sum(ex, axis=0, keepdims=True)
                    o = nn(vtt[pl.ds(64 * e, 64), pl.ds(k0, kn)], ex.astype(BF))
                    tot = t if tot is None else tot + t
                    acc = o if acc is None else acc + o
                ot[pl.ds(64 * e, 64), pl.ds(q0, qn)] = acc / tot
                lse[p, e, :, pl.ds(q0, qn)] = m + jnp.log(tot)
        mixed[p] = ot[...].T.astype(BF)
        return 0
    lax.fori_loop(0, 3, pair, 0)

def attn_fwd(xt, wa, bias, idk, idq, rows):
    feats = xt.shape[0]
    V = lambda *s, d=BF: pltpu.VMEM(s, d)
    vm = pl.BlockSpec(memory_space=pltpu.VMEM); an = pl.BlockSpec(memory_space=pl.ANY)
    S = jax.ShapeDtypeStruct
    t3 = S((3, rows, 128), BF)
    return pl.pallas_call(attn_fwd_kernel,
        out_shape=(S((rows, feats), BF), t3, t3, t3, t3, S((3, 2, 1, rows), F32)),
        in_specs=[vm, an, vm, vm, vm], out_specs=(vm,) * 6,
        scratch_shapes=[V(*wa.shape), V(3, feats, 384), V(128, rows), V(128, rows, d=F32), pltpu.SemaphoreType.DMA],
        compiler_params=pltpu.CompilerParams(vmem_limit_bytes=63*2**20))(xt, wa, bias, idk, idq)

def attn_bwd_kernel(ga, mixed, xt, qt, kt, vt, lse, idk, idq, wa_hbm, gpart, bgrad, gown_hbm, w, wp, wt, gat, gm, gp, dv, dk, dqt, ktt, dd, ro, gown, sem):
    feats = xt.shape[0]; rows = ga.shape[0]; length = xt.shape[1] - 128
    c = pltpu.make_async_copy(wa_hbm, w, sem); c.start()
    gat[...] = ga[...].T
    c.wait()
    assemble_pairs(w, wp, feats)
    wt[:, pl.ds(0, 128)] = w[0, :, pl.ds(640, 128)]
    wt[:, pl.ds(128, 128)] = w[1, :, pl.ds(640, 128)]
    lo = lax.broadcasted_iota(jnp.int32, (feats, 128), 1) < 64
    wt[:, pl.ds(256, 128)] = jnp.where(lo, pltpu.roll(w[0, :, pl.ds(512, 128)].astype(F32), 64, 1), w[1, :, pl.ds(512, 128)].astype(F32)).astype(BF)
    for p in range(3):
        gm[p] = nn(ga[...], wt[:, pl.ds(128 * p, 128)]).astype(BF)

    def pair(p, _):
        ktt[...] = kt[p].T
        prod = (gm[p].astype(F32) * mixed[p].astype(F32)).T
        dd[0:1, :] = jnp.sum(prod[:64, :], axis=0, keepdims=True)
        dd[1:2, :] = jnp.sum(prod[64:, :], axis=0, keepdims=True)
        dv[...] = jnp.zeros_like(dv)
        dk[...] = jnp.zeros_like(dk)
        for e in range(2):
            lanes = (tn_lanes() < 64) if e == 0 else (tn_lanes() >= 64)
            for q0, qn, spans in tiles(rows, length):
                q = qt[p, pl.ds(q0, qn), :]
                qm = jnp.where(lanes, q, jnp.zeros_like(q))
                g = gm[p, pl.ds(q0, qn), :]
                gmm = jnp.where(lanes, g, jnp.zeros_like(g))
                ss = scores_of(kt, qm, idk, idq[0:1, pl.ds(q0, qn)], p, spans)
                l = lse[p, e, :, pl.ds(q0, qn)]
                d = dd[pl.ds(e, 1), pl.ds(q0, qn)]
                acc = None
                for s, (k0, kn, _) in zip(ss, spans):
                    pr = jnp.exp(s - l)
                    dp = nt(vt[p, pl.ds(k0, kn), :], gmm)
                    ds = (pr * (dp - d)).astype(BF)
                    dv[pl.ds(k0, kn), :] += nn(pr.astype(BF), gmm)
                    dk[pl.ds(k0, kn), :] += nn(ds, qm)
                    o = nn(ktt[pl.ds(64 * e, 64), pl.ds(k0, kn)], ds)
                    acc = o if acc is None else acc + o
                dqt[pl.ds(64 * e, 64), pl.ds(q0, qn)] = acc * 0.125
        gp[p, :, pl.ds(0, 128)] = dqt[...].T.astype(BF)
        gp[p, :, pl.ds(128, 128)] = dk[...].astype(BF)
        gp[p, :, pl.ds(256, 128)] = dv[...].astype(BF)
        return 0
    lax.fori_loop(0, 3, pair, 0)
    for p in range(3):
        bgrad[p] = group_sum(gp[p].astype(F32))
    r3 = rows // 3

    def rowsgrad(i, _):
        r = pl.ds(pl.multiple_of(i * r3, 16), r3)
        gpart[r, :] = nt(gp[0, r, :], wp[0]) + nt(gp[1, r, :], wp[1]) + nt(gp[2, r, :], wp[2])
        return 0
    lax.fori_loop(0, 3, rowsgrad, 0)
    fc = 256
    for f0 in range(0, feats, fc):
        f = pl.ds(f0, fc)
        xf = xt[f, pl.ds(0, rows)]
        af = gat[f, :]
        r0 = nn(xf, gp[0]); r1 = nn(xf, gp[1]); r2 = nn(xf, gp[2])
        o = [nn(af, mixed[p]) for p in range(3)]
        lo = lax.broadcasted_iota(jnp.int32, (fc, 128), 1) < 64
        rq, rk, rv = r2[:, :128], r2[:, 128:256], r2[:, 256:]
        sw = lambda a: pltpu.roll(a, 64, 1)
        gown[0, f, pl.ds(0, 384)] = r0.astype(BF)
        gown[1, f, pl.ds(0, 384)] = r1.astype(BF)
        gown[0, f, pl.ds(384, 128)] = jnp.where(lo, rq, sw(rk)).astype(BF)
        gown[1, f, pl.ds(384, 128)] = jnp.where(lo, sw(rq), rk).astype(BF)
        gown[0, f, pl.ds(512, 128)] = jnp.where(lo, rv, sw(o[2])).astype(BF)
        gown[1, f, pl.ds(512, 128)] = jnp.where(lo, sw(rv), o[2]).astype(BF)
        gown[0, f, pl.ds(640, 128)] = o[0].astype(BF)
        gown[1, f, pl.ds(640, 128)] = o[1].astype(BF)
    c = pltpu.make_async_copy(gown, gown_hbm, sem); c.start(); c.wait()

def attn_bwd(ga, mixed, xt, qt, kt, vt, lse, idk, idq, wa):
    feats = xt.shape[0]; rows = ga.shape[0]
    V = lambda *s, d=BF: pltpu.VMEM(s, d)
    vm = pl.BlockSpec(memory_space=pltpu.VMEM); an = pl.BlockSpec(memory_space=pl.ANY)
    S = jax.ShapeDtypeStruct
    return pl.pallas_call(attn_bwd_kernel,
        out_shape=(S((rows, feats), F32), S((3, 8, 384), F32), S(wa.shape, BF)),
        in_specs=[vm] * 9 + [an], out_specs=(vm, vm, an),
        scratch_shapes=[V(*wa.shape), V(3, feats, 384), V(feats, 384), V(feats, rows), V(3, rows, 128), V(3, rows, 384), V(rows, 128, d=F32), V(rows, 128, d=F32),
            V(128, rows, d=F32), V(128, rows), V(8, rows, d=F32), V(8, 128), V(*wa.shape), pltpu.SemaphoreType.DMA],
        compiler_params=pltpu.CompilerParams(vmem_limit_bytes=63*2**20))(ga, mixed, xt, qt, kt, vt, lse, idk, idq, wa)
MESH = pl.DeviceIdType.MESH

class Net:
    def __init__(self, send_sems, recv_sems, local_sems):
        self.ss, self.rs, self.ls = send_sems, recv_sems, local_sems
        self.count, self.locals, self.sent = 0, 0, []
        self.d, self.z, self.c = (lax.axis_index(a) for a in ("dp", "row", "col"))
        self.nd, self.nz = lax.axis_size("dp"), lax.axis_size("row")
        self.y, self.k = self.c // 2, self.c % 2
        self.x = self.d % 2
        self.xp = (self.d + 1 - 2 * self.x, self.z, self.c)
        self.yp = (self.d, self.z, lax.rem(self.c + 2, 4))
        self.kp = (self.d, self.z, self.c + 1 - 2 * self.k)
        self.ykp = (self.d, self.z, 3 - self.c)
        self.zs = [lax.rem(self.z + i, self.nz) for i in range(self.nz)]
        self.zp = [(self.d, zz, self.c) for zz in self.zs]
        self.others = [(lax.rem(self.d + 2 * i, self.nd), self.z, self.c) for i in range(1, self.nd // 2)]

    def barrier(self, peers):
        b = pltpu.get_barrier_semaphore()
        for p in peers:
            pl.semaphore_signal(b, inc=1, device_id=p, device_id_type=MESH)
        pl.semaphore_wait(b, len(peers))

    def send(self, src, dst, dev):
        i = self.count
        self.count += 1
        c = pltpu.make_async_remote_copy(src_ref=src, dst_ref=dst, send_sem=self.ss.at[i], recv_sem=self.rs.at[i], device_id=dev, device_id_type=MESH)
        c.start()
        self.sent.append(c)
        return c

    def local(self, src, dst):
        c = pltpu.make_async_copy(src, dst, self.ls.at[self.locals])
        self.locals += 1
        c.start()
        return c

    def finish(self):
        for c in self.sent:
            c.wait_send()

def gather_kernel(tok, mem, tch, la, lu, ld, ls, xt, tt, wa, wu, wd, sm, ss, rs, lsem):
    n = Net(ss, rs, lsem)
    n.barrier(n.zp[1:] + [n.yp, n.ykp, n.kp, n.xp])
    nz, y, k, c, z = n.nz, n.y, n.k, n.c, n.z
    b = la.shape[0]; hb = b // 2
    length = tok.shape[2]
    oc = lax.rem(c + 2, 4)
    half = n.x * hb
    row = lambda cc, off=0, num=b: pl.ds(pl.multiple_of(cc * b + off, 16), num)
    seq = lambda r: r

    def blk(w, zz, cc):
        return w.at[zz, row(cc)]
    def hlf(w, zz, cc, h):
        return w.at[zz, row(cc, h * hb, hb)]
    mine, theirs = n.x, 1 - n.x
    local = [n.local(tok.at[y], xt.at[row(c), pl.ds(0, length)]), n.local(mem.at[y], xt.at[row(c), pl.ds(length, 128)])]
    t_y = n.send(tok.at[1 - y], xt.at[row(c), pl.ds(0, length)], n.yp)
    m_y = n.send(mem.at[1 - y], xt.at[row(c), pl.ds(length, 128)], n.yp)
    s_z = [n.send(ls, sm.at[z, c], n.zp[i]) for i in range(1, nz)]
    s_y = [n.send(ls, sm.at[z, c], n.yp)]
    s_k = [n.send(ls, sm.at[z, c], n.kp)]
    ha = la.at[pl.ds(pl.multiple_of(half, 16), hb)]
    hu = lu.at[pl.ds(pl.multiple_of(half, 16), hb)]
    a_z = [n.send(ha, hlf(wa, z, c, mine), n.zp[i]) for i in range(1, nz)]
    a_y = [n.send(ha, hlf(wa, z, c, mine), n.yp)]
    t_k = [n.send(tok.at[y], xt.at[row(c), pl.ds(0, length)], n.kp), n.send(mem.at[y], xt.at[row(c), pl.ds(length, 128)], n.kp)]
    a_k = [n.send(la, blk(wa, z, c), n.kp)]
    for w, l in ((wa, la), (wu, lu), (wd, ld)):
        local.append(n.local(l, blk(w, z, c)))
    local.append(n.local(ls, sm.at[z, c]))
    a_x = []
    zz = lambda i: n.zs[(nz - i) % nz]
    def fwd(src, dst_list):
        return [n.send(src, src, d) for d in dst_list]
    for i in range(1, nz):
        a_z[i - 1].wait_recv()
        u = hlf(wa, zz(i), c, mine)
        a_y.append(n.send(u, u, n.yp)); a_x.append(n.send(u, u, n.xp)); a_k.append(n.send(u, u, n.kp))
        s_z[i - 1].wait_recv()
        u = sm.at[zz(i), c]
        s_y.append(n.send(u, u, n.yp)); s_k.append(n.send(u, u, n.kp))
    u_y = n.send(hu, hlf(wu, z, c, mine), n.yp)
    u_z = [n.send(hu, hlf(wu, z, c, mine), n.zp[i]) for i in range(1, nz)]
    u_k = [n.send(lu, blk(wu, z, c), n.kp)]
    d_z = [n.send(ld, blk(wd, z, c), n.zp[i]) for i in range(1, nz)]
    d_y = [n.send(ld, blk(wd, z, c), n.yp)]
    d_k = [n.send(ld, blk(wd, z, c), n.kp)]
    hw = length // 2
    tsl = lambda s, kk: tch.at[s, :, pl.ds(pl.multiple_of(kk * hw, 128), hw)]
    h_y = [n.send(tsl(1 - y, k), tt.at[row(c)], n.yp), n.send(tsl(1 - y, 1 - k), tt.at[row(c)], n.ykp), n.send(tsl(y, 1 - k), tt.at[row(c)], n.kp)]
    local.append(n.local(tsl(y, k), tt.at[row(c)]))
    t_y.wait_recv(); m_y.wait_recv()
    for w_ in (pl.ds(0, length), pl.ds(length, 128)):
        u = xt.at[row(oc), w_]
        t_k.append(n.send(u, u, n.kp))
    for i in range(nz):
        a_y[i].wait_recv()
        u = hlf(wa, zz(i), oc, mine)
        a_x.append(n.send(u, u, n.xp)); a_k.append(n.send(u, u, n.kp))
        s_y[i].wait_recv()
        u = sm.at[zz(i), oc]
        s_k.append(n.send(u, u, n.kp))
    u_x = []
    u_y.wait_recv()
    u = hlf(wu, z, oc, mine)
    u_z2 = [n.send(u, u, n.zp[i]) for i in range(1, nz)]
    u_x.append(n.send(u, u, n.xp)); u_k.append(n.send(u, u, n.kp))
    order = [(i, c) for i in range(1, nz)] + [(i, oc) for i in range(nz)]
    for cp, (i, cc) in zip(a_x, order):
        cp.wait_recv()
        u = hlf(wa, zz(i), cc, theirs)
        a_k.append(n.send(u, u, n.kp))
    for i in range(1, nz):
        u_z[i - 1].wait_recv()
        u = hlf(wu, zz(i), c, mine)
        u_x.append(n.send(u, u, n.xp)); u_k.append(n.send(u, u, n.kp))
    for i in range(1, nz):
        d_z[i - 1].wait_recv()
        u = blk(wd, zz(i), c)
        d_y.append(n.send(u, u, n.yp)); d_k.append(n.send(u, u, n.kp))
    for i in range(1, nz):
        u_z2[i - 1].wait_recv()
        u = hlf(wu, zz(i), oc, mine)
        u_x.append(n.send(u, u, n.xp)); u_k.append(n.send(u, u, n.kp))
    for i in range(nz):
        d_y[i].wait_recv()
        u = blk(wd, zz(i), oc)
        d_k.append(n.send(u, u, n.kp))
    order = [(0, oc)] + [(i, c) for i in range(1, nz)] + [(i, oc) for i in range(1, nz)]
    for cp, (i, cc) in zip(u_x, order):
        cp.wait_recv()
        u = hlf(wu, zz(i), cc, theirs)
        u_k.append(n.send(u, u, n.kp))
    for cp in h_y + t_k + a_k + s_k + u_k + d_k:
        cp.wait_recv()
    for cp in local:
        cp.wait()
    n.finish()

def gather(tok, mem, tch, la, lu, ld, ls, nz):
    b, width = lu.shape
    feats = 4 * b; length = tok.shape[2]
    vm = pl.BlockSpec(memory_space=pltpu.VMEM); an = pl.BlockSpec(memory_space=pl.ANY)
    S = jax.ShapeDtypeStruct
    w = S((nz, feats, width), BF)
    return pl.pallas_call(gather_kernel,
        out_shape=(S((feats, length + 128), BF), S((feats, length // 2), BF), w, w, w, S((nz, 4) + ls.shape, F32)),
        in_specs=[vm] * 7, out_specs=(an,) * 6,
        scratch_shapes=[pltpu.SemaphoreType.DMA((128,)), pltpu.SemaphoreType.DMA((128,)), pltpu.SemaphoreType.DMA((16,))],
        compiler_params=pltpu.CompilerParams(collective_id=1, has_side_effects=True, vmem_limit_bytes=40*2**20))(tok, mem, tch, la, lu, ld, ls)

def add_to(dst, src):
    dst[...] = (dst[...].astype(F32) + src[...].astype(F32)).astype(BF)

def sum_refs(refs):
    acc = refs[0][...].astype(F32)
    for r in refs[1:]:
        acc = acc + r[...].astype(F32)
    return acc

def reduce_kernel(gu, gd, ga, lo, gpart, g1, sv, out4, grad4, fa, fu, fd, svo,
                  hu, hd, ha, ru, rd, ux, ax, uz, uy, ut, dy, dz, dx, df, ay, az, o4, g4, gs, gr, svk, svy, svx, svz, svt, ss, rs, lsem):
    n = Net(ss, rs, lsem)
    n.barrier(n.zp[1:] + [n.yp, n.ykp, n.kp, n.xp] + n.others)
    nz, y, k, c, z, x = n.nz, n.y, n.k, n.c, n.z, n.x
    b = fu.shape[0]; hb = b // 2
    feats = gu.shape[1]
    row = lambda cc: pl.ds(pl.multiple_of(cc * b, 16), b)
    mine = pl.ds(pl.multiple_of(x * hb, 16), hb)
    theirs = pl.ds(pl.multiple_of((1 - x) * hb, 16), hb)
    d_k = [n.send(gd.at[:, row(2 * yy + 1 - k)], rd.at[yy], n.kp) for yy in range(2)]
    u_k = [n.send(gu.at[:, row(2 * yy + 1 - k)], ru.at[yy], n.kp) for yy in range(2)]
    l_d = [n.local(gd.at[:, row(2 * yy + k)], hd.at[yy]) for yy in range(2)]
    l_u = [n.local(gu.at[:, row(2 * yy + k)], hu.at[yy]) for yy in range(2)]
    oz = pl.ds(2 * k, 2)
    a_k = [n.send(ga.at[:, row(2 * yy + 1 - k)], ha.at[yy, oz], n.kp) for yy in range(2)]
    l_a = [n.local(ga.at[:, row(2 * yy + k)], ha.at[yy, oz]) for yy in range(2)]
    s_k = n.send(sv, svk, n.kp)
    rows = lo.shape[0]; main = rows - 16
    gs[pl.ds(0, main), :] = gpart[pl.ds(pl.multiple_of((1 - k) * main, 16), main), :].astype(BF)
    gs[pl.ds(main, 16), :] = gpart[pl.ds(pl.multiple_of(2 * main + (1 - k) * 16, 16), 16), :].astype(BF)
    g_k = n.send(gs, gr, n.kp)

    def split(get, dst):
        def step(i, _):
            r = pl.ds(pl.multiple_of(i * CH, 16), CH)
            v = get(r)
            for cc in range(4):
                dst[cc, r, :] = v[:, cc * b:(cc + 1) * b].astype(BF)
            return 0
        lax.fori_loop(0, rows // CH, step, 0)
    def spread(src, dst):
        l = n.local(src.at[c], dst.at[y, k])
        return l, [n.send(src.at[lax.rem(c + 2, 4)], dst.at[y, k], n.yp), n.send(src.at[3 - c], dst.at[y, k], n.ykp), n.send(src.at[c + 1 - 2 * k], dst.at[y, k], n.kp)]

    for cp in d_k:
        cp.wait_recv()
    for cp in l_d:
        cp.wait()
    zz = lambda i: n.zs[(nz - i) % nz]
    d_y = []
    for i in list(range(1, nz)) + [0]:
        add_to(hd.at[1 - y, n.zs[i]], rd.at[1 - y, n.zs[i]])
        d_y.append(n.send(hd.at[1 - y, n.zs[i]], dy.at[n.zs[i]], n.yp))
    for i in range(nz):
        add_to(hd.at[y, i], rd.at[y, i])
    for cp in u_k:
        cp.wait_recv()
    for cp in l_u:
        cp.wait()
    u_x = []
    for i in list(range(1, nz)) + [0]:
        for yy in range(2):
            add_to(hu.at[yy, n.zs[i]], ru.at[yy, n.zs[i]])
            u_x.append(n.send(hu.at[yy, n.zs[i], theirs], ux.at[yy, n.zs[i]], n.xp))
    l_o = []
    split(lambda r: lo[r, :].astype(F32), o4)
    l, o_s = spread(o4, out4)
    l_o.append(l)
    g_k.wait_recv()

    def total(r):
        return gr[r, :].astype(F32) + g1[r, :]
    def own(i, _):
        r = pl.ds(pl.multiple_of(i * 16, 16), 16)
        src = jnp.where(i < main // 16, k * main + i * 16, 2 * main + k * 16)
        v = gpart[pl.ds(pl.multiple_of(src, 16), 16), :] + gr[r, :].astype(F32) + g1[r, :]
        for cc in range(4):
            g4[cc, r, :] = v[:, cc * b:(cc + 1) * b].astype(BF)
        return 0
    lax.fori_loop(0, rows // 16, own, 0)
    l, g_s = spread(g4, grad4)
    l_o.append(l)
    for cp in a_k:
        cp.wait_recv()
    for cp in l_a:
        cp.wait()
    a_x = []
    for yy in (0, 1):
        for i in list(range(1, nz)) + [0]:
            yv = 1 - y if yy == 0 else y
            a_x.append(n.send(ha.at[yv, n.zs[i], theirs], ax.at[yv, n.zs[i]], n.xp))
    s_k.wait_recv()
    svt[...] = sv[...] + svk[...]
    s_y = n.send(svt, svy, n.yp)
    d_z = []
    for j, i in enumerate(list(range(1, nz)) + [0]):
        d_y[j].wait_recv()
        add_to(hd.at[y, n.zs[i]], dy.at[n.zs[i]])
        if i:
            d_z.append(n.send(hd.at[y, n.zs[i]], dz.at[i], n.zp[i]))
    s_y.wait_recv()
    svo[...] = svt[...] + svy[...]
    s_x = n.send(svo, svx, n.xp)
    u_z = []
    for j, i in enumerate(list(range(1, nz)) + [0]):
        for yy in range(2):
            u_x[2 * j + yy].wait_recv()
            add_to(hu.at[yy, n.zs[i], mine], ux.at[yy, n.zs[i]])
            if i:
                u_z.append(n.send(hu.at[yy, n.zs[i], mine], uz.at[i, yy], n.zp[i]))
    a_y = []
    for j, i in enumerate(list(range(1, nz)) + [0]):
        a_x[j].wait_recv()
        add_to(ha.at[1 - y, n.zs[i], mine], ax.at[1 - y, n.zs[i]])
        a_y.append(n.send(ha.at[1 - y, n.zs[i], mine], ay.at[n.zs[i]], n.yp))
    for j, i in enumerate(list(range(1, nz)) + [0]):
        a_x[nz + j].wait_recv()
        add_to(ha.at[y, n.zs[i], mine], ax.at[y, n.zs[i]])
    for cp in d_z:
        cp.wait_recv()
    df[...] = sum_refs([hd.at[y, z]] + [dz.at[i] for i in range(1, nz)]).astype(BF)
    me = n.d
    d_d = [n.send(df, dx.at[n.d], (lax.rem(n.d + i, n.nd), n.z, n.c)) for i in range(1, n.nd)]
    l_f = n.local(df, dx.at[n.d])
    s_x.wait_recv()
    svt2 = svo[...] + svx[...]
    svz[z] = svt2
    s_z = [n.send(svz.at[z], svz.at[z], n.zp[i]) for i in range(1, nz)]
    for cp in u_z:
        cp.wait_recv()
    for yy in range(2):
        ut[yy] = sum_refs([hu.at[yy, z, mine]] + [uz.at[i, yy] for i in range(1, nz)]).astype(BF)
    u_y = n.send(ut.at[1 - y], uy, n.yp)
    a_z = []
    for j, i in enumerate(list(range(1, nz)) + [0]):
        a_y[j].wait_recv()
        add_to(ha.at[y, n.zs[i], mine], ay.at[n.zs[i]])
        if i:
            a_z.append(n.send(ha.at[y, n.zs[i], mine], az.at[i], n.zp[i]))
    u_y.wait_recv()
    fu[mine, :] = sum_refs([ut.at[y], uy]).astype(BF)
    u_f = n.send(fu.at[mine], fu.at[mine], n.xp)
    for cp in a_z:
        cp.wait_recv()
    fa[mine, :] = sum_refs([ha.at[y, z, mine]] + [az.at[i] for i in range(1, nz)]).astype(BF)
    a_f = n.send(fa.at[mine], fa.at[mine], n.xp)
    l_f.wait()
    for cp in d_d + s_z:
        cp.wait_recv()
    fd[...] = sum_refs([dx.at[i] for i in range(n.nd)])
    acc = svz[0]
    for i in range(1, nz):
        acc = acc + svz[i]
    n.finish()
    svo[...] = acc
    for cp in o_s + g_s + [u_f, a_f]:
        cp.wait_recv()
    for cp in l_o:
        cp.wait()

def reduce(gu, gd, ga, lo, gpart, g1, sv, nz, nd):
    feats, width = gu.shape[1:]
    b = feats // 4; hb = b // 2; rows = lo.shape[0]
    V = lambda *s, d=BF: pltpu.VMEM(s, d)
    vm = pl.BlockSpec(memory_space=pltpu.VMEM); an = pl.BlockSpec(memory_space=pl.ANY)
    S = jax.ShapeDtypeStruct
    o = S((2, 2, rows, b), BF)
    w = S((b, width), BF)
    sm = lambda: V(*sv.shape, d=F32)
    return pl.pallas_call(reduce_kernel,
        out_shape=(o, o, w, w, S((b, width), F32), S(sv.shape, F32)),
        in_specs=[an, an, an, vm, vm, vm, vm], out_specs=(vm,) * 6,
        scratch_shapes=[V(2, nz, b, width)] * 5 + [V(2, nz, hb, width)] * 2 + [V(nz, 2, hb, width), V(hb, width), V(2, hb, width),
            V(nz, b, width), V(nz, b, width), V(nd, b, width), V(b, width), V(nz, hb, width), V(nz, hb, width),
            V(4, rows, b), V(4, rows, b), V(rows, feats), V(rows, feats), sm(), sm(), sm(), V(nz, *sv.shape, d=F32), sm(),
            pltpu.SemaphoreType.DMA((96 + nd,)), pltpu.SemaphoreType.DMA((96 + nd,)), pltpu.SemaphoreType.DMA((16,))],
        compiler_params=pltpu.CompilerParams(collective_id=2, has_side_effects=True, vmem_limit_bytes=63*2**20))(gu, gd, ga, lo, gpart, g1, sv)

def per_device(tokens, memory, block_ids, valid, teacher, w_qkv, bias_qv, w_out, bias_out, ln1_gain, ln1_bias, w_up, bias_up, w_down, bias_down, ln2_gain, ln2_bias):
    _, b, length = tokens.shape
    nd, nz = lax.axis_size("dp"), lax.axis_size("row")
    d, z, c = (lax.axis_index(a) for a in ("dp", "row", "col"))
    y, k = c // 2, c % 2
    feats = 4 * b
    half = memory.shape[1] // 2
    main = length // 2
    rows = length + 32
    wq = w_qkv.reshape(3, b, 192)
    wo = jnp.transpose(w_out)
    la = jnp.concatenate([wq[0, :, :64], wq[1, :, :64], wq[0, :, 64:128], wq[1, :, 64:128], wq[0, :, 128:], wq[1, :, 128:], wq[2], wo[:, 128:], wo[:, :128]], axis=1)
    mem = jnp.pad(jnp.swapaxes(memory, 1, 2), ((0, 0), (0, 0), (0, 128 - 2 * half)))
    ls = jnp.concatenate([jnp.concatenate([bias_out, ln1_gain, ln1_bias, bias_down, ln2_gain, ln2_bias, bias_up]).reshape(-1, 128), bias_qv, jnp.zeros((6, 128), F32)])
    xt, tt, wa, wu, wd, sm = gather(tokens, mem, teacher, la, w_up, w_down, ls, nz)
    fv = 6 * b // 128
    vecs = jnp.swapaxes(sm[0, :, :fv].reshape(4, 6, b), 0, 1).reshape(6, feats)
    scale = (valid.shape[0] * length) / jnp.sum(valid).astype(F32)
    vec = jnp.concatenate([vecs, jnp.full((2, feats), scale, F32)])
    bup = sm[:, 0, fv:fv + 6].reshape(nz, 1, 6 * 128)
    bq = lax.dynamic_slice_in_dim(sm[:, 0, fv + 6:fv + 9], 2 * k, 2, 0)
    zero = jnp.zeros((128,), F32)
    def pair_bias(h0, h1):
        return jnp.concatenate([h0[:64], h1[:64], zero, h0[64:], h1[64:]])
    bias = jnp.stack([pair_bias(bq[0, 0], bq[0, 1]), pair_bias(bq[1, 0], bq[1, 1]), pair_bias(bq[0, 2], bq[1, 2])])[:, None]
    ids = lax.dynamic_index_in_dim(block_ids, y, 0, keepdims=False)
    ids = jnp.concatenate([ids, jnp.full((half,), -1, jnp.int32), jnp.full((half,), length, jnp.int32), jnp.full((32 - 2 * half,), 2 * length, jnp.int32)])
    idk = jnp.broadcast_to(ids[:, None], (rows, 128))
    wown = lax.dynamic_slice_in_dim(wa, 2 * k, 2, 0)
    x, qt, kt, vt, mixed, lse = attn_fwd(xt, wown, bias, idk, ids[None], rows)
    def rows_of(a, kk, axis=0):
        return jnp.concatenate([lax.dynamic_slice_in_dim(a, kk * main, main, axis), lax.dynamic_slice_in_dim(a, length + kk * 16, 16, axis)], axis)
    swap = [(0, 1), (1, 0), (2, 3), (3, 2)]
    got = lax.ppermute(rows_of(mixed, 1 - k, 1), "col", swap)
    own = rows_of(mixed, k, 1)
    first = jnp.where(k == 0, own, got)
    second = jnp.where(k == 0, got, own)
    mixed_rows = jnp.concatenate([first[0], first[1], first[2], second[0], second[1], second[2]], axis=1)
    count = lax.dynamic_index_in_dim(valid, (d * nz + z) * 2 + y, 0)
    out, g_one, g_attn, vgrad, bupgrad, gu, gd = mlp(k[None], count, mixed_rows, rows_of(x, k), tt, vec, bup, wa, wu, wd)
    other = lax.ppermute(g_attn, "col", swap)
    first = jnp.where(k == 0, g_attn, other)
    second = jnp.where(k == 0, other, g_attn)
    ga = jnp.concatenate([first[:main], second[:main], first[main:], second[main:]])
    gpart, bgrad, gown = attn_bwd(ga, mixed, xt, qt, kt, vt, lse, idk, ids[None], wown)
    bg = jnp.sum(bgrad, axis=1)[None]
    bg = jnp.where((jnp.arange(2) == k)[:, None, None], bg, 0.0).reshape(3, feats)
    sv = jnp.concatenate([jnp.sum(vgrad, axis=1), jnp.sum(bupgrad, axis=1), bg, jnp.zeros((3, feats), F32)])
    out4, grad4, fa, fu, fd, sv = reduce(gu, gd, gown, out, gpart, g_one, sv, nz, nd)
    layer_out = jnp.concatenate([out4[:, 0, main:main + half], out4[:, 0, :main], out4[:, 1, :main], out4[:, 0, main + half:], out4[:, 1, main:main + 2 * half - 16]], axis=1)
    grad_tokens = grad4[:, :, :main].reshape(2, length, b).astype(F32)
    grad_memory = jnp.concatenate([grad4[:, 0, main:], grad4[:, 1, main:main + 2 * half - 16]], axis=1).astype(F32)
    fa = fa.astype(F32)
    g0 = jnp.concatenate([fa[:, 0:64], fa[:, 128:192], fa[:, 256:320]], axis=1)
    g1 = jnp.concatenate([fa[:, 64:128], fa[:, 192:256], fa[:, 320:384]], axis=1)
    grad_w_qkv = jnp.stack([g0, g1, fa[:, 384:576]]).reshape(3, b * 192)
    grad_w_out = jnp.transpose(jnp.concatenate([fa[:, 640:768], fa[:, 576:640]], axis=1))
    hb = sv[10:13].reshape(2, 3, 384)
    hb = lax.dynamic_index_in_dim(hb, z // 2, 0, keepdims=False)
    zl = z % 2
    two = lax.dynamic_index_in_dim(hb, zl, 0, keepdims=False)
    last = hb[2]
    pick = lambda r, e: jnp.concatenate([r[64 * e:64 * e + 64], r[256 + 64 * e:320 + 64 * e]])
    grad_bias_qv = jnp.stack([pick(two, 0), pick(two, 1), jnp.where(zl == 0, pick(last, 0), pick(last, 1))])
    fvec = lax.dynamic_slice_in_dim(sv[:6], c * b, b, 1)
    grad_bias_up = lax.dynamic_index_in_dim(sv[6:10], z, 0, keepdims=False)
    return (layer_out, grad_tokens, grad_memory, grad_w_qkv, grad_bias_qv, grad_w_out, fvec[5], fvec[3], fvec[4], fu.astype(F32), grad_bias_up, fd, fvec[2], fvec[0], fvec[1])

def solution(mesh):
    rows, feat = ("dp", "row"), "col"
    in_specs = (P(rows, feat, None), P(rows, None, feat), P(rows, None), P(), P(rows, feat, None), P("row", feat), P("row", None), P("row", feat), P(feat), P(feat), P(feat), P(feat, "row"), P("row"), P(feat, "row"), P(feat), P(feat), P(feat))
    out_specs = (P(rows, None, feat), P(rows, None, feat), P(rows, None, feat), P("row", feat), P("row", None), P("row", feat), P(feat), P(feat), P(feat), P(feat, "row"), P("row"), P(feat, "row"), P(feat), P(feat), P(feat))
    return jax.shard_map(per_device, mesh=mesh, in_specs=in_specs, out_specs=out_specs, check_vma=False)
```

time: 987 us -> 356 us (0.36)
  waiting for transfers between devices: 413 us -> 0.52 us
  Pallas kernels: 0 us -> 301 us
  blocking collectives: 178 us -> 0 us
  matrix products: 162 us -> 0 us
  local copies, waits for them, and re-layouts: 134 us -> 38.2 us
  other arithmetic: 71.6 us -> 11.8 us
  between operations: 15.7 us -> 2.09 us
    pallas_call x0 -> x5, Pallas kernels: none -> 301 us  [the longest x1 117 us: reduce(): pl.pallas_call(reduce_kernel, out_shape=(o, o, w, w, S((b, width), F32),...]
    all_gather x8 -> x0, waiting for transfers between devices: 237 us -> none  [the longest x2 60 us: back_gather(): return lax.all_gather(shard, 'col', axis=1, tiled=True)]
    reduce_scatter x8 -> x0, waiting for transfers between devices: 175 us -> none  [the longest x2 73.6 us: forward_reduce(): lax.psum_scatter(partial_rows.astype(jnp.bfloat16), 'col', scatter_dimens...]
    dot_general x30 -> x0, matrix products: 162 us -> none  [the longest x4 40 us: against(): lax.dot_general(piece_rows, matrix, (((1,), (1,)), ((), ())), preferred_e...]
    psum x5 -> x0, blocking collectives: 81 us -> none  [the longest x1 39.6 us: per_device(): lax.psum((heads_pad, units_pad, feat_pad), ('dp', 'row', 'col'))]
    all_to_all x4 -> x0, blocking collectives: 70.1 us -> none  [the longest x1 22.5 us: per_device(): lax.all_to_all(grad_heads.astype(jnp.bfloat16), 'col', split_axis=1, conc...]
    reshape x18 -> x3, local copies, waits for them, and re-layouts: 71.2 us -> 1.38 us  [the longest x1 1.28 us: per_device(): wq = w_qkv.reshape(3, b, 192)]
    all_gather x2 -> x0, blocking collectives: 26.9 us -> none  [the longest x1 13.6 us: per_device(): lax.all_gather(bias_qv, 'row', axis=0, tiled=True)]
  transfers between devices with their start and end apart: 17 -> 2, of which waited for: 14 -> 1; matrix products, arithmetic and copies ran while one was open for 10% -> 2% of each run, Pallas kernels for 0% -> 0%
where the time goes in v1:
time: 356 us; the launch traced here: 354 us
  Pallas kernels  301 us (85%)
  local copies, waits for them, and re-layouts  38.2 us (11%)
  other arithmetic  11.8 us (3%)
    pallas_call x1, Pallas kernels, reduce(): pl.pallas_call(reduce_kernel, out_shape=(o, o, w, w, S((b, width), F32),...  117 us
    pallas_call x1, Pallas kernels, gather(): pl.pallas_call(gather_kernel, out_shape=(S((feats, length + 128), BF), S(...  80.2 us
    pallas_call x1, Pallas kernels, mlp(): pl.pallas_call(mlp_kernel, out_shape=(S((rows, feats), BF), S((rows, feat...  42.1 us
    pallas_call x1, Pallas kernels, attn_bwd(): pl.pallas_call(attn_bwd_kernel, out_shape=(S((rows, feats), F32), S((3, 8...  39.2 us
    pallas_call x1, Pallas kernels, attn_fwd(): pl.pallas_call(attn_fwd_kernel, out_shape=(S((rows, feats), BF), t3, t3,...  22.3 us
    unnamed x68, local copies, waits for them, and re-layouts  12.3 us
  transfers between devices with their start and end apart: 2, of which 1 were waited for; matrix products, arithmetic and copies ran while one was open for 2% of the time, Pallas kernels for 0%

profile of v1, /device:TPU:0, one launch (start us, length us, event | category | flops | bytes accessed | tf_op | source)
XLA Modules:
  0.0 354.2 jit_solution(16557881651830054812)
XLA Ops:
  0.8 1.1 copy.42
  2.0 1.3 reshape.149
  3.3 1.4 slice_reduce_fusion
  4.7 0.1 slice_bitcast_fusion.8
  4.8 0.1 squeeze.104
  5.0 0.2 copy.41
  5.3 0.1 concatenate.93
  5.4 0.2 concatenate.92.la
  5.6 80.2 %shard_map.280 = (bf16[768,1152]{1,0:T(8,128)(2,1)S(1)}, bf16[768,512]{1,0:T(8,128)(2,1)S(1)}, bf16[4,768,768]{2,1,0:T(8,128)(2,1)S(1)}, bf16[4,768,768]{2,1,0:T...) custom-call(bf16[2,192,1024]{2,1,0:T(8,128)(2,1)S(1)} %copy-done.5, ...), custom_call_target="tpu_custom_call" | custom-call | tf_op jit(solution)/shard_map/pallas_call | solution.py:503
  85.9 2.2 copy-done.2
  88.1 1.2 copy-done.3
  89.3 0.9 copy-done.4
  90.2 0.1 concatenate.95
  90.3 0.1 concatenate.96
  90.5 0.6 broadcast_in_dim.51.bias
  91.1 3.3 constant_dynamic-slice_fusion.11.wa_hbm
  94.4 0.1 concatenate.98
  94.5 0.6 broadcast_in_dim.53.idq
  95.1 1.0 broadcast_in_dim.52.idk
  96.1 22.3 %shard_map.281 = (bf16[1056,768]{1,0:T(8,128)(2,1)}, bf16[3,1056,128]{2,1,0:T(8,128)(2,1)}, bf16[3,1056,128]{2,1,0:T(8,128)(2,1)}, bf16[3,1056,128]{2,1,0:T(8,12...) custom-call(bf16[768,1152]{1,0:T(8,128)(2,1)} %copy-done.3, ...), custom_call_target="tpu_custom_call" | custom-call | tf_op jit(solution)/shard_map/pallas_call | solution.py:264
  118.5 1.3 constant_dynamic-slice_fusion.9
  119.8 0.7 constant_dynamic-slice_fusion.8
  120.5 0.8 pad_maximum_fusion.4
  121.3 0.5 collective-permute-start
  121.9 0.6 reduce_sum.36
  122.5 0.6 dynamic_slice.49.valid_ref
  123.2 0.1 reshape.151
  123.9 0.6 reshape_squeeze.8.bup
  124.6 0.6 concatenate.103.vec
  125.2 1.0 pad_maximum_fusion.1.x
  126.2 0.2 broadcast_select_fusion.2
  126.6 0.9 copy-done.10
  127.5 42.1 %shard_map.282 = (bf16[528,768]{1,0:T(8,128)(2,1)}, f32[528,768]{1,0:T(8,128)}, bf16[528,768]{1,0:T(8,128)(2,1)}, f32[6,8,768]{2,1,0:T(8,128)}, f32[4,8,768]{2,1...) custom-call(s32[1]{0:T(128)} %bitcast.half_ref, s32[1]{0:T(128)} %dynamic_slice.49.valid_ref, ...), custom_call_target="tpu_custom_call" | custom-call | tf_op jit(solution)/shard_map/pallas_call | solution.py:172
  169.8 1.0 reduce_sum.37
  170.8 0.9 reduce_sum.38
  171.7 0.5 collective-permute-done.1
  172.2 1.3 broadcast_select_fusion.1
  173.6 1.3 pad_maximum_fusion.ga
  174.9 39.2 %shard_map.283 = (f32[1056,768]{1,0:T(8,128)}, f32[3,8,384]{2,1,0:T(8,128)}, bf16[2,768,768]{2,1,0:T(8,128)(2,1)}) custom-call(bf16[1056,768]{1,0:T(8,128)(2,1)} %pad_maximum_fusion.ga, bf16[3,1056,128]{2,1,0:T(8,128)(2,1)} %get-tuple-element.46.mixed, bf16[768,1152]{1,0:T(8,128)(2,1)} %copy-done.3, bf16[3,1056,128]{2,1,0:T(8,128)(2,1)} %get-tuple-element.54.qt, ...), custom_call_target="tpu_custom_call" | custom-call | tf_op jit(solution)/shard_map/pallas_call | solution.py:349
  214.1 0.8 reduce_sum.39
  215.0 0.7 maximum_maximum_fusion.sv
  215.7 117.1 %shard_map.284 = (bf16[2,2,528,192]{3,2,1,0:T(8,128)(2,1)}, bf16[2,2,528,192]{3,2,1,0:T(8,128)(2,1)}, bf16[192,768]{1,0:T(8,128)(2,1)}, bf16[192,768]{1,0:T(8,12...) custom-call(bf16[4,768,768]{2,1,0:T(8,128)(2,1)} %get-tuple-element.51.gu, bf16[4,768,768]{2,1,0:T(8,128)(2,1)} %get-tuple-element.52.gd, ...), custom_call_target="tpu_custom_call" | custom-call | tf_op jit(solution)/shard_map/pallas_call | solution.py:678
  332.8 1.2 fusion.9
  334.0 0.9 slice.404
  335.0 0.3 copy-done.11
  335.3 0.8 slice_bitcast_fusion
  336.2 0.8 slice_bitcast_fusion.1
  337.1 0.8 copy.50
  337.9 0.2 pad_maximum_fusion.5
  338.1 0.2 stack.38
  338.3 0.2 stack.39
  338.4 0.8 stack.40
  339.3 0.6 copy.49
  339.9 0.2 bitcast_convert_fusion
  340.2 1.7 copy.48
  341.9 6.0 %concatenate.106 = bf16[2,1044,192]{2,1,0:T(8,128)(2,1)S(1)} concatenate(bf16[2,10,192]{2,1,0:T(8,128)(2,1)S(1)} %slice_bitcast_fusion.14, bf16[2,512,192]{2,1,0:T(8,128)(2,1)} %slice_bitcast_fusion, bf16[2,512,192]{2,1,0:T(8,128)(2,1)} %slice_bitcast_fusion.1, bf16[2,6,192]{2,1,0:T(8,128)(2,1)S(1)} %slice_bitcast_fusion.16, bf16[2,4,192]{2,1,0:T(4,128)(2,1)S(1)} %get-tuple-element.149), dimensions={1} | concatenate | bytes 1603584 | tf_op jit(solution)/shard_map/concatenate | solution.py:736
  347.9 1.3 copy.47
  349.2 0.9 convert_element_type.25
  350.1 0.6 fusion.6
  350.7 0.1 fusion.7
  350.9 0.6 pad_maximum_fusion.8
  351.5 1.2 pad_maximum_fusion.2
  352.7 0.7 fusion.10
  353.4 0.8 copy.61
  (107 shorter events, 1.5 us)
Async XLA Ops:
  0.7 93.8 %copy-start = (s32[2,1024]{1,0:T(2,128)S(1)}, s32[2,1024]{1,0:T(2,128)}, u32[]{:S(2)}) copy-start(s32[2,1024]{1,0:T(2,128)} %param.19) | copy-start | bytes 24580
  0.7 4.3 %copy-start.18 = (bf16[2,20,192]{2,0,1:T(2,128)(2,1)S(1)}, bf16[2,20,192]{2,0,1:T(2,128)(2,1)}, u32[]{:S(2)}) copy-start(bf16[2,20,192]{2,0,1:T(2,128)(2,1)} %param.18) | copy-start | bytes 46084
  0.7 4.6 %copy-start.21 = (f32[192]{0:T(256)S(1)}, f32[192]{0:T(256)}, u32[]{:S(2)}) copy-start(f32[192]{0:T(256)} %param.25) | copy-start | bytes 2308
  0.7 4.5 %copy-start.22 = (f32[192]{0:T(256)S(1)}, f32[192]{0:T(256)}, u32[]{:S(2)}) copy-start(f32[192]{0:T(256)} %param.26) | copy-start | bytes 2308
  0.7 4.5 %copy-start.23 = (f32[192]{0:T(256)S(1)}, f32[192]{0:T(256)}, u32[]{:S(2)}) copy-start(f32[192]{0:T(256)} %param.27) | copy-start | bytes 2308
  0.7 4.5 %copy-start.19 = (f32[768]{0:T(1024)S(1)}, f32[768]{0:T(1024)}, u32[]{:S(2)}) copy-start(f32[768]{0:T(1024)} %param.29) | copy-start | bytes 9220
  0.7 4.5 %copy-start.24 = (f32[192]{0:T(256)S(1)}, f32[192]{0:T(256)}, u32[]{:S(2)}) copy-start(f32[192]{0:T(256)} %param.31) | copy-start | bytes 2308
  0.7 4.5 %copy-start.25 = (f32[192]{0:T(256)S(1)}, f32[192]{0:T(256)}, u32[]{:S(2)}) copy-start(f32[192]{0:T(256)} %param.32) | copy-start | bytes 2308
  0.7 4.5 %copy-start.26 = (f32[192]{0:T(256)S(1)}, f32[192]{0:T(256)}, u32[]{:S(2)}) copy-start(f32[192]{0:T(256)} %param.33) | copy-start | bytes 2308
  0.7 4.6 %copy-start.20 = (f32[3,128]{1,0:T(4,128)S(1)}, f32[3,128]{1,0:T(4,128)}, u32[]{:S(2)}) copy-start(f32[3,128]{1,0:T(4,128)} %param.23) | copy-start | bytes 4612
  0.8 4.8 %copy-start.5 = (bf16[2,192,1024]{2,1,0:T(8,128)(2,1)S(1)}, bf16[2,192,1024]{2,1,0:T(8,128)(2,1)}, u32[]{:S(2)}) copy-start(bf16[2,192,1024]{2,1,0:T(8,128)(2,1)} %tok.1) | copy-start | bytes 2359300
  0.8 4.8 %copy-start.6 = (bf16[2,192,1024]{2,1,0:T(8,128)(2,1)S(1)}, bf16[2,192,1024]{2,1,0:T(8,128)(2,1)}, u32[]{:S(2)}) copy-start(bf16[2,192,1024]{2,1,0:T(8,128)(2,1)} %tch.1) | copy-start | bytes 2359300
  0.8 4.8 %copy-start.7 = (bf16[192,768]{1,0:T(8,128)(2,1)S(1)}, bf16[192,768]{1,0:T(8,128)(2,1)}, u32[]{:S(2)}) copy-start(bf16[192,768]{1,0:T(8,128)(2,1)} %lu.1) | copy-start | bytes 884740
  0.8 4.8 %copy-start.8 = (bf16[192,768]{1,0:T(8,128)(2,1)S(1)}, bf16[192,768]{1,0:T(8,128)(2,1)}, u32[]{:S(2)}) copy-start(bf16[192,768]{1,0:T(8,128)(2,1)} %ld.1) | copy-start | bytes 884740
  85.9 2.2 copy-start.2
  88.0 1.2 copy-start.3
  89.3 0.9 copy-start.4
  118.5 3.4 copy-start.27
  118.5 6.7 %copy-start.15 = (bf16[1056,768]{1,0:T(8,128)(2,1)S(1)}, bf16[1056,768]{1,0:T(8,128)(2,1)}, u32[]{:S(2)}) copy-start(bf16[1056,768]{1,0:T(8,128)(2,1)} %get-tuple-element.47) | copy-start | bytes 4866052
  121.3 4.9 %collective-permute-start = (bf16[3,528,128]{2,1,0:T(8,128)(2,1)}, bf16[3,528,128]{2,1,0:T(8,128)(2,1)S(1)}, u32[]{:S(2)}, u32[]{:S(2)}) collective-permute-start(bf16[3,528,128]{2,1,0:T(8,128)(2,1)} %pad_maximum_fusion.4), channel_id=1, source_target_pairs={{0,1},{1,0},{2,3},{3,2},{4,5},{5,4},{6,7},{7,6},{8,9},{9,8},{10,11... | collective-permute-start | bytes 1216520 | tf_op jit(solution)/shard_map/ppermute | solution.py:720
  126.6 0.9 copy-start.10
  169.6 2.6 collective-permute-start.1
  332.8 2.1 copy-start.9
  332.8 2.1 copy-start.12
  334.0 1.3 copy-start.11
  335.0 2.1 copy-start.17
  341.9 7.4 %copy-start.16 = (bf16[192,768]{1,0:T(8,128)(2,1)S(1)}, bf16[192,768]{1,0:T(8,128)(2,1)}, u32[]{:S(2)}) copy-start(bf16[192,768]{1,0:T(8,128)(2,1)} %get-tuple-element.69) | copy-start | bytes 884740
  347.9 3.6 %copy-start.14 = (f32[1,36864]{1,0:T(1,128)S(1)}, f32[1,36864]{1,0:T(1,128)}, u32[]{:S(2)}) copy-start(f32[1,36864]{1,0:T(1,128)} %stack.40) | copy-start | bytes 442372
  347.9 5.5 %copy-start.13 = (f32[192,768]{1,0:T(8,128)S(1)}, f32[192,768]{1,0:T(8,128)}, u32[]{:S(2)}) copy-start(f32[192,768]{1,0:T(8,128)} %get-tuple-element.180) | copy-start | bytes 1769476
  347.9 6.3 %copy-start.1 = (s32[2,1024]{1,0:T(2,128)S(1)}, s32[2,1024]{1,0:T(2,128)}, u32[]{:S(2)}) copy-start(s32[2,1024]{1,0:T(2,128)} %param.19) | copy-start | bytes 24580

commit v2 on v1

--- a/solution.py
+++ b/solution.py
@@ -354,7 +354,504 @@
         compiler_params=pltpu.CompilerParams(vmem_limit_bytes=63*2**20))(ga, mixed, xt, qt, kt, vt, lse, idk, idq, wa)
 MESH = pl.DeviceIdType.MESH
 
+class Move:
+    def __init__(self, net, src, dst, dev, index):
+        self.net, self.src, self.dst, self.dev, self.index = net, src, dst, dev, index
+    def make(self):
+        return pltpu.make_async_remote_copy(src_ref=self.src(), dst_ref=self.dst(), send_sem=self.net.ss.at[self.index],
+                                            recv_sem=self.net.rs.at[self.index], device_id=self.dev, device_id_type=MESH)
+    def start(self):
+        self.make().start()
+    def wait_recv(self):
+        self.make().wait_recv()
+    def wait_send(self):
+        self.make().wait_send()
+
+class Copy:
+    def __init__(self, net, src, dst, index):
+        self.net, self.src, self.dst, self.index = net, src, dst, index
+    def make(self):
+        return pltpu.make_async_copy(self.src(), self.dst(), self.net.ls.at[self.index])
+    def start(self):
+        self.make().start()
+    def wait(self):
+        self.make().wait()
+
 class Net:
+    def __init__(self, send_sems, recv_sems, local_sems):
+        self.ss, self.rs, self.ls = send_sems, recv_sems, local_sems
+        self.count, self.locals, self.moves, self.copies = 0, 0, [], []
+        self.d, self.z, self.c = (lax.axis_index(a) for a in ("dp", "row", "col"))
+        self.nd, self.nz = lax.axis_size("dp"), lax.axis_size("row")
+        self.y, self.k = self.c // 2, self.c % 2
+        self.x = self.d % 2
+        self.oc = lax.rem(self.c + 2, 4)
+        self.xp = (self.d + 1 - 2 * self.x, self.z, self.c)
+        self.yp = (self.d, self.z, self.oc)
+        self.kp = (self.d, self.z, self.c + 1 - 2 * self.k)
+        self.ykp = (self.d, self.z, 3 - self.c)
+        self.zs = [lax.rem(self.z + i, self.nz) for i in range(self.nz)]
+        self.zp = [(self.d, zz, self.c) for zz in self.zs]
+        self.others = [(lax.rem(self.d + 2 * i, self.nd), self.z, self.c) for i in range(1, self.nd // 2)]
+    def from_row(self, i):
+        return self.zs[(self.nz - i) % self.nz]
+    def barrier(self, peers):
+        b = pltpu.get_barrier_semaphore()
+        for p in peers:
+            pl.semaphore_signal(b, inc=1, device_id=p, device_id_type=MESH)
+        pl.semaphore_wait(b, len(peers))
+    def move(self, src, dst, dev):
+        m = Move(self, src, dst, dev, self.count)
+        self.count += 1
+        self.moves.append(m)
+        return m
+    def send(self, src, dst, dev):
+        m = self.move(src, dst, dev)
+        m.start()
+        return m
+    def copy(self, src, dst):
+        m = Copy(self, src, dst, self.locals)
+        self.locals += 1
+        self.copies.append(m)
+        return m
+    def local(self, src, dst):
+        m = self.copy(src, dst)
+        m.start()
+        return m
+    def finish(self):
+        for m in self.moves:
+            m.wait_send()
+
+def at(i, table):
+    for j, events in table.items():
+        if events:
+            @pl.when(i == j)
+            def _(events=events):
+                for e in events:
+                    e()
+
+def spread_events(events, steps):
+    table = {}
+    for n, e in enumerate(events):
+        table.setdefault(n * steps // len(events), []).append(e)
+    return table
+
+def join192(t, dst):
+    lo = lax.broadcasted_iota(jnp.int32, t[0][0].shape, 1) < 64
+    sw = lambda a: pltpu.roll(a, 64, 1)
+    for h in range(2):
+        a, b = t[2 * h], t[2 * h + 1]
+        dst[:, pl.ds(384 * h, 128)] = a[0]
+        dst[:, pl.ds(384 * h + 128, 128)] = jnp.where(lo, a[1], sw(b[0]))
+        dst[:, pl.ds(384 * h + 256, 128)] = jnp.where(lo, sw(b[0]), sw(b[1]))
+
+def forward_kernel(valid_ref, tok, mem, tch, la, lu, ld, ls, idk, idq,
+                   xt_o, q_o, k_o, v_o, mixed_o, wa_o, ga_o, hu_o, hd_o, lse, g_one, vgrad, bupgrad, out4,
+                   xt, x, wa, wu, wd, sm, tt, tr, wp, qt, kt, vt, vtt, ot, mixed, mrows, bias, vec, wt,
+                   h1, h2, rs1, low, lowt, br, brt, hid, dgl, gdz, guz, hu, hd, ru, rd, ga, o4, ss, rs, lsem, zsem, zrem):
+    n = Net(ss, rs, lsem)
+    n.barrier(n.zp[1:] + [n.yp, n.ykp, n.kp, n.xp])
+    nz, y, k, c, z, oc = n.nz, n.y, n.k, n.c, n.z, n.oc
+    b = la.shape[0]; hb = b // 2
+    feats = x.shape[1]; rows = x.shape[0]; length = tok.shape[2]; main = length // 2
+    own_rows = main + 16
+    row = lambda cc, off=0, num=b: pl.ds(pl.multiple_of(cc * b + off, 16), num)
+    blk = lambda w, zz, cc: (lambda: w.at[zz, row(cc)])
+    hlf = lambda w, zz, cc, h: (lambda: w.at[zz, row(cc, h * hb, hb)])
+    mine, theirs = n.x, 1 - n.x
+    part = lambda w: (lambda: w.at[pl.ds(pl.multiple_of(n.x * hb, 16), hb)])
+    all_of = lambda r: (lambda: r)
+    tail = pl.ds(length, 128); body = pl.ds(0, length)
+    fz = n.from_row
+    R = range(1, nz)
+    local = [n.local(lambda: tok.at[y], lambda: xt.at[row(c), body]), n.local(lambda: mem.at[y], lambda: xt.at[row(c), tail])]
+    s_blk = lambda zz, cc: (lambda: sm.at[zz, cc])
+    a_z = [n.send(part(la), hlf(wa, z, c, mine), n.zp[i]) for i in R]
+    s_z = [n.send(all_of(ls), s_blk(z, c), n.zp[i]) for i in R]
+    a_y = [n.send(part(la), hlf(wa, z, c, mine), n.yp)]
+    t_y = [n.send(lambda: tok.at[1 - y], lambda: xt.at[row(c), body], n.yp), n.send(lambda: mem.at[1 - y], lambda: xt.at[row(c), tail], n.yp)]
+    s_y = [n.send(all_of(ls), s_blk(z, c), n.yp)]
+    u_y = n.send(part(lu), hlf(wu, z, c, mine), n.yp)
+    s_k = [n.send(all_of(ls), s_blk(z, c), n.kp)]
+    t_k = [n.send(lambda: tok.at[y], lambda: xt.at[row(c), body], n.kp), n.send(lambda: mem.at[y], lambda: xt.at[row(c), tail], n.kp)]
+    a_k = [n.send(all_of(la), blk(wa, z, c), n.kp)]
+    for w, l in ((wa, la), (wu, lu), (wd, ld)):
+        local.append(n.local(all_of(l), blk(w, z, c)))
+    local.append(n.local(all_of(ls), s_blk(z, c)))
+    fwd = lambda u, dev: n.move(u, u, dev)
+    a_x = []
+    for i in R:
+        a_z[i - 1].wait_recv()
+        u = hlf(wa, fz(i), c, mine)
+        for lst, dev in ((a_y, n.yp), (a_x, n.xp), (a_k, n.kp)):
+            lst.append(fwd(u, dev)); lst[-1].start()
+        s_z[i - 1].wait_recv()
+        u = s_blk(fz(i), c)
+        for lst, dev in ((s_y, n.yp), (s_k, n.kp)):
+            lst.append(fwd(u, dev)); lst[-1].start()
+    u_z = [n.send(part(lu), hlf(wu, z, c, mine), n.zp[i]) for i in R]
+    u_k = [n.send(all_of(lu), blk(wu, z, c), n.kp)]
+    u_y.wait_recv()
+    uo = hlf(wu, z, oc, mine)
+    u_z2 = [fwd(uo, n.zp[i]) for i in R]
+    for m in u_z2:
+        m.start()
+    u_x = [fwd(uo, n.xp)]
+    u_k.append(fwd(uo, n.kp)); u_k[-1].start()
+    for m, w_ in zip(t_y, (body, tail)):
+        m.wait_recv()
+        t_k.append(fwd((lambda w_=w_: xt.at[row(oc), w_]), n.kp)); t_k[-1].start()
+    for i in range(nz):
+        a_y[i].wait_recv()
+        u = hlf(wa, fz(i), oc, mine)
+        for lst, dev in ((a_x, n.xp), (a_k, n.kp)):
+            lst.append(fwd(u, dev)); lst[-1].start()
+        s_y[i].wait_recv()
+        u = s_blk(fz(i), oc)
+        s_k.append(fwd(u, n.kp)); s_k[-1].start()
+    u_x[0].start()
+    d_z = [n.send(all_of(ld), blk(wd, z, c), n.zp[i]) for i in R]
+    d_y = [n.send(all_of(ld), blk(wd, z, c), n.yp)]
+    d_k = [n.send(all_of(ld), blk(wd, z, c), n.kp)]
+    tsl = lambda s, kk: (lambda: tch.at[s, :, pl.ds(pl.multiple_of(kk * main, 128), main)])
+    th = lambda: tt.at[row(c)]
+    h_y = [n.send(tsl(y, 1 - k), th, n.kp)]
+    local.append(n.local(tsl(y, k), th))
+    local[0].wait(); local[1].wait()
+    for m in t_k:
+        m.wait_recv()
+    def turn(i, _):
+        f = pl.ds(pl.multiple_of(128 * i, 128), 128)
+        x[f, :] = xt[:, f].T
+        return 0
+    lax.fori_loop(0, length // 128, turn, 0)
+    x[pl.ds(length, rows - length), :] = xt[:, tail].T[: rows - length, :]
+    o_x = n.local(all_of(xt), all_of(xt_o))
+    order = [(i, c) for i in R] + [(i, oc) for i in range(nz)]
+    for m, (i, cc) in zip(a_x, order):
+        m.wait_recv()
+        a_k.append(fwd(hlf(wa, fz(i), cc, theirs), n.kp)); a_k[-1].start()
+    h_y += [n.send(tsl(1 - y, k), th, n.yp), n.send(tsl(1 - y, 1 - k), th, n.ykp)]
+    events = []
+    def relay(wait, u, pairs):
+        ms = []
+        for lst, dev in pairs:
+            m = fwd(u, dev)
+            lst.append(m)
+            ms.append(m)
+        def run():
+            wait()
+            for m in ms:
+                m.start()
+        events.append(run)
+    for i in R:
+        relay(u_z[i - 1].wait_recv, hlf(wu, fz(i), c, mine), ((u_x, n.xp), (u_k, n.kp)))
+    for i in R:
+        relay(u_z2[i - 1].wait_recv, hlf(wu, fz(i), oc, mine), ((u_x, n.xp), (u_k, n.kp)))
+    u_order = [(0, oc)] + [(i, c) for i in R] + [(i, oc) for i in R]
+    u_units = list(zip(u_x, u_order))
+    for i in R:
+        relay(d_z[i - 1].wait_recv, blk(wd, fz(i), c), ((d_y, n.yp), (d_k, n.kp)))
+    for m, (i, cc) in u_units:
+        relay(m.wait_recv, hlf(wu, fz(i), cc, theirs), ((u_k, n.kp),))
+    u_events, d_events = events, []
+    events = []
+    for i in range(nz):
+        relay(d_y[i].wait_recv, blk(wd, fz(i), oc), ((d_k, n.kp),))
+    d_events = events
+    for m in s_k:
+        m.wait_recv()
+    for m in local[2:6]:
+        m.wait()
+    join192([[sm[0, cc, pl.ds(0, 8), pl.ds(0, 128)], sm[0, cc, pl.ds(0, 8), pl.ds(128, 128)]] for cc in range(4)], vec)
+    lo1 = lax.broadcasted_iota(jnp.int32, (1, 128), 1) < 64
+    sw = lambda a: pltpu.roll(a, 64, 1)
+    bias[...] = jnp.zeros_like(bias)
+    hv = [[sm[2 * k + j, 0, 11:12, pl.ds(0, 128)], sm[2 * k + j, 0, 11:12, pl.ds(128, 128)], sm[2 * k + j, 0, 12:13, pl.ds(0, 128)]] for j in range(2)]
+    for p, (e0, e1) in enumerate(((hv[0][0], hv[0][1]), (hv[1][0], hv[1][1]), (hv[0][2], hv[1][2]))):
+        w8 = lambda a: jnp.broadcast_to(a, (8, 128))
+        lo8 = lax.broadcasted_iota(jnp.int32, (8, 128), 1) < 64
+        bias[p, :, pl.ds(0, 128)] = jnp.where(lo8, w8(e0), sw(w8(e1)))
+        bias[p, :, pl.ds(256, 128)] = jnp.where(lo8, sw(w8(e0)), w8(e1))
+    for m in a_k:
+        m.wait_recv()
+    own = pl.ds(2 * k, 2)
+    o_w = n.local(lambda: wa.at[own], all_of(wa_o))
+    w = wa.at[own]
+    assemble_pairs(w, wp, feats)
+    rc = rows // 3
+    ev = spread_events(u_events[:6], 9)
+
+    def project(i, _):
+        p = i // 3
+        r = pl.ds(pl.multiple_of((i % 3) * rc, 16), rc)
+        v = nn(x[r, :], wp[p]) + bias[p, 0:1, :]
+        qt[p, r, :] = (v[:, :128].astype(BF).astype(F32) * 0.125).astype(BF)
+        kt[p, r, :] = v[:, 128:256].astype(BF)
+        vt[p, r, :] = v[:, 256:].astype(BF)
+        at(i, ev)
+        return 0
+    lax.fori_loop(0, 9, project, 0)
+    o_q = [n.local(all_of(a), all_of(o)) for a, o in ((qt, q_o), (kt, k_o), (vt, v_o))]
+    m_k = [(n.move((lambda p=p: mixed.at[p, pl.ds(pl.multiple_of((1 - k) * main, 16), main)]), (lambda p=p: mrows.at[k * 3 + p, pl.ds(0, main)]), n.kp),
+            n.move((lambda p=p: mixed.at[p, pl.ds(pl.multiple_of(length + (1 - k) * 16, 16), 16)]), (lambda p=p: mrows.at[k * 3 + p, pl.ds(main, 16)]), n.kp)) for p in range(3)]
+    m_l = [(n.copy((lambda p=p: mixed.at[p, pl.ds(pl.multiple_of(k * main, 16), main)]), (lambda p=p: mrows.at[k * 3 + p, pl.ds(0, main)])),
+            n.copy((lambda p=p: mixed.at[p, pl.ds(pl.multiple_of(length + k * 16, 16), 16)]), (lambda p=p: mrows.at[k * 3 + p, pl.ds(main, 16)]))) for p in range(3)]
+    ev = spread_events(u_events[6:], 6)
+
+    def head(i, _):
+        p = i // 2
+        e = i % 2
+        he = pl.ds(pl.multiple_of(64 * e, 64), 64)
+
+        @pl.when(e == 0)
+        def _():
+            vtt[...] = vt[p].T
+        lanes = (lax.broadcasted_iota(jnp.int32, (1, 128), 1) // 64) == e
+        for q0, qn, spans in tiles(rows, length):
+            q = qt[p, pl.ds(q0, qn), :]
+            qm = jnp.where(lanes, q, jnp.zeros_like(q))
+            sc = scores_of(kt, qm, idk, idq[0:1, pl.ds(q0, qn)], p, spans)
+            m = jnp.max(sc[0], axis=0, keepdims=True)
+            for s in sc[1:]:
+                m = jnp.maximum(m, jnp.max(s, axis=0, keepdims=True))
+            tot, acc = None, None
+            for s, (k0, kn, _) in zip(sc, spans):
+                ex = jnp.exp(s - m)
+                t = jnp.sum(ex, axis=0, keepdims=True)
+                o = nn(vtt[he, pl.ds(k0, kn)], ex.astype(BF))
+                tot = t if tot is None else tot + t
+                acc = o if acc is None else acc + o
+            ot[he, pl.ds(q0, qn)] = acc / tot
+            lse[i, :, pl.ds(q0, qn)] = m + jnp.log(tot)
+
+        @pl.when(e == 1)
+        def _():
+            mixed[p] = ot[...].T.astype(BF)
+        at(i, ev)
+        at(i, {2 * p + 1: [m.start for m in m_k[p] + m_l[p]] for p in range(3)})
+        return 0
+    lax.fori_loop(0, 6, head, 0)
+    o_m = n.local(all_of(mixed), all_of(mixed_o))
+    lo = lax.broadcasted_iota(jnp.int32, (feats, 128), 1) < 64
+    for kk in range(2):
+        z0, z1 = 2 * kk, 2 * kk + 1
+        wt[:, pl.ds(384 * kk, 128)] = wa[z0, :, pl.ds(640, 128)]
+        wt[:, pl.ds(384 * kk + 128, 128)] = wa[z1, :, pl.ds(640, 128)]
+        t0 = pltpu.roll(wa[z0, :, pl.ds(512, 128)].astype(F32), 64, 1)
+        wt[:, pl.ds(384 * kk + 256, 128)] = jnp.where(lo, t0, wa[z1, :, pl.ds(512, 128)].astype(F32)).astype(BF)
+    for pair_ in m_k:
+        for m in pair_:
+            m.wait_recv()
+    for pair_ in m_l:
+        for m in pair_:
+            m.wait()
+    nb = feats // 256
+    CHS = own_rows // CH
+    for e in d_events[:0]:
+        e()
+
+    def own_slice(i, num):
+        start = jnp.where(i < main, k * main + i, length + k * 16)
+        return pl.ds(pl.multiple_of(start, 16), num)
+
+    for f0 in range(0, feats, 256):
+        f = pl.ds(f0, 256)
+        acc = nt(mrows[0], wt[f, pl.ds(0, 128)])
+        for j in range(1, 6):
+            acc = acc + nt(mrows[j], wt[f, pl.ds(128 * j, 128)])
+        h1[:, f] = acc + vec[0:1, f]
+    inv = 1.0 / feats
+    vgrad[...] = jnp.zeros_like(vgrad)
+    bupgrad[...] = jnp.zeros_like(bupgrad)
+
+    def norm1(i, _):
+        r = pl.ds(pl.multiple_of(i * 16, 16), 16)
+        h = h1[r, :] + x[own_slice(i * 16, 16), :].astype(F32)
+        m = jnp.sum(h, axis=1, keepdims=True) * inv
+        s = jnp.sum(h * h, axis=1, keepdims=True) * inv
+        rstd = lax.rsqrt(s - m * m + EPSILON)
+        xhat = (h - m) * rstd
+        h1[r, :] = xhat
+        rs1[r, :] = jnp.broadcast_to(rstd, (16, 128))
+        low[r, :] = (xhat * vec[1:2, :] + vec[2:3, :]).astype(BF)
+        return 0
+    lax.fori_loop(0, own_rows // 16, norm1, 0, unroll=3)
+    lowt[...] = low[...].T
+    for m in u_k:
+        m.wait_recv()
+    ev = spread_events(d_events, 12)
+
+    def gate(i, _):
+        zz = i // nb
+        j = i % nb
+        f = pl.ds(pl.multiple_of(j * 256, 256), 256)
+        v = nn(low[...], wu[zz, :, f]) + sm[zz, 0, pl.ds(8 + j, 1), :]
+        a, g = gelu_pair(v)
+        hid[zz, :, f] = a.astype(BF)
+        dgl[zz, :, f] = g.astype(BF)
+        at(i, ev)
+        return 0
+    lax.fori_loop(0, nz * nb, gate, 0)
+    for m in h_y:
+        m.wait_recv()
+    local[6].wait()
+    def turn_t(i, _):
+        f = pl.ds(pl.multiple_of(128 * i, 128), 128)
+        tr[f, :] = tt[:, f].T
+        return 0
+    lax.fori_loop(0, main // 128, turn_t, 0)
+    tr[pl.ds(main, 16), :] = jnp.zeros((16, feats), BF)
+    for m in d_k:
+        m.wait_recv()
+
+    def down(j, _):
+        f = pl.ds(pl.multiple_of(j * 256, 256), 256)
+        acc = nt(hid[0], wd[0, f, :])
+        for zz in range(1, nz):
+            acc = acc + nt(hid[zz], wd[zz, f, :])
+        h2[:, f] = acc
+        return 0
+    lax.fori_loop(0, nb, down, 0)
+    scale = vec[6:7, 0:1]
+
+    def norm2(i, _):
+        r = pl.ds(pl.multiple_of(i * CH, 16), CH)
+        h = h2[r, :] + (h1[r, :] * vec[1:2, :] + vec[2:3, :]) + vec[3:4, :]
+        m = jnp.sum(h, axis=1, keepdims=True) * inv
+        s = jnp.sum(h * h, axis=1, keepdims=True) * inv
+        rstd = lax.rsqrt(s - m * m + EPSILON)
+        xhat = (h - m) * rstd
+        o = xhat * vec[4:5, :] + vec[5:6, :]
+        for cc in range(4):
+            o4[cc, r, :] = o[:, cc * b:(cc + 1) * b].astype(BF)
+        place = lax.broadcasted_iota(jnp.int32, (CH, 1), 0) + i * CH
+        place = jnp.where(place < main, place + k * main, valid_ref[0])
+        go = jnp.where(place < valid_ref[0], scale * (o - tr[r, :].astype(F32)), 0.0)
+        a = go * vec[4:5, :]
+        m1 = jnp.sum(a, axis=1, keepdims=True) * inv
+        m2 = jnp.sum(a * xhat, axis=1, keepdims=True) * inv
+        g2 = rstd * (a - m1 - xhat * m2)
+        h2[r, :] = g2
+        g2b = g2.astype(BF)
+        br[r, :] = g2b
+        vgrad[0] += group_sum(go * xhat)
+        vgrad[1] += group_sum(go)
+        vgrad[2] += group_sum(g2b.astype(F32))
+        return 0
+    lax.fori_loop(0, CHS, norm2, 0)
+    o_dst = lambda: out4.at[y, k]
+    o_s = [n.send(lambda: o4.at[oc], o_dst, n.yp), n.send(lambda: o4.at[3 - c], o_dst, n.ykp), n.send(lambda: o4.at[c + 1 - 2 * k], o_dst, n.kp)]
+    o_l = n.local(lambda: o4.at[c], o_dst)
+    brt[...] = br[...].T
+    def gmove(which, src, dst, zz, slot, yy):
+        return pltpu.make_async_remote_copy(src_ref=src.at[slot, 2 * yy + 1 - k], dst_ref=dst.at[yy, zz], send_sem=zsem.at[which, yy, zz],
+                                            recv_sem=zrem.at[which, yy, zz], device_id=n.kp, device_id_type=MESH)
+    def each(fn, zz, slot):
+        for which, src, dst in ((0, gdz, rd), (1, guz, ru)):
+            for yy in range(2):
+                fn(gmove(which, src, dst, zz, slot, yy))
+    def fold(zz):
+        each(lambda m: m.wait_recv(), zz, 0)
+        for yy in range(2):
+            add_to(hd.at[yy, zz], rd.at[yy, zz])
+            add_to(hu.at[yy, zz], ru.at[yy, zz])
+
+    def back(zz, _):
+        slot = zz % 2
+
+        @pl.when(zz >= 2)
+        def _():
+            each(lambda m: m.wait_send(), zz - 2, slot)
+
+        def chunk(j, _):
+            f = pl.ds(pl.multiple_of(j * 256, 256), 256)
+            gh = nn(br[...], wd[zz, :, f])
+            g = (gh * dgl[zz, :, f].astype(F32)).astype(BF)
+            bupgrad[zz, :, f] += group_sum(g.astype(F32))
+            gdc = nn(brt[...], hid[zz, :, f])
+            guc = nn(lowt[...], g)
+            hid[zz, :, f] = g
+            for cc in range(4):
+                gdz[slot, cc, :, f] = gdc[cc * b:(cc + 1) * b, :].astype(BF)
+                guz[slot, cc, :, f] = guc[cc * b:(cc + 1) * b, :].astype(BF)
+            return 0
+        lax.fori_loop(0, nb, chunk, 0)
+        each(lambda m: m.start(), zz, slot)
+        for yy in range(2):
+            hd[yy, zz] = gdz[slot, 2 * yy + k]
+            hu[yy, zz] = guz[slot, 2 * yy + k]
+
+        @pl.when(zz >= 1)
+        def _():
+            fold(zz - 1)
+        return 0
+    lax.fori_loop(0, nz, back, 0)
+
+    def first_grad(j, _):
+        f = pl.ds(pl.multiple_of(j * 256, 256), 256)
+        acc = h2[:, f]
+        for zz in range(nz):
+            acc = acc + nt(hid[zz], wu[zz, f, :])
+        h2[:, f] = acc
+        return 0
+    lax.fori_loop(0, nb, first_grad, 0)
+    fold(nz - 1)
+    o_h = [n.local(all_of(hd), all_of(hd_o)), n.local(all_of(hu), all_of(hu_o))]
+
+    def norm1_back(i, _):
+        r = pl.ds(pl.multiple_of(i * 16, 16), 16)
+        g = h2[r, :]
+        xhat = h1[r, :]
+        a = g * vec[1:2, :]
+        m1 = jnp.sum(a, axis=1, keepdims=True) * inv
+        m2 = jnp.sum(a * xhat, axis=1, keepdims=True) * inv
+        g1 = rs1[r, 0:1] * (a - m1 - xhat * m2)
+        g_one[r, :] = g1
+        gb = g1.astype(BF)
+        ga[own_slice(i * 16, 16), :] = gb
+        vgrad[3] += group_sum(g * xhat)
+        vgrad[4] += group_sum(g)
+        vgrad[5] += group_sum(gb.astype(F32))
+        return 0
+    lax.fori_loop(0, own_rows // 16, norm1_back, 0, unroll=3)
+    g_main = lambda: ga.at[pl.ds(pl.multiple_of(k * main, 16), main)]
+    g_tail = lambda: ga.at[pl.ds(pl.multiple_of(length + k * 16, 16), 16)]
+    g_k = [n.send(g_main, g_main, n.kp), n.send(g_tail, g_tail, n.kp)]
+    for m in g_k:
+        m.wait_recv()
+    o_g = n.local(all_of(ga), all_of(ga_o))
+    for m in o_s:
+        m.wait_recv()
+    for m in [o_x, o_w, o_m, o_l, o_g] + o_q + o_h:
+        m.wait()
+    for zz in range(nz - 2, nz):
+        each(lambda m: m.wait_send(), zz, zz % 2)
+    n.finish()
+
+def add_to(dst, src):
+    dst[...] = (dst[...].astype(F32) + src[...].astype(F32)).astype(BF)
+
+def forward(valid, tok, mem, tch, la, lu, ld, ls, idk, idq, nz):
+    b, width = lu.shape
+    feats = 4 * b; length = tok.shape[2]; rows = idk.shape[0]; main = length // 2; own = main + 16
+    V = lambda *s, d=BF: pltpu.VMEM(s, d)
+    vm = pl.BlockSpec(memory_space=pltpu.VMEM); sm = pl.BlockSpec(memory_space=pltpu.SMEM); an = pl.BlockSpec(memory_space=pl.ANY)
+    S = jax.ShapeDtypeStruct
+    t3 = S((3, rows, 128), BF); h = S((2, nz, b, width), BF)
+    outs = [(S((feats, length + 128), BF), an), (t3, an), (t3, an), (t3, an), (t3, an), (S((2, feats, width), BF), an), (S((rows, feats), BF), an), (h, an), (h, an),
+            (S((6, 1, rows), F32), vm), (S((own, feats), F32), vm), (S((6, 8, feats), F32), vm), (S((nz, 8, width), F32), vm), (S((2, 2, own, b), BF), vm)]
+    w = V(nz, feats, width)
+    scratch = [V(feats, length + 128), V(rows, feats), w, w, w, V(nz, 4, *ls.shape, d=F32), V(feats, main), V(own, feats), V(3, feats, 384),
+               V(3, rows, 128), V(3, rows, 128), V(3, rows, 128), V(128, rows), V(128, rows, d=F32), V(3, rows, 128), V(6, own, 128), V(3, 8, 384, d=F32), V(8, feats, d=F32), V(feats, feats),
+               V(own, feats, d=F32), V(own, feats, d=F32), V(own, 128, d=F32), V(own, feats), V(feats, own), V(own, feats), V(feats, own),
+               V(nz, own, width), V(nz, own, width), V(2, 4, b, width), V(2, 4, b, width)] + [V(2, nz, b, width)] * 4 + [V(rows, feats), V(4, own, b),
+               pltpu.SemaphoreType.DMA((136,)), pltpu.SemaphoreType.DMA((136,)), pltpu.SemaphoreType.DMA((32,)),
+               pltpu.SemaphoreType.DMA((2, 2, nz)), pltpu.SemaphoreType.DMA((2, 2, nz))]
+    return pl.pallas_call(forward_kernel, out_shape=[o for o, _ in outs], out_specs=[s for _, s in outs],
+        in_specs=[sm, an, an, an, an, an, an, an, vm, vm], scratch_shapes=scratch,
+        compiler_params=pltpu.CompilerParams(collective_id=1, has_side_effects=True, vmem_limit_bytes=67043328))(valid, tok, mem, tch, la, lu, ld, ls, idk, idq)
+class OldNet:
     def __init__(self, send_sems, recv_sems, local_sems):
         self.ss, self.rs, self.ls = send_sems, recv_sems, local_sems
         self.count, self.locals, self.sent = 0, 0, []
@@ -394,120 +891,6 @@
         for c in self.sent:
             c.wait_send()
 
-def gather_kernel(tok, mem, tch, la, lu, ld, ls, xt, tt, wa, wu, wd, sm, ss, rs, lsem):
-    n = Net(ss, rs, lsem)
-    n.barrier(n.zp[1:] + [n.yp, n.ykp, n.kp, n.xp])
-    nz, y, k, c, z = n.nz, n.y, n.k, n.c, n.z
-    b = la.shape[0]; hb = b // 2
-    length = tok.shape[2]
-    oc = lax.rem(c + 2, 4)
-    half = n.x * hb
-    row = lambda cc, off=0, num=b: pl.ds(pl.multiple_of(cc * b + off, 16), num)
-    seq = lambda r: r
-
-    def blk(w, zz, cc):
-        return w.at[zz, row(cc)]
-    def hlf(w, zz, cc, h):
-        return w.at[zz, row(cc, h * hb, hb)]
-    mine, theirs = n.x, 1 - n.x
-    local = [n.local(tok.at[y], xt.at[row(c), pl.ds(0, length)]), n.local(mem.at[y], xt.at[row(c), pl.ds(length, 128)])]
-    t_y = n.send(tok.at[1 - y], xt.at[row(c), pl.ds(0, length)], n.yp)
-    m_y = n.send(mem.at[1 - y], xt.at[row(c), pl.ds(length, 128)], n.yp)
-    s_z = [n.send(ls, sm.at[z, c], n.zp[i]) for i in range(1, nz)]
-    s_y = [n.send(ls, sm.at[z, c], n.yp)]
-    s_k = [n.send(ls, sm.at[z, c], n.kp)]
-    ha = la.at[pl.ds(pl.multiple_of(half, 16), hb)]
-    hu = lu.at[pl.ds(pl.multiple_of(half, 16), hb)]
-    a_z = [n.send(ha, hlf(wa, z, c, mine), n.zp[i]) for i in range(1, nz)]
-    a_y = [n.send(ha, hlf(wa, z, c, mine), n.yp)]
-    t_k = [n.send(tok.at[y], xt.at[row(c), pl.ds(0, length)], n.kp), n.send(mem.at[y], xt.at[row(c), pl.ds(length, 128)], n.kp)]
-    a_k = [n.send(la, blk(wa, z, c), n.kp)]
-    for w, l in ((wa, la), (wu, lu), (wd, ld)):
-        local.append(n.local(l, blk(w, z, c)))
-    local.append(n.local(ls, sm.at[z, c]))
-    a_x = []
-    zz = lambda i: n.zs[(nz - i) % nz]
-    def fwd(src, dst_list):
-        return [n.send(src, src, d) for d in dst_list]
-    for i in range(1, nz):
-        a_z[i - 1].wait_recv()
-        u = hlf(wa, zz(i), c, mine)
-        a_y.append(n.send(u, u, n.yp)); a_x.append(n.send(u, u, n.xp)); a_k.append(n.send(u, u, n.kp))
-        s_z[i - 1].wait_recv()
-        u = sm.at[zz(i), c]
-        s_y.append(n.send(u, u, n.yp)); s_k.append(n.send(u, u, n.kp))
-    u_y = n.send(hu, hlf(wu, z, c, mine), n.yp)
-    u_z = [n.send(hu, hlf(wu, z, c, mine), n.zp[i]) for i in range(1, nz)]
-    u_k = [n.send(lu, blk(wu, z, c), n.kp)]
-    d_z = [n.send(ld, blk(wd, z, c), n.zp[i]) for i in range(1, nz)]
-    d_y = [n.send(ld, blk(wd, z, c), n.yp)]
-    d_k = [n.send(ld, blk(wd, z, c), n.kp)]
-    hw = length // 2
-    tsl = lambda s, kk: tch.at[s, :, pl.ds(pl.multiple_of(kk * hw, 128), hw)]
-    h_y = [n.send(tsl(1 - y, k), tt.at[row(c)], n.yp), n.send(tsl(1 - y, 1 - k), tt.at[row(c)], n.ykp), n.send(tsl(y, 1 - k), tt.at[row(c)], n.kp)]
-    local.append(n.local(tsl(y, k), tt.at[row(c)]))
-    t_y.wait_recv(); m_y.wait_recv()
-    for w_ in (pl.ds(0, length), pl.ds(length, 128)):
-        u = xt.at[row(oc), w_]
-        t_k.append(n.send(u, u, n.kp))
-    for i in range(nz):
-        a_y[i].wait_recv()
-        u = hlf(wa, zz(i), oc, mine)
-        a_x.append(n.send(u, u, n.xp)); a_k.append(n.send(u, u, n.kp))
-        s_y[i].wait_recv()
-        u = sm.at[zz(i), oc]
-        s_k.append(n.send(u, u, n.kp))
-    u_x = []
-    u_y.wait_recv()
-    u = hlf(wu, z, oc, mine)
-    u_z2 = [n.send(u, u, n.zp[i]) for i in range(1, nz)]
-    u_x.append(n.send(u, u, n.xp)); u_k.append(n.send(u, u, n.kp))
-    order = [(i, c) for i in range(1, nz)] + [(i, oc) for i in range(nz)]
-    for cp, (i, cc) in zip(a_x, order):
-        cp.wait_recv()
-        u = hlf(wa, zz(i), cc, theirs)
-        a_k.append(n.send(u, u, n.kp))
-    for i in range(1, nz):
-        u_z[i - 1].wait_recv()
-        u = hlf(wu, zz(i), c, mine)
-        u_x.append(n.send(u, u, n.xp)); u_k.append(n.send(u, u, n.kp))
-    for i in range(1, nz):
-        d_z[i - 1].wait_recv()
-        u = blk(wd, zz(i), c)
-        d_y.append(n.send(u, u, n.yp)); d_k.append(n.send(u, u, n.kp))
-    for i in range(1, nz):
-        u_z2[i - 1].wait_recv()
-        u = hlf(wu, zz(i), oc, mine)
-        u_x.append(n.send(u, u, n.xp)); u_k.append(n.send(u, u, n.kp))
-    for i in range(nz):
-        d_y[i].wait_recv()
-        u = blk(wd, zz(i), oc)
-        d_k.append(n.send(u, u, n.kp))
-    order = [(0, oc)] + [(i, c) for i in range(1, nz)] + [(i, oc) for i in range(1, nz)]
-    for cp, (i, cc) in zip(u_x, order):
-        cp.wait_recv()
-        u = hlf(wu, zz(i), cc, theirs)
-        u_k.append(n.send(u, u, n.kp))
-    for cp in h_y + t_k + a_k + s_k + u_k + d_k:
-        cp.wait_recv()
-    for cp in local:
-        cp.wait()
-    n.finish()
-
-def gather(tok, mem, tch, la, lu, ld, ls, nz):
-    b, width = lu.shape
-    feats = 4 * b; length = tok.shape[2]
-    vm = pl.BlockSpec(memory_space=pltpu.VMEM); an = pl.BlockSpec(memory_space=pl.ANY)
-    S = jax.ShapeDtypeStruct
-    w = S((nz, feats, width), BF)
-    return pl.pallas_call(gather_kernel,
-        out_shape=(S((feats, length + 128), BF), S((feats, length // 2), BF), w, w, w, S((nz, 4) + ls.shape, F32)),
-        in_specs=[vm] * 7, out_specs=(an,) * 6,
-        scratch_shapes=[pltpu.SemaphoreType.DMA((128,)), pltpu.SemaphoreType.DMA((128,)), pltpu.SemaphoreType.DMA((16,))],
-        compiler_params=pltpu.CompilerParams(collective_id=1, has_side_effects=True, vmem_limit_bytes=40*2**20))(tok, mem, tch, la, lu, ld, ls)
-
-def add_to(dst, src):
-    dst[...] = (dst[...].astype(F32) + src[...].astype(F32)).astype(BF)
 
 def sum_refs(refs):
     acc = refs[0][...].astype(F32)
@@ -515,65 +898,41 @@
         acc = acc + r[...].astype(F32)
     return acc
 
-def reduce_kernel(gu, gd, ga, lo, gpart, g1, sv, out4, grad4, fa, fu, fd, svo,
-                  hu, hd, ha, ru, rd, ux, ax, uz, uy, ut, dy, dz, dx, df, ay, az, o4, g4, gs, gr, svk, svy, svx, svz, svt, ss, rs, lsem):
-    n = Net(ss, rs, lsem)
+def reduce_kernel(gu, gd, ga, gpart, g1, sv, grad4, fa, fu, fd, svo,
+                  hu, hd, ha, ux, ax, uz, uy, ut, dy, dz, dx, df, ay, az, g4, gs, gr, svk, svy, svx, svz, svt, ss, rs, lsem):
+    n = OldNet(ss, rs, lsem)
     n.barrier(n.zp[1:] + [n.yp, n.ykp, n.kp, n.xp] + n.others)
     nz, y, k, c, z, x = n.nz, n.y, n.k, n.c, n.z, n.x
     b = fu.shape[0]; hb = b // 2
-    feats = gu.shape[1]
     row = lambda cc: pl.ds(pl.multiple_of(cc * b, 16), b)
     mine = pl.ds(pl.multiple_of(x * hb, 16), hb)
     theirs = pl.ds(pl.multiple_of((1 - x) * hb, 16), hb)
-    d_k = [n.send(gd.at[:, row(2 * yy + 1 - k)], rd.at[yy], n.kp) for yy in range(2)]
-    u_k = [n.send(gu.at[:, row(2 * yy + 1 - k)], ru.at[yy], n.kp) for yy in range(2)]
-    l_d = [n.local(gd.at[:, row(2 * yy + k)], hd.at[yy]) for yy in range(2)]
-    l_u = [n.local(gu.at[:, row(2 * yy + k)], hu.at[yy]) for yy in range(2)]
+    l_d = [n.local(gd, hd)]
+    l_u = [n.local(gu, hu)]
     oz = pl.ds(2 * k, 2)
     a_k = [n.send(ga.at[:, row(2 * yy + 1 - k)], ha.at[yy, oz], n.kp) for yy in range(2)]
     l_a = [n.local(ga.at[:, row(2 * yy + k)], ha.at[yy, oz]) for yy in range(2)]
     s_k = n.send(sv, svk, n.kp)
-    rows = lo.shape[0]; main = rows - 16
+    rows = g1.shape[0]; main = rows - 16
     gs[pl.ds(0, main), :] = gpart[pl.ds(pl.multiple_of((1 - k) * main, 16), main), :].astype(BF)
     gs[pl.ds(main, 16), :] = gpart[pl.ds(pl.multiple_of(2 * main + (1 - k) * 16, 16), 16), :].astype(BF)
     g_k = n.send(gs, gr, n.kp)
 
-    def split(get, dst):
-        def step(i, _):
-            r = pl.ds(pl.multiple_of(i * CH, 16), CH)
-            v = get(r)
-            for cc in range(4):
-                dst[cc, r, :] = v[:, cc * b:(cc + 1) * b].astype(BF)
-            return 0
-        lax.fori_loop(0, rows // CH, step, 0)
     def spread(src, dst):
         l = n.local(src.at[c], dst.at[y, k])
         return l, [n.send(src.at[lax.rem(c + 2, 4)], dst.at[y, k], n.yp), n.send(src.at[3 - c], dst.at[y, k], n.ykp), n.send(src.at[c + 1 - 2 * k], dst.at[y, k], n.kp)]
 
-    for cp in d_k:
-        cp.wait_recv()
-    for cp in l_d:
+    for cp in l_d + l_u:
         cp.wait()
     zz = lambda i: n.zs[(nz - i) % nz]
     d_y = []
     for i in list(range(1, nz)) + [0]:
-        add_to(hd.at[1 - y, n.zs[i]], rd.at[1 - y, n.zs[i]])
         d_y.append(n.send(hd.at[1 - y, n.zs[i]], dy.at[n.zs[i]], n.yp))
-    for i in range(nz):
-        add_to(hd.at[y, i], rd.at[y, i])
-    for cp in u_k:
-        cp.wait_recv()
-    for cp in l_u:
-        cp.wait()
     u_x = []
     for i in list(range(1, nz)) + [0]:
         for yy in range(2):
-            add_to(hu.at[yy, n.zs[i]], ru.at[yy, n.zs[i]])
             u_x.append(n.send(hu.at[yy, n.zs[i], theirs], ux.at[yy, n.zs[i]], n.xp))
     l_o = []
-    split(lambda r: lo[r, :].astype(F32), o4)
-    l, o_s = spread(o4, out4)
-    l_o.append(l)
     g_k.wait_recv()
 
     def total(r):
@@ -661,14 +1020,14 @@
         acc = acc + svz[i]
     n.finish()
     svo[...] = acc
-    for cp in o_s + g_s + [u_f, a_f]:
+    for cp in g_s + [u_f, a_f]:
         cp.wait_recv()
     for cp in l_o:
         cp.wait()
 
-def reduce(gu, gd, ga, lo, gpart, g1, sv, nz, nd):
-    feats, width = gu.shape[1:]
-    b = feats // 4; hb = b // 2; rows = lo.shape[0]
+def reduce(gu, gd, ga, gpart, g1, sv, nz, nd):
+    b, width = gu.shape[2:]
+    feats = 4 * b; hb = b // 2; rows = g1.shape[0]
     V = lambda *s, d=BF: pltpu.VMEM(s, d)
     vm = pl.BlockSpec(memory_space=pltpu.VMEM); an = pl.BlockSpec(memory_space=pl.ANY)
     S = jax.ShapeDtypeStruct
@@ -676,13 +1035,13 @@
     w = S((b, width), BF)
     sm = lambda: V(*sv.shape, d=F32)
     return pl.pallas_call(reduce_kernel,
-        out_shape=(o, o, w, w, S((b, width), F32), S(sv.shape, F32)),
-        in_specs=[an, an, an, vm, vm, vm, vm], out_specs=(vm,) * 6,
-        scratch_shapes=[V(2, nz, b, width)] * 5 + [V(2, nz, hb, width)] * 2 + [V(nz, 2, hb, width), V(hb, width), V(2, hb, width),
+        out_shape=(o, w, w, S((b, width), F32), S(sv.shape, F32)),
+        in_specs=[an, an, an, vm, vm, vm], out_specs=(vm,) * 5,
+        scratch_shapes=[V(2, nz, b, width)] * 3 + [V(2, nz, hb, width)] * 2 + [V(nz, 2, hb, width), V(hb, width), V(2, hb, width),
             V(nz, b, width), V(nz, b, width), V(nd, b, width), V(b, width), V(nz, hb, width), V(nz, hb, width),
-            V(4, rows, b), V(4, rows, b), V(rows, feats), V(rows, feats), sm(), sm(), sm(), V(nz, *sv.shape, d=F32), sm(),
+            V(4, rows, b), V(rows, feats), V(rows, feats), sm(), sm(), sm(), V(nz, *sv.shape, d=F32), sm(),
             pltpu.SemaphoreType.DMA((96 + nd,)), pltpu.SemaphoreType.DMA((96 + nd,)), pltpu.SemaphoreType.DMA((16,))],
-        compiler_params=pltpu.CompilerParams(collective_id=2, has_side_effects=True, vmem_limit_bytes=63*2**20))(gu, gd, ga, lo, gpart, g1, sv)
+        compiler_params=pltpu.CompilerParams(collective_id=2, has_side_effects=True, vmem_limit_bytes=63*2**20))(gu, gd, ga, gpart, g1, sv)
 
 def per_device(tokens, memory, block_ids, valid, teacher, w_qkv, bias_qv, w_out, bias_out, ln1_gain, ln1_bias, w_up, bias_up, w_down, bias_down, ln2_gain, ln2_bias):
     _, b, length = tokens.shape
@@ -697,42 +1056,19 @@
     wo = jnp.transpose(w_out)
     la = jnp.concatenate([wq[0, :, :64], wq[1, :, :64], wq[0, :, 64:128], wq[1, :, 64:128], wq[0, :, 128:], wq[1, :, 128:], wq[2], wo[:, 128:], wo[:, :128]], axis=1)
     mem = jnp.pad(jnp.swapaxes(memory, 1, 2), ((0, 0), (0, 0), (0, 128 - 2 * half)))
-    ls = jnp.concatenate([jnp.concatenate([bias_out, ln1_gain, ln1_bias, bias_down, ln2_gain, ln2_bias, bias_up]).reshape(-1, 128), bias_qv, jnp.zeros((6, 128), F32)])
-    xt, tt, wa, wu, wd, sm = gather(tokens, mem, teacher, la, w_up, w_down, ls, nz)
-    fv = 6 * b // 128
-    vecs = jnp.swapaxes(sm[0, :, :fv].reshape(4, 6, b), 0, 1).reshape(6, feats)
     scale = (valid.shape[0] * length) / jnp.sum(valid).astype(F32)
-    vec = jnp.concatenate([vecs, jnp.full((2, feats), scale, F32)])
-    bup = sm[:, 0, fv:fv + 6].reshape(nz, 1, 6 * 128)
-    bq = lax.dynamic_slice_in_dim(sm[:, 0, fv + 6:fv + 9], 2 * k, 2, 0)
-    zero = jnp.zeros((128,), F32)
-    def pair_bias(h0, h1):
-        return jnp.concatenate([h0[:64], h1[:64], zero, h0[64:], h1[64:]])
-    bias = jnp.stack([pair_bias(bq[0, 0], bq[0, 1]), pair_bias(bq[1, 0], bq[1, 1]), pair_bias(bq[0, 2], bq[1, 2])])[:, None]
+    fv = jnp.stack([bias_out, ln1_gain, ln1_bias, bias_down, ln2_gain, ln2_bias, jnp.full((b,), scale, F32), jnp.zeros((b,), F32)])
+    ls = jnp.concatenate([jnp.pad(fv, ((0, 0), (0, 256 - b))), bias_up.reshape(3, 256), jnp.pad(bias_qv.reshape(1, 384), ((0, 0), (0, 128))).reshape(2, 256), jnp.zeros((3, 256), F32)])
     ids = lax.dynamic_index_in_dim(block_ids, y, 0, keepdims=False)
     ids = jnp.concatenate([ids, jnp.full((half,), -1, jnp.int32), jnp.full((half,), length, jnp.int32), jnp.full((32 - 2 * half,), 2 * length, jnp.int32)])
     idk = jnp.broadcast_to(ids[:, None], (rows, 128))
-    wown = lax.dynamic_slice_in_dim(wa, 2 * k, 2, 0)
-    x, qt, kt, vt, mixed, lse = attn_fwd(xt, wown, bias, idk, ids[None], rows)
-    def rows_of(a, kk, axis=0):
-        return jnp.concatenate([lax.dynamic_slice_in_dim(a, kk * main, main, axis), lax.dynamic_slice_in_dim(a, length + kk * 16, 16, axis)], axis)
-    swap = [(0, 1), (1, 0), (2, 3), (3, 2)]
-    got = lax.ppermute(rows_of(mixed, 1 - k, 1), "col", swap)
-    own = rows_of(mixed, k, 1)
-    first = jnp.where(k == 0, own, got)
-    second = jnp.where(k == 0, got, own)
-    mixed_rows = jnp.concatenate([first[0], first[1], first[2], second[0], second[1], second[2]], axis=1)
     count = lax.dynamic_index_in_dim(valid, (d * nz + z) * 2 + y, 0)
-    out, g_one, g_attn, vgrad, bupgrad, gu, gd = mlp(k[None], count, mixed_rows, rows_of(x, k), tt, vec, bup, wa, wu, wd)
-    other = lax.ppermute(g_attn, "col", swap)
-    first = jnp.where(k == 0, g_attn, other)
-    second = jnp.where(k == 0, other, g_attn)
-    ga = jnp.concatenate([first[:main], second[:main], first[main:], second[main:]])
-    gpart, bgrad, gown = attn_bwd(ga, mixed, xt, qt, kt, vt, lse, idk, ids[None], wown)
+    xt, qt, kt, vt, mixed, wown, ga, hu, hd, lse, g_one, vgrad, bupgrad, out4 = forward(count, tokens, mem, teacher, la, w_up, w_down, ls, idk, ids[None], nz)
+    gpart, bgrad, gown = attn_bwd(ga, mixed, xt, qt, kt, vt, lse.reshape(3, 2, 1, rows), idk, ids[None], wown)
     bg = jnp.sum(bgrad, axis=1)[None]
     bg = jnp.where((jnp.arange(2) == k)[:, None, None], bg, 0.0).reshape(3, feats)
     sv = jnp.concatenate([jnp.sum(vgrad, axis=1), jnp.sum(bupgrad, axis=1), bg, jnp.zeros((3, feats), F32)])
-    out4, grad4, fa, fu, fd, sv = reduce(gu, gd, gown, out, gpart, g_one, sv, nz, nd)
+    grad4, fa, fu, fd, sv = reduce(hu, hd, gown, gpart, g_one, sv, nz, nd)
     layer_out = jnp.concatenate([out4[:, 0, main:main + half], out4[:, 0, :main], out4[:, 1, :main], out4[:, 0, main + half:], out4[:, 1, main:main + 2 * half - 16]], axis=1)
     grad_tokens = grad4[:, :, :main].reshape(2, length, b).astype(F32)
     grad_memory = jnp.concatenate([grad4[:, 0, main:], grad4[:, 1, main:main + 2 * half - 16]], axis=1).astype(F32)

time: 356 us -> 314 us (0.88)
  Pallas kernels: 301 us -> 273 us
  local copies, waits for them, and re-layouts: 38.2 us -> 29.1 us
    pallas_call x4 -> x2, Pallas kernels: 262 us -> 234 us  [the longest x1 133 us: forward(): pl.pallas_call(forward_kernel, out_shape=[o for o, _ in outs], out_specs=...]
    dynamic_slice x6 -> x0, local copies, waits for them, and re-layouts: 5.4 us -> none  [the longest x1 3.3 us: per_device(): wown = lax.dynamic_slice_in_dim(wa, 2 * k, 2, 0)]
    unnamed x68 -> x24, local copies, waits for them, and re-layouts: 12.3 us -> 6.94 us
    concatenate x1, local copies, waits for them, and re-layouts: 6 us -> 1.99 us  [per_device(): jnp.concatenate([out4[:, 0, main:main + half], out4[:, 0, :main], out4[:,...]
  transfers between devices with their start and end apart: 2 -> 0, of which waited for: 1 -> 0; matrix products, arithmetic and copies ran while one was open for 2% -> 0% of each run, Pallas kernels for 0% -> 0%
where the time goes in v2:
time: 314 us; the launch traced here: 313 us
  Pallas kernels  273 us (87%)
  local copies, waits for them, and re-layouts  29.1 us (9%)
  other arithmetic  9.18 us (3%)
    pallas_call x1, Pallas kernels, forward(): pl.pallas_call(forward_kernel, out_shape=[o for o, _ in outs], out_specs=...  133 us
    pallas_call x1, Pallas kernels, reduce(): pl.pallas_call(reduce_kernel, out_shape=(o, w, w, S((b, width), F32), S(s...  101 us
    pallas_call x1, Pallas kernels, attn_bwd(): pl.pallas_call(attn_bwd_kernel, out_shape=(S((rows, feats), F32), S((3, 8...  39.2 us
    unnamed x24, local copies, waits for them, and re-layouts  6.94 us

profile of v2, /device:TPU:0, one launch (start us, length us, event | category | flops | bytes accessed | tf_op | source)
XLA Modules:
  0.0 313.1 jit_solution(13438689707268009919)
XLA Ops:
  0.6 0.0 copy-start.1
  0.7 1.3 reduce_sum.36
  2.8 1.2 dynamic_slice.23.valid_ref
  4.0 0.5 iota_compare_fusion.1
  4.5 0.1 pad.46.clone
  4.6 0.7 copy.54
  5.3 0.7 constant_dynamic-slice_fusion.3
  6.0 0.1 concatenate.64
  6.1 0.7 reshape.143
  6.8 0.6 broadcast_in_dim.40.idq
  7.4 0.8 stack.49
  8.2 0.7 fusion.1.ls
  8.9 0.0 copy-done.5
  8.9 1.4 slice_reduce_fusion
  10.3 0.1 squeeze.79
  10.4 0.9 copy.40
  11.3 0.7 pad.12.mem
  12.0 0.0 copy-done.4
  12.0 0.1 copy.41
  12.1 0.0 copy-done.1
  12.1 0.3 reshape.142
  12.4 0.1 slice_bitcast_fusion.2
  12.5 0.9 concatenate.62.la
  13.4 1.0 broadcast_in_dim.39.idk
  14.4 132.7 %shard_map.280 = (bf16[768,1152]{1,0:T(8,128)(2,1)}, bf16[3,1056,128]{2,1,0:T(8,128)(2,1)}, bf16[3,1056,128]{2,1,0:T(8,128)(2,1)}, bf16[3,1056,128]{2,1,0:T(8,12...) custom-call(s32[1]{0:T(128)} %dynamic_slice.23.valid_ref, ...), custom_call_target="tpu_custom_call" | custom-call | tf_op jit(solution)/shard_map/pallas_call | solution.py:851
  147.1 0.7 slice_bitcast_fusion.12
  147.8 0.7 slice_bitcast_fusion.10
  148.6 0.9 reduce_sum.38
  149.5 0.7 slice_bitcast_fusion.8
  150.2 0.9 reduce_sum.37
  151.2 1.1 slice_bitcast_fusion
  152.2 1.1 slice_bitcast_fusion.1
  153.3 2.0 concatenate.65
  155.3 1.3 copy.44
  156.6 39.2 %shard_map.281 = (f32[1056,768]{1,0:T(8,128)}, f32[3,8,384]{2,1,0:T(8,128)}, bf16[2,768,768]{2,1,0:T(8,128)(2,1)}) custom-call(bf16[1056,768]{1,0:T(8,128)(2,1)} %get-tuple-element.40.ga, bf16[3,1056,128]{2,1,0:T(8,128)(2,1)} %get-tuple-element.41.mixed, bf16[768,1152]{1,0:T(8,128)(2,1)} %get-tuple-element.42.xt, ...), custom_call_target="tpu_custom_call" | custom-call | tf_op jit(solution)/shard_map/pallas_call | solution.py:349
  195.9 0.8 reduce_sum.39
  196.7 0.1 broadcast_select_fusion
  196.8 0.0 copy-done.6
  196.8 0.7 maximum_maximum_fusion.sv
  197.5 101.3 %shard_map.282 = (bf16[2,2,528,192]{3,2,1,0:T(8,128)(2,1)}, bf16[192,768]{1,0:T(8,128)(2,1)}, bf16[192,768]{1,0:T(8,128)(2,1)}, f32[192,768]{1,0:T(8,128)}, f32[16,768]{1,0:T(8,128)}) custom-call(bf16[2,4,192,768]{3,2,1,0:T(8,128)(2,1)} %get-tuple-element.38.gu, bf16[2,4,192,768]{3,2,1,0:T(8,128)(2,1)} %get-tuple-element.39.gd, ...), custom_call_target="tpu_custom_call" | custom-call | tf_op jit(solution)/shard_map/pallas_call | solution.py:1037
  298.7 0.7 slice_bitcast_fusion.11
  299.4 0.8 slice.195
  300.2 0.6 dynamic-slice_reduce_fusion
  300.8 0.7 slice.176
  301.6 0.7 slice.191
  302.3 0.7 fusion.5
  303.0 0.1 fusion.2
  303.1 0.1 maximum_bitcast_fusion.1
  303.2 0.1 broadcast_select_fusion.1
  303.3 0.6 pad_maximum_fusion.3
  303.8 0.7 slice_bitcast_fusion.9
  304.6 1.4 slice.166
  305.9 0.6 copy.46
  306.6 0.2 stack.52
  306.8 0.9 convert_element_type.29
  307.7 0.1 fusion.4
  307.8 0.8 copy.47
  308.6 0.2 pad_maximum_fusion.1
  308.8 0.2 stack.50
  309.0 0.2 stack.51
  309.2 1.2 pad_maximum_fusion
  310.4 0.2 bitcast_convert_fusion
  310.6 1.7 copy.45
  312.3 0.8 copy.56
  (27 shorter events, 0.2 us)
Async XLA Ops:
  0.6 11.5 %copy-start.1 = (bf16[3,36864]{1,0:T(4,128)(2,1)S(1)}, bf16[3,36864]{1,0:T(4,128)(2,1)}, u32[]{:S(2)}) copy-start(bf16[3,36864]{1,0:T(4,128)(2,1)} %param.22) | copy-start | bytes 663556
  0.7 11.3 %copy-start.4 = (bf16[192,192]{1,0:T(8,128)(2,1)S(1)}, bf16[192,192]{1,0:T(8,128)(2,1)}, u32[]{:S(2)}) copy-start(bf16[192,192]{1,0:T(8,128)(2,1)} %param.24) | copy-start | bytes 221188
  4.6 4.3 %copy-start.5 = (f32[16]{0:T(128)}, f32[16]{0:T(128)S(1)}, u32[]{:S(2)}) copy-start(f32[16]{0:T(128)S(1)} %pad.46.clone) | copy-start | bytes 196
  156.6 40.0 %copy-start.7 = (pred[2]{0:T(512)(128)(4,1)S(1)}, pred[2]{0:T(512)(128)(4,1)}, u32[]{:S(2)}) copy-start(pred[2]{0:T(512)(128)(4,1)} %iota_compare_fusion.1) | copy-start | bytes 10
  156.6 40.1 %copy-start.6 = (f32[16]{0:T(128)S(1)}, f32[16]{0:T(128)}, u32[]{:S(2)}) copy-start(f32[16]{0:T(128)} %copy-done.5) | copy-start | bytes 196
  304.6 2.0 copy-start
  304.6 2.2 copy-start.3
  310.6 1.7 copy-start.2

commit v3 on v2

--- a/solution.py
+++ b/solution.py
@@ -851,197 +851,395 @@
     return pl.pallas_call(forward_kernel, out_shape=[o for o, _ in outs], out_specs=[s for _, s in outs],
         in_specs=[sm, an, an, an, an, an, an, an, vm, vm], scratch_shapes=scratch,
         compiler_params=pltpu.CompilerParams(collective_id=1, has_side_effects=True, vmem_limit_bytes=67043328))(valid, tok, mem, tch, la, lu, ld, ls, idk, idq)
-class OldNet:
-    def __init__(self, send_sems, recv_sems, local_sems):
-        self.ss, self.rs, self.ls = send_sems, recv_sems, local_sems
-        self.count, self.locals, self.sent = 0, 0, []
-        self.d, self.z, self.c = (lax.axis_index(a) for a in ("dp", "row", "col"))
-        self.nd, self.nz = lax.axis_size("dp"), lax.axis_size("row")
-        self.y, self.k = self.c // 2, self.c % 2
-        self.x = self.d % 2
-        self.xp = (self.d + 1 - 2 * self.x, self.z, self.c)
-        self.yp = (self.d, self.z, lax.rem(self.c + 2, 4))
-        self.kp = (self.d, self.z, self.c + 1 - 2 * self.k)
-        self.ykp = (self.d, self.z, 3 - self.c)
-        self.zs = [lax.rem(self.z + i, self.nz) for i in range(self.nz)]
-        self.zp = [(self.d, zz, self.c) for zz in self.zs]
-        self.others = [(lax.rem(self.d + 2 * i, self.nd), self.z, self.c) for i in range(1, self.nd // 2)]
-
-    def barrier(self, peers):
-        b = pltpu.get_barrier_semaphore()
-        for p in peers:
-            pl.semaphore_signal(b, inc=1, device_id=p, device_id_type=MESH)
-        pl.semaphore_wait(b, len(peers))
-
-    def send(self, src, dst, dev):
-        i = self.count
-        self.count += 1
-        c = pltpu.make_async_remote_copy(src_ref=src, dst_ref=dst, send_sem=self.ss.at[i], recv_sem=self.rs.at[i], device_id=dev, device_id_type=MESH)
-        c.start()
-        self.sent.append(c)
-        return c
-
-    def local(self, src, dst):
-        c = pltpu.make_async_copy(src, dst, self.ls.at[self.locals])
-        self.locals += 1
-        c.start()
-        return c
-
-    def finish(self):
-        for c in self.sent:
-            c.wait_send()
-
-
-def sum_refs(refs):
+def total_of(refs):
     acc = refs[0][...].astype(F32)
     for r in refs[1:]:
         acc = acc + r[...].astype(F32)
     return acc
 
-def reduce_kernel(gu, gd, ga, gpart, g1, sv, grad4, fa, fu, fd, svo,
-                  hu, hd, ha, ux, ax, uz, uy, ut, dy, dz, dx, df, ay, az, g4, gs, gr, svk, svy, svx, svz, svt, ss, rs, lsem):
-    n = OldNet(ss, rs, lsem)
-    n.barrier(n.zp[1:] + [n.yp, n.ykp, n.kp, n.xp] + n.others)
-    nz, y, k, c, z, x = n.nz, n.y, n.k, n.c, n.z, n.x
+class Piece:
+    def __init__(self, n, env, col0, num, js, x_first):
+        self.n, self.x_first = n, x_first
+        gown, ha, ax, ay, ayf, axf, mine, theirs, order = env
+        C = pl.ds(col0, num); y, k = n.y, n.k
+        self.core = [n.move((lambda j=j, yy=yy: gown.at[j, 2 * yy + 1 - k, :, C]), (lambda j=j, yy=yy: ha.at[yy, 2 * k + j, :, C]), n.kp) for j in js for yy in range(2)]
+        self.keep = [n.copy((lambda j=j, yy=yy: gown.at[j, 2 * yy + k, :, C]), (lambda j=j, yy=yy: ha.at[yy, 2 * k + j, :, C])) for j in js for yy in range(2)]
+        zz = order if len(js) == 2 else [js[0], js[0] + 2]
+        self.first, self.second, self.add1, self.add2 = [], [], [], []
+        for q in zz:
+            if x_first:
+                self.first.append(n.move((lambda q=q: ha.at[:, q, theirs, C]), (lambda q=q: ax.at[:, q, :, C]), n.xp))
+                self.add1.append(lambda q=q: [add_to(ha.at[yy, q, mine, C], ax.at[yy, q, :, C]) for yy in range(2)])
+                self.second.append(n.move((lambda q=q: ha.at[1 - y, q, mine, C]), (lambda q=q: ay.at[q, :, C]), n.yp))
+                self.add2.append(lambda q=q: add_to(ha.at[y, q, mine, C], ay.at[q, :, C]))
+            else:
+                self.first.append(n.move((lambda q=q: ha.at[1 - y, q, :, C]), (lambda q=q: ayf.at[q, :, C]), n.yp))
+                self.add1.append(lambda q=q: add_to(ha.at[y, q, :, C], ayf.at[q, :, C]))
+                self.second.append(n.move((lambda q=q: ha.at[y, q, theirs, C]), (lambda q=q: axf.at[q, :, C]), n.xp))
+                self.add2.append(lambda q=q: add_to(ha.at[y, q, mine, C], axf.at[q, :, C]))
+    def start(self):
+        for m in self.core + self.keep:
+            m.start()
+    def ev1(self):
+        for m in self.core:
+            m.wait_recv()
+        for m in self.keep:
+            m.wait()
+        for m in self.first:
+            m.start()
+    def ev2(self):
+        for m, f, s in zip(self.first, self.add1, self.second):
+            m.wait_recv(); f(); s.start()
+    def ev3(self):
+        for m, f in zip(self.second, self.add2):
+            m.wait_recv(); f()
+
+class Rows:
+    def __init__(self, n, here, z1, z2, e, dev1, dev2, add):
+        e1, e2, e3 = e
+        self.a = n.move((lambda: here(e3)), (lambda: z1(1)), dev1)
+        self.b = n.move((lambda: here(e1)), (lambda: z1(0)), dev1)
+        self.c = n.move((lambda: here(e2)), z2, dev2)
+        self.mid = lambda: add(here(e2), z1(1))
+    def start(self):
+        self.a.start(); self.b.start()
+    def middle(self):
+        self.a.wait_recv(); self.mid(); self.c.start()
+    def end(self):
+        self.b.wait_recv(); self.c.wait_recv()
+
+def backward_kernel(hu_h, hd_h, ga_h, mixed_h, xt_h, q_h, k_h, v_h, w_h, o4_h, g1_h, lse, vgrad, bupgrad, idk, idq,
+                    grad4, lout, gmem, g3, gwo, fu, fd, fvec, bup, bqv,
+                    hu, hd, ux, uz1, uz2, ut, uy, fub, pu, dy, dz1, dz2, df, dx, pd,
+                    ha, ax, ay, ayf, axf, az1, az2, fa, pa, gown,
+                    ga, mixed, xt, qt, kt, vt, w, o4, g1, wp, wt, gat, gm, gp, dv, dk, dqt, ktt, dd, g4, gs, gr, lo32,
+                    sv, svk, svt, svy, svo, svx, ps, svz, ss, rs, lsem):
+    n = Net(ss, rs, lsem)
+    nz, y, k, c, z, x, d, nd = n.nz, n.y, n.k, n.c, n.z, n.x, n.d, n.nd
     b = fu.shape[0]; hb = b // 2
-    row = lambda cc: pl.ds(pl.multiple_of(cc * b, 16), b)
+    rows, feats = ga.shape
+    own_rows = g1.shape[0]; main = own_rows - 16; length = 2 * main
     mine = pl.ds(pl.multiple_of(x * hb, 16), hb)
     theirs = pl.ds(pl.multiple_of((1 - x) * hb, 16), hb)
-    l_d = [n.local(gd, hd)]
-    l_u = [n.local(gu, hu)]
-    oz = pl.ds(2 * k, 2)
-    a_k = [n.send(ga.at[:, row(2 * yy + 1 - k)], ha.at[yy, oz], n.kp) for yy in range(2)]
-    l_a = [n.local(ga.at[:, row(2 * yy + k)], ha.at[yy, oz]) for yy in range(2)]
-    s_k = n.send(sv, svk, n.kp)
-    rows = g1.shape[0]; main = rows - 16
-    gs[pl.ds(0, main), :] = gpart[pl.ds(pl.multiple_of((1 - k) * main, 16), main), :].astype(BF)
-    gs[pl.ds(main, 16), :] = gpart[pl.ds(pl.multiple_of(2 * main + (1 - k) * 16, 16), 16), :].astype(BF)
-    g_k = n.send(gs, gr, n.kp)
-
-    def spread(src, dst):
-        l = n.local(src.at[c], dst.at[y, k])
-        return l, [n.send(src.at[lax.rem(c + 2, 4)], dst.at[y, k], n.yp), n.send(src.at[3 - c], dst.at[y, k], n.ykp), n.send(src.at[c + 1 - 2 * k], dst.at[y, k], n.kp)]
-
-    for cp in l_d + l_u:
-        cp.wait()
-    zz = lambda i: n.zs[(nz - i) % nz]
-    d_y = []
-    for i in list(range(1, nz)) + [0]:
-        d_y.append(n.send(hd.at[1 - y, n.zs[i]], dy.at[n.zs[i]], n.yp))
-    u_x = []
-    for i in list(range(1, nz)) + [0]:
+    all_of = lambda r: (lambda: r)
+    l_w, l_ga, l_m = [n.local(all_of(s), all_of(t)) for s, t in ((w_h, w), (ga_h, ga), (mixed_h, mixed))]
+    l_q = [n.local(all_of(s), all_of(t)) for s, t in ((k_h, kt), (q_h, qt), (v_h, vt))]
+    l_x = n.local(all_of(xt_h), all_of(xt))
+    l_d = n.local(lambda: hd_h.at[y], lambda: hd)
+    l_u = n.local(lambda: hu_h.at[:, :, mine], lambda: hu)
+    l_o = [n.local(all_of(o4_h), all_of(o4)), n.local(all_of(g1_h), all_of(g1))]
+    n.barrier(n.zp[1:] + [n.yp, n.ykp, n.kp, n.xp] + n.others)
+    e1 = z + 1 - 2 * lax.rem(z, 2)
+    e2 = lax.rem(z + 2, nz)
+    e3 = lax.rem(e1 + 2, nz)
+    e = (e1, e2, e3)
+    order = [e3, e1, e2, z]
+    dev1, dev2 = (d, e1, c), (d, e2, c)
+    d_y = [n.send((lambda q=q: hd_h.at[1 - y, q]), (lambda q=q: dy.at[q]), n.yp) for q in order]
+    u_x = [n.send((lambda q=q: hu_h.at[:, q, theirs]), (lambda q=q: ux.at[:, q]), n.xp) for q in order]
+
+    def add2(a, s):
         for yy in range(2):
-            u_x.append(n.send(hu.at[yy, n.zs[i], theirs], ux.at[yy, n.zs[i]], n.xp))
-    l_o = []
+            add_to(a.at[yy], s.at[yy])
+    dz = Rows(n, lambda q: hd.at[q], lambda s: dz1.at[s], lambda: dz2, e, dev1, dev2, add_to)
+    uz = Rows(n, lambda q: hu.at[:, q], lambda s: uz1.at[s], lambda: uz2, e, dev1, dev2, add2)
+    d_x = n.move(all_of(df), all_of(dx), n.xp)
+    u_y = n.move(lambda: ut.at[1 - y], all_of(uy), n.yp)
+    u_f = n.move(lambda: fub.at[mine], lambda: fub.at[mine], n.xp)
+
+    mypair = d // 2
+
+    def pairs_sum(value, slots, view):
+        if nd == 2:
+            return value
+        view(slots, mypair)[...] = value.astype(slots.dtype)
+        ms = [n.send((lambda: view(slots, mypair)), (lambda: view(slots, mypair)), o) for o in n.others]
+        for m in ms:
+            m.wait_recv()
+        return total_of([view(slots, i) for i in range(nd // 2)])
+
+    def ev_dy(j):
+        def run():
+            d_y[j].wait_recv()
+            if j == 0:
+                l_d.wait()
+            add_to(hd.at[order[j]], dy.at[order[j]])
+            if j == 1:
+                dz.start()
+        return run
+    def ev_ux(j):
+        def run():
+            u_x[j].wait_recv()
+            if j == 0:
+                l_u.wait()
+            add2(hu.at[:, order[j]], ux.at[:, order[j]])
+            if j == 1:
+                uz.start()
+        return run
+    def ev_df():
+        dz.end()
+        df[...] = total_of([hd.at[z], dz1.at[0], dz2]).astype(BF)
+        d_x.start()
+    def ev_ut():
+        uz.end()
+        for yy in range(2):
+            ut[yy] = total_of([hu.at[yy, z], uz1.at[0, yy], uz2.at[yy]]).astype(BF)
+        u_y.start()
+    def ev_uf():
+        u_y.wait_recv()
+        fub[mine, :] = pairs_sum(total_of([ut.at[y], uy]), pu, lambda s, i: s.at[i]).astype(BF)
+        u_f.start()
+    env = (gown, ha, ax, ay, ayf, axf, mine, theirs, order)
+    PO = Piece(n, env, 640, 128, (0, 1), True)
+    P0 = Piece(n, env, 0, 384, (0,), True)
+    P1 = Piece(n, env, 0, 384, (1,), False)
+    P2 = Piece(n, env, 384, 128, (0, 1), True)
+    P3 = Piece(n, env, 512, 128, (0, 1), False)
+    class Cols:
+        def __init__(self, col0, num):
+            C = pl.ds(col0, num)
+            self.C = C
+            self.z = Rows(n, lambda q: ha.at[y, q, mine, C], lambda s: az1.at[s, :, C], lambda: az2.at[:, C], e, dev1, dev2, add_to)
+            self.f = n.move(lambda: fa.at[mine, C], lambda: fa.at[mine, C], n.xp)
+        def end(self):
+            self.z.end()
+            C = self.C
+            fa[mine, C] = pairs_sum(total_of([ha.at[y, z, mine, C], az1.at[0, :, C], az2.at[:, C]]), pa, lambda s, i: s.at[i, :, C]).astype(BF)
+            self.f.start()
+    ZO, Z01, Z2, Z3 = Cols(640, 128), Cols(0, 384), Cols(384, 128), Cols(512, 128)
+    l_w.wait(); l_ga.wait()
+    gat[...] = ga[...].T
+    assemble_pairs(w, wp, feats)
+    wt[:, pl.ds(0, 128)] = w[0, :, pl.ds(640, 128)]
+    wt[:, pl.ds(128, 128)] = w[1, :, pl.ds(640, 128)]
+    lo = lax.broadcasted_iota(jnp.int32, (feats, 128), 1) < 64
+    wt[:, pl.ds(256, 128)] = jnp.where(lo, pltpu.roll(w[0, :, pl.ds(512, 128)].astype(F32), 64, 1), w[1, :, pl.ds(512, 128)].astype(F32)).astype(BF)
+    r3 = rows // 3
+
+    def mixed_grad(i, _):
+        r = pl.ds(pl.multiple_of(i * r3, 16), r3)
+        v = nn(ga[r, :], wt[...])
+        for p in range(3):
+            gm[p, r, :] = v[:, 128 * p:128 * p + 128].astype(BF)
+        return 0
+    lax.fori_loop(0, 3, mixed_grad, 0)
+    l_m.wait()
+    for cc in range(4):
+        af = gat[pl.ds(b * cc, b), :]
+        for j in range(2):
+            gown[j, cc, :, pl.ds(640, 128)] = nn(af, mixed[j]).astype(BF)
+    PO.start()
+    for m in l_q:
+        m.wait()
+    l_x.wait()
+    table = {0: [ev_dy(0), ev_ux(0)], 1: [PO.ev1], 3: [ev_dy(1), ev_ux(1)], 6: [ev_dy(2), P0.ev1], 7: [dz.middle, ev_ux(2)],
+             9: [ev_dy(3)], 10: [ev_ux(3), uz.middle], 12: [P1.ev1, PO.ev2], 13: [ev_df], 14: [P0.ev2], 15: [ev_ut, PO.ev3, ZO.z.start], 16: [P1.ev2], 17: [P0.ev3, ev_uf]}
+    cuts = {1: 0, 3: 1, 4: 2}
+
+    def head(i, _):
+        p = i // 2
+        h = i % 2
+        he = pl.ds(pl.multiple_of(64 * h, 64), 64)
+
+        @pl.when(h == 0)
+        def _():
+            ktt[...] = kt[p].T
+            prod = (gm[p].astype(F32) * mixed[p].astype(F32)).T
+            dd[0] = jnp.sum(prod[:64, :], axis=0, keepdims=True)
+            dd[1] = jnp.sum(prod[64:, :], axis=0, keepdims=True)
+            dv[...] = jnp.zeros_like(dv)
+            dk[...] = jnp.zeros_like(dk)
+        lanes = (lax.broadcasted_iota(jnp.int32, (1, 128), 1) // 64) == h
+        for t, (q0, qn, spans) in enumerate(tiles(rows, length)):
+            q = qt[p, pl.ds(q0, qn), :]
+            qm = jnp.where(lanes, q, jnp.zeros_like(q))
+            g = gm[p, pl.ds(q0, qn), :]
+            gmm = jnp.where(lanes, g, jnp.zeros_like(g))
+            sc = scores_of(kt, qm, idk, idq[0:1, pl.ds(q0, qn)], p, spans)
+            l = lse[i, :, pl.ds(q0, qn)]
+            dl = dd[h, :, pl.ds(q0, qn)]
+            acc = None
+            for s, (k0, kn, _) in zip(sc, spans):
+                pr = jnp.exp(s - l)
+                dp = nt(vt[p, pl.ds(k0, kn), :], gmm)
+                ds = (pr * (dp - dl)).astype(BF)
+                dv[pl.ds(k0, kn), :] += nn(pr.astype(BF), gmm)
+                dk[pl.ds(k0, kn), :] += nn(ds, qm)
+                o = nn(ktt[he, pl.ds(k0, kn)], ds)
+                acc = o if acc is None else acc + o
+            dqt[he, pl.ds(q0, qn)] = acc * 0.125
+            if t in cuts:
+                at(3 * i + cuts[t], table)
+
+        @pl.when(h == 1)
+        def _():
+            gp[p, :, pl.ds(0, 128)] = dqt[...].T.astype(BF)
+            gp[p, :, pl.ds(128, 128)] = dk[...].astype(BF)
+            gp[p, :, pl.ds(256, 128)] = dv[...].astype(BF)
+
+        @pl.when(jnp.logical_and(h == 1, p < 2))
+        def _():
+            def part(cc, _):
+                f = pl.ds(pl.multiple_of(b * cc, 16), b)
+                gown[p, cc, :, pl.ds(0, 384)] = nn(xt[f, pl.ds(0, rows)], gp[p]).astype(BF)
+                return 0
+            lax.fori_loop(0, 4, part, 0)
+        at(i, {1: [P0.start], 3: [P1.start]})
+        return 0
+    lax.fori_loop(0, 6, head, 0)
+    sw = lambda a: pltpu.roll(a, 64, 1)
+
+    def last(cc, _):
+        f = pl.ds(pl.multiple_of(b * cc, 16), b)
+        r2 = nn(xt[f, pl.ds(0, rows)], gp[2])
+        o2 = nn(gat[f, :], mixed[2])
+        lo = lax.broadcasted_iota(jnp.int32, (b, 128), 1) < 64
+        rq, rk, rv = r2[:, :128], r2[:, 128:256], r2[:, 256:]
+        gown[0, cc, :, pl.ds(384, 128)] = jnp.where(lo, rq, sw(rk)).astype(BF)
+        gown[1, cc, :, pl.ds(384, 128)] = jnp.where(lo, sw(rq), rk).astype(BF)
+        gown[0, cc, :, pl.ds(512, 128)] = jnp.where(lo, rv, sw(o2)).astype(BF)
+        gown[1, cc, :, pl.ds(512, 128)] = jnp.where(lo, sw(rv), o2).astype(BF)
+        return 0
+    lax.fori_loop(0, 4, last, 0)
+    P2.start(); P3.start()
+    def rowsgrad(r):
+        return nt(gp[0, r, :], wp[0]) + nt(gp[1, r, :], wp[1]) + nt(gp[2, r, :], wp[2])
+
+    def half_rows(kk, put):
+        def chunk(i, _):
+            put(pl.ds(pl.multiple_of(i * 256, 16), 256), rowsgrad(pl.ds(pl.multiple_of(kk * main + i * 256, 16), 256)))
+            return 0
+        lax.fori_loop(0, main // 256, chunk, 0)
+        put(pl.ds(main, 16), rowsgrad(pl.ds(pl.multiple_of(length + kk * 16, 16), 16)))
+    def put_other(r, v):
+        gs[r, :] = v.astype(BF)
+    half_rows(1 - k, put_other)
+    g_k = n.send(all_of(gs), all_of(gr), n.kp)
+    P2.ev1(); P3.ev1()
+    sv[...] = jnp.zeros_like(sv)
+    for i in range(6):
+        sv[pl.ds(i, 1), :] = jnp.sum(vgrad[i], axis=0, keepdims=True)
+    for i in range(nz):
+        sv[pl.ds(6 + i, 1), :] = jnp.sum(bupgrad[i], axis=0, keepdims=True)
+    for p in range(3):
+        t = jnp.sum(group_sum(gp[p].astype(F32)), axis=0, keepdims=True)
+        sv[pl.ds(6 + nz + p, 1), pl.ds(0, 384)] = jnp.where(k == 0, t, 0.0)
+        sv[pl.ds(6 + nz + p, 1), pl.ds(384, 384)] = jnp.where(k == 1, t, 0.0)
+    s_k = n.send(all_of(sv), all_of(svk), n.kp)
+    P1.ev3()
+    Z01.z.start()
+    ZO.z.middle()
+    for m in l_o:
+        m.wait()
+    def put_own(r, v):
+        g1[r, :] = g1[r, :] + v
+    half_rows(k, put_own)
+    P2.ev2(); P3.ev2()
+    s_k.wait_recv()
+    svt[...] = sv[...] + svk[...]
+    s_y = n.send(all_of(svt), all_of(svy), n.yp)
     g_k.wait_recv()
 
-    def total(r):
-        return gr[r, :].astype(F32) + g1[r, :]
     def own(i, _):
-        r = pl.ds(pl.multiple_of(i * 16, 16), 16)
-        src = jnp.where(i < main // 16, k * main + i * 16, 2 * main + k * 16)
-        v = gpart[pl.ds(pl.multiple_of(src, 16), 16), :] + gr[r, :].astype(F32) + g1[r, :]
+        r = pl.ds(pl.multiple_of(i * 48, 16), 48)
+        v = g1[r, :] + gr[r, :].astype(F32)
         for cc in range(4):
             g4[cc, r, :] = v[:, cc * b:(cc + 1) * b].astype(BF)
         return 0
-    lax.fori_loop(0, rows // 16, own, 0)
-    l, g_s = spread(g4, grad4)
-    l_o.append(l)
-    for cp in a_k:
-        cp.wait_recv()
-    for cp in l_a:
-        cp.wait()
-    a_x = []
-    for yy in (0, 1):
-        for i in list(range(1, nz)) + [0]:
-            yv = 1 - y if yy == 0 else y
-            a_x.append(n.send(ha.at[yv, n.zs[i], theirs], ax.at[yv, n.zs[i]], n.xp))
-    s_k.wait_recv()
-    svt[...] = sv[...] + svk[...]
-    s_y = n.send(svt, svy, n.yp)
-    d_z = []
-    for j, i in enumerate(list(range(1, nz)) + [0]):
-        d_y[j].wait_recv()
-        add_to(hd.at[y, n.zs[i]], dy.at[n.zs[i]])
-        if i:
-            d_z.append(n.send(hd.at[y, n.zs[i]], dz.at[i], n.zp[i]))
+    lax.fori_loop(0, own_rows // 48, own, 0)
+    g_l = n.local(lambda: g4.at[c], lambda: grad4.at[y, k])
+    dst = lambda: grad4.at[y, k]
+    g_s = [n.send(lambda: g4.at[n.oc], dst, n.yp), n.send(lambda: g4.at[3 - c], dst, n.ykp), n.send(lambda: g4.at[c + 1 - 2 * k], dst, n.kp)]
+    P2.ev3(); Z2.z.start()
+    P3.ev3(); Z3.z.start()
     s_y.wait_recv()
     svo[...] = svt[...] + svy[...]
-    s_x = n.send(svo, svx, n.xp)
-    u_z = []
-    for j, i in enumerate(list(range(1, nz)) + [0]):
-        for yy in range(2):
-            u_x[2 * j + yy].wait_recv()
-            add_to(hu.at[yy, n.zs[i], mine], ux.at[yy, n.zs[i]])
-            if i:
-                u_z.append(n.send(hu.at[yy, n.zs[i], mine], uz.at[i, yy], n.zp[i]))
-    a_y = []
-    for j, i in enumerate(list(range(1, nz)) + [0]):
-        a_x[j].wait_recv()
-        add_to(ha.at[1 - y, n.zs[i], mine], ax.at[1 - y, n.zs[i]])
-        a_y.append(n.send(ha.at[1 - y, n.zs[i], mine], ay.at[n.zs[i]], n.yp))
-    for j, i in enumerate(list(range(1, nz)) + [0]):
-        a_x[nz + j].wait_recv()
-        add_to(ha.at[y, n.zs[i], mine], ax.at[y, n.zs[i]])
-    for cp in d_z:
-        cp.wait_recv()
-    df[...] = sum_refs([hd.at[y, z]] + [dz.at[i] for i in range(1, nz)]).astype(BF)
-    me = n.d
-    d_d = [n.send(df, dx.at[n.d], (lax.rem(n.d + i, n.nd), n.z, n.c)) for i in range(1, n.nd)]
-    l_f = n.local(df, dx.at[n.d])
+    s_x = n.send(all_of(svo), all_of(svx), n.xp)
+    Z01.z.middle(); ZO.end()
+    half = (lout.shape[1] - length) // 2
+    for s in range(2):
+        lo32[pl.ds(0, half), :] = o4[s, 0, pl.ds(main, 16), :].astype(F32)[:half]
+        lo32[pl.ds(half, main), :] = o4[s, 0, pl.ds(0, main), :].astype(F32)
+        lo32[pl.ds(half + main, main), :] = o4[s, 1, pl.ds(0, main), :].astype(F32)
+        lo32[pl.ds(half + length, 16 - half), :] = o4[s, 0, pl.ds(main, 16), :].astype(F32)[half:]
+        lo32[pl.ds(length + 16, 2 * half - 16), :] = o4[s, 1, pl.ds(main, 16), :].astype(F32)[:2 * half - 16]
+        lout[s] = lo32[pl.ds(0, length + 2 * half), :].astype(BF)
+    Z2.z.middle(); Z3.z.middle()
     s_x.wait_recv()
-    svt2 = svo[...] + svx[...]
-    svz[z] = svt2
-    s_z = [n.send(svz.at[z], svz.at[z], n.zp[i]) for i in range(1, nz)]
-    for cp in u_z:
-        cp.wait_recv()
-    for yy in range(2):
-        ut[yy] = sum_refs([hu.at[yy, z, mine]] + [uz.at[i, yy] for i in range(1, nz)]).astype(BF)
-    u_y = n.send(ut.at[1 - y], uy, n.yp)
-    a_z = []
-    for j, i in enumerate(list(range(1, nz)) + [0]):
-        a_y[j].wait_recv()
-        add_to(ha.at[y, n.zs[i], mine], ay.at[n.zs[i]])
-        if i:
-            a_z.append(n.send(ha.at[y, n.zs[i], mine], az.at[i], n.zp[i]))
-    u_y.wait_recv()
-    fu[mine, :] = sum_refs([ut.at[y], uy]).astype(BF)
-    u_f = n.send(fu.at[mine], fu.at[mine], n.xp)
-    for cp in a_z:
-        cp.wait_recv()
-    fa[mine, :] = sum_refs([ha.at[y, z, mine]] + [az.at[i] for i in range(1, nz)]).astype(BF)
-    a_f = n.send(fa.at[mine], fa.at[mine], n.xp)
-    l_f.wait()
-    for cp in d_d + s_z:
-        cp.wait_recv()
-    fd[...] = sum_refs([dx.at[i] for i in range(n.nd)])
+    svz[z] = pairs_sum(svo[...] + svx[...], ps, lambda s, i: s.at[i])
+    s_z = [n.send(lambda: svz.at[z], lambda: svz.at[z], n.zp[i]) for i in range(1, nz)]
+    Z01.end()
+    d_x.wait_recv()
+    fd[...] = pairs_sum(total_of([df, dx]), pd, lambda s, i: s.at[i])
+    u_f.wait_recv()
+    fu[...] = fub[...].astype(F32)
+    Z2.end(); Z3.end()
+    for m in s_z:
+        m.wait_recv()
     acc = svz[0]
     for i in range(1, nz):
         acc = acc + svz[i]
+    pick = jnp.where(c == 0, acc[:8, 0:b], 0.0)
+    for cc in range(1, 4):
+        pick = pick + jnp.where(c == cc, acc[:8, cc * b:(cc + 1) * b], 0.0)
+    fvec[...] = pick
+    t = jnp.where(z == 0, acc[6:7], 0.0)
+    for i in range(1, nz):
+        t = t + jnp.where(z == i, acc[6 + i:7 + i], 0.0)
+    bup[...] = t
+    hbias = acc[6 + nz:9 + nz]
+    hbias = jnp.where(z // 2 == 0, hbias[:, :384], hbias[:, 384:])
+    odd = z % 2 == 1
+    two = jnp.where(odd, hbias[1:2], hbias[0:1])
+    lo1 = lax.broadcasted_iota(jnp.int32, (8, 128), 1) < 64
+    w8 = lambda a: jnp.broadcast_to(a, (8, 128))
+    left = lambda a, v: jnp.where(lo1, w8(a), sw(w8(v)))[0:1]
+    right = lambda a, v: jnp.where(lo1, sw(w8(a)), w8(v))[0:1]
+    lq, lv = hbias[2:3, :128], hbias[2:3, 256:]
+    bqv[pl.ds(0, 1), :] = left(two[:, :128], two[:, 256:])
+    bqv[pl.ds(1, 1), :] = right(two[:, :128], two[:, 256:])
+    bqv[pl.ds(2, 1), :] = jnp.where(odd, right(lq, lv), left(lq, lv))
+    for m in (ZO, Z01, Z2, Z3):
+        m.f.wait_recv()
+    lob = lax.broadcasted_iota(jnp.int32, (b, 128), 1) < 64
+    tile = lambda i: fa[:, pl.ds(128 * i, 128)].astype(F32)
+    t0, t1, t2, t3, t4, t5 = [tile(i) for i in range(6)]
+    g3[0, :, pl.ds(0, 128)] = jnp.where(lob, t0, sw(t1))
+    g3[0, :, pl.ds(128, 64)] = t2[:, :64]
+    g3[1, :, pl.ds(0, 128)] = jnp.where(lob, sw(t0), t1)
+    g3[1, :, pl.ds(128, 64)] = sw(t2)[:, :64]
+    g3[2, :, pl.ds(0, 128)] = t3
+    g3[2, :, pl.ds(128, 64)] = t4[:, :64]
+    gwo[pl.ds(0, 128), :] = t5.T
+    gwo[pl.ds(128, 64), :] = sw(t4).T[:64]
+    for m in g_s:
+        m.wait_recv()
+    g_l.wait()
+    for s in range(2):
+        gmem[s, pl.ds(0, 16), :] = grad4[s, 0, pl.ds(main, 16), :].astype(F32)
+        gmem[s, pl.ds(16, 2 * half - 16), :] = grad4[s, 1, pl.ds(main, 16), :].astype(F32)[:2 * half - 16]
     n.finish()
-    svo[...] = acc
-    for cp in g_s + [u_f, a_f]:
-        cp.wait_recv()
-    for cp in l_o:
-        cp.wait()
-
-def reduce(gu, gd, ga, gpart, g1, sv, nz, nd):
-    b, width = gu.shape[2:]
-    feats = 4 * b; hb = b // 2; rows = g1.shape[0]
+
+def backward(hu, hd, ga, mixed, xt, qt, kt, vt, w, o4, g1, lse, vgrad, bupgrad, idk, idq, half, nz, nd):
+    b, width = hu.shape[2:]
+    feats = 4 * b; hb = b // 2; rows = ga.shape[0]; own = g1.shape[0]; length = 2 * (own - 16)
     V = lambda *s, d=BF: pltpu.VMEM(s, d)
     vm = pl.BlockSpec(memory_space=pltpu.VMEM); an = pl.BlockSpec(memory_space=pl.ANY)
     S = jax.ShapeDtypeStruct
-    o = S((2, 2, rows, b), BF)
-    w = S((b, width), BF)
-    sm = lambda: V(*sv.shape, d=F32)
-    return pl.pallas_call(reduce_kernel,
-        out_shape=(o, w, w, S((b, width), F32), S(sv.shape, F32)),
-        in_specs=[an, an, an, vm, vm, vm], out_specs=(vm,) * 5,
-        scratch_shapes=[V(2, nz, b, width)] * 3 + [V(2, nz, hb, width)] * 2 + [V(nz, 2, hb, width), V(hb, width), V(2, hb, width),
-            V(nz, b, width), V(nz, b, width), V(nd, b, width), V(b, width), V(nz, hb, width), V(nz, hb, width),
-            V(4, rows, b), V(rows, feats), V(rows, feats), sm(), sm(), sm(), V(nz, *sv.shape, d=F32), sm(),
-            pltpu.SemaphoreType.DMA((96 + nd,)), pltpu.SemaphoreType.DMA((96 + nd,)), pltpu.SemaphoreType.DMA((16,))],
-        compiler_params=pltpu.CompilerParams(collective_id=2, has_side_effects=True, vmem_limit_bytes=63*2**20))(gu, gd, ga, gpart, g1, sv)
+    np_ = max(1, nd // 2) if nd > 2 else 1
+    pw = (hb, width) if nd > 2 else (16, 128)
+    t3 = V(3, rows, 128); f3 = lambda *s: V(*s, d=F32)
+    sm = f3(16, feats)
+    outs = (S((2, 2, own, b), BF), S((2, length + 2 * half, b), BF), S((2, 2 * half, b), F32), S((3, b, b), F32), S((b, b), F32), S((b, width), F32), S((b, width), F32), S((8, b), F32), S((1, feats), F32), S((3, 128), F32))
+    scratch = [V(2, nz, hb, width), V(nz, b, width), V(2, nz, hb, width), V(2, 2, hb, width), V(2, hb, width), V(2, hb, width), V(hb, width), V(b, width), V(np_, *pw),
+               V(nz, b, width), V(2, b, width), V(b, width), V(b, width), V(b, width), V(np_, b, width) if nd > 2 else V(1, 16, 128),
+               V(2, nz, b, width), V(2, nz, hb, width), V(nz, hb, width), V(nz, b, width), V(nz, hb, width), V(2, hb, width), V(hb, width), V(b, width), V(np_, *pw), V(2, 4, b, width),
+               V(rows, feats), t3, V(*xt.shape), t3, t3, t3, V(*w.shape), V(*o4.shape), f3(*g1.shape), V(3, feats, 384), V(feats, 384), V(feats, rows), t3, V(3, rows, 384),
+               f3(rows, 128), f3(rows, 128), f3(128, rows), V(128, rows), f3(2, 1, rows), V(4, own, b), V(own, feats), V(own, feats), f3(rows, b),
+               sm, sm, sm, sm, sm, sm, f3(np_, 16, feats), f3(nz, 16, feats),
+               pltpu.SemaphoreType.DMA((128 + 5 * nd,)), pltpu.SemaphoreType.DMA((128 + 5 * nd,)), pltpu.SemaphoreType.DMA((40,))]
+    return pl.pallas_call(backward_kernel, out_shape=outs, in_specs=[an] * 11 + [vm] * 5, out_specs=(vm,) * len(outs), scratch_shapes=scratch,
+        compiler_params=pltpu.CompilerParams(collective_id=2, has_side_effects=True, vmem_limit_bytes=67043328))(hu, hd, ga, mixed, xt, qt, kt, vt, w, o4, g1, lse, vgrad, bupgrad, idk, idq)
 
 def per_device(tokens, memory, block_ids, valid, teacher, w_qkv, bias_qv, w_out, bias_out, ln1_gain, ln1_bias, w_up, bias_up, w_down, bias_down, ln2_gain, ln2_bias):
     _, b, length = tokens.shape
@@ -1064,29 +1262,9 @@
     idk = jnp.broadcast_to(ids[:, None], (rows, 128))
     count = lax.dynamic_index_in_dim(valid, (d * nz + z) * 2 + y, 0)
     xt, qt, kt, vt, mixed, wown, ga, hu, hd, lse, g_one, vgrad, bupgrad, out4 = forward(count, tokens, mem, teacher, la, w_up, w_down, ls, idk, ids[None], nz)
-    gpart, bgrad, gown = attn_bwd(ga, mixed, xt, qt, kt, vt, lse.reshape(3, 2, 1, rows), idk, ids[None], wown)
-    bg = jnp.sum(bgrad, axis=1)[None]
-    bg = jnp.where((jnp.arange(2) == k)[:, None, None], bg, 0.0).reshape(3, feats)
-    sv = jnp.concatenate([jnp.sum(vgrad, axis=1), jnp.sum(bupgrad, axis=1), bg, jnp.zeros((3, feats), F32)])
-    grad4, fa, fu, fd, sv = reduce(hu, hd, gown, gpart, g_one, sv, nz, nd)
-    layer_out = jnp.concatenate([out4[:, 0, main:main + half], out4[:, 0, :main], out4[:, 1, :main], out4[:, 0, main + half:], out4[:, 1, main:main + 2 * half - 16]], axis=1)
+    grad4, lout, gmem, g3, gwo, fu, fd, fvec, bup, bqv = backward(hu, hd, ga, mixed, xt, qt, kt, vt, wown, out4, g_one, lse, vgrad, bupgrad, idk, ids[None], half, nz, nd)
     grad_tokens = grad4[:, :, :main].reshape(2, length, b).astype(F32)
-    grad_memory = jnp.concatenate([grad4[:, 0, main:], grad4[:, 1, main:main + 2 * half - 16]], axis=1).astype(F32)
-    fa = fa.astype(F32)
-    g0 = jnp.concatenate([fa[:, 0:64], fa[:, 128:192], fa[:, 256:320]], axis=1)
-    g1 = jnp.concatenate([fa[:, 64:128], fa[:, 192:256], fa[:, 320:384]], axis=1)
-    grad_w_qkv = jnp.stack([g0, g1, fa[:, 384:576]]).reshape(3, b * 192)
-    grad_w_out = jnp.transpose(jnp.concatenate([fa[:, 640:768], fa[:, 576:640]], axis=1))
-    hb = sv[10:13].reshape(2, 3, 384)
-    hb = lax.dynamic_index_in_dim(hb, z // 2, 0, keepdims=False)
-    zl = z % 2
-    two = lax.dynamic_index_in_dim(hb, zl, 0, keepdims=False)
-    last = hb[2]
-    pick = lambda r, e: jnp.concatenate([r[64 * e:64 * e + 64], r[256 + 64 * e:320 + 64 * e]])
-    grad_bias_qv = jnp.stack([pick(two, 0), pick(two, 1), jnp.where(zl == 0, pick(last, 0), pick(last, 1))])
-    fvec = lax.dynamic_slice_in_dim(sv[:6], c * b, b, 1)
-    grad_bias_up = lax.dynamic_index_in_dim(sv[6:10], z, 0, keepdims=False)
-    return (layer_out, grad_tokens, grad_memory, grad_w_qkv, grad_bias_qv, grad_w_out, fvec[5], fvec[3], fvec[4], fu.astype(F32), grad_bias_up, fd, fvec[2], fvec[0], fvec[1])
+    return (lout, grad_tokens, gmem, g3.reshape(3, b * b), bqv, gwo, fvec[5], fvec[3], fvec[4], fu, bup[0], fd, fvec[2], fvec[0], fvec[1])
 
 def solution(mesh):
     rows, feat = ("dp", "row"), "col"

time: 314 us -> 267 us (0.85)
  Pallas kernels: 273 us -> 240 us
  local copies, waits for them, and re-layouts: 29.1 us -> 21.8 us
  other arithmetic: 9.18 us -> 2.8 us
    pallas_call x2 -> x1, Pallas kernels: 140 us -> 107 us  [backward(): pl.pallas_call(backward_kernel, out_shape=outs, in_specs=[an] * 11 + [vm]...]
    squeeze x7 -> x0, local copies, waits for them, and re-layouts: 5.73 us -> none  [the longest x1 1.08 us: per_device(): out4[:, 1, :main]]
    unnamed x24 -> x28, local copies, waits for them, and re-layouts: 6.94 us -> 10.2 us
where the time goes in v3:
time: 267 us; the launch traced here: 266 us
  Pallas kernels  240 us (90%)
  local copies, waits for them, and re-layouts  21.8 us (8%)
  other arithmetic  2.8 us (1%)
    pallas_call x1, Pallas kernels, forward(): pl.pallas_call(forward_kernel, out_shape=[o for o, _ in outs], out_specs=...  133 us
    pallas_call x1, Pallas kernels, backward(): pl.pallas_call(backward_kernel, out_shape=outs, in_specs=[an] * 11 + [vm]...  107 us
    unnamed x28, local copies, waits for them, and re-layouts  10.2 us

profile of v3, /device:TPU:0, one launch (start us, length us, event | category | flops | bytes accessed | tf_op | source)
XLA Modules:
  0.0 266.1 jit_solution(18374211715363672908)
XLA Ops:
  0.7 1.3 reduce_sum.9
  2.7 1.2 dynamic_slice.8.valid_ref
  3.9 0.1 pad.18.clone
  4.0 0.7 copy.39
  4.7 0.7 constant_dynamic-slice_fusion
  5.4 0.1 concatenate.11
  5.5 0.7 reshape.52
  6.2 0.6 broadcast_in_dim.15.idq
  6.8 0.8 stack.27
  7.6 0.7 fusion.1.ls
  8.3 1.4 slice_reduce_fusion
  9.7 0.1 squeeze.52
  9.8 0.9 copy.32
  10.7 0.7 pad.12.mem
  11.3 1.0 copy.33
  12.4 1.3 reshape.51
  13.7 0.1 slice_bitcast_fusion
  13.8 0.9 concatenate.9.la
  14.6 1.0 broadcast_in_dim.14.idk
  15.6 132.7 %shard_map.280 = (bf16[768,1152]{1,0:T(8,128)(2,1)}, bf16[3,1056,128]{2,1,0:T(8,128)(2,1)}, bf16[3,1056,128]{2,1,0:T(8,128)(2,1)}, bf16[3,1056,128]{2,1,0:T(8,12...) custom-call(s32[1]{0:T(128)} %dynamic_slice.8.valid_ref, ...), custom_call_target="tpu_custom_call" | custom-call | tf_op jit(solution)/shard_map/pallas_call | solution.py:851
  148.3 107.4 %shard_map.281 = (bf16[2,2,528,192]{3,2,1,0:T(8,128)(2,1)}, bf16[2,1044,192]{2,1,0:T(8,128)(2,1)}, f32[2,20,192]{2,1,0:T(8,128)}, f32[3,192,192]{2,1,0:T(8,128)}...) custom-call(bf16[2,4,192,768]{3,2,1,0:T(8,128)(2,1)} %get-tuple-elem, ...), custom_call_target="tpu_custom_call" | custom-call | tf_op jit(solution)/shard_map/pallas_call | solution.py:1241
  255.7 0.0 copy-start.7
  255.7 0.0 copy-start.6
  255.7 0.0 copy-start.5
  255.7 0.0 copy-start.3
  255.7 0.0 copy-start
  255.8 2.4 copy.34
  258.2 0.0 copy-done.7
  258.2 0.6 reduce.2
  258.8 0.0 copy-done.6
  258.8 0.6 fusion.2
  259.3 0.0 copy-done.5
  259.3 0.6 copy.36
  260.0 0.0 copy-done.3
  260.0 1.2 reshape.55
  261.2 0.0 copy-done
  261.2 0.1 slice.58
  261.3 0.2 bitcast_convert_fusion
  261.5 0.0 copy-start.8
  261.5 0.0 copy-start.4
  261.5 0.0 copy-start.2
  261.5 0.0 copy-start.1
  261.6 1.7 copy.35
  263.2 0.0 copy-done.8
  263.2 0.6 copy.44
  263.8 0.0 copy-done.4
  263.8 0.7 copy.45
  264.5 0.0 copy-done.2
  264.5 0.8 copy.46
  265.3 0.0 copy-done.1
  265.3 0.8 copy.47
  (10 shorter events, 0.1 us)
Async XLA Ops:
  255.7 2.4 copy-start.7
  255.7 3.0 %copy-start.6 = (f32[8,192]{1,0:T(8,128)S(1)}, f32[8,192]{1,0:T(8,128)}, u32[]{:S(2)}) copy-start(f32[8,192]{1,0:T(8,128)} %get-tuple-element.59) | copy-start | bytes 18436
  255.7 3.6 %copy-start.5 = (f32[2,20,192]{2,1,0:T(8,128)S(1)}, f32[2,20,192]{2,1,0:T(8,128)}, u32[]{:S(2)}) copy-start(f32[2,20,192]{2,1,0:T(8,128)} %get-tuple-element.65) | copy-start | bytes 92164
  255.7 4.3 %copy-start.3 = (f32[3,192,192]{2,1,0:T(8,128)S(1)}, f32[3,192,192]{2,1,0:T(8,128)}, u32[]{:S(2)}) copy-start(f32[3,192,192]{2,1,0:T(8,128)} %get-tuple-element.56) | copy-start | bytes 1327108
  255.7 5.5 %copy-start = (bf16[2,2,528,192]{3,2,1,0:T(8,128)(2,1)S(1)}, bf16[2,2,528,192]{3,2,1,0:T(8,128)(2,1)}, u32[]{:S(2)}) copy-start(bf16[2,2,528,192]{3,2,1,0:T(8,128)(2,1)} %get-tuple-element.54) | copy-start | bytes 2433028
  261.5 1.7 copy-start.8
  261.5 2.3 copy-start.4
  261.5 3.0 %copy-start.2 = (f32[192,768]{1,0:T(8,128)S(1)}, f32[192,768]{1,0:T(8,128)}, u32[]{:S(2)}) copy-start(f32[192,768]{1,0:T(8,128)} %get-tuple-element.114) | copy-start | bytes 1769476
  261.5 3.8 %copy-start.1 = (f32[192,768]{1,0:T(8,128)S(1)}, f32[192,768]{1,0:T(8,128)}, u32[]{:S(2)}) copy-start(f32[192,768]{1,0:T(8,128)} %get-tuple-element.116) | copy-start | bytes 1769476

commit v4 on v3

--- a/solution.py
+++ b/solution.py
@@ -445,11 +445,50 @@
         dst[:, pl.ds(384 * h + 128, 128)] = jnp.where(lo, a[1], sw(b[0]))
         dst[:, pl.ds(384 * h + 256, 128)] = jnp.where(lo, sw(b[0]), sw(b[1]))
 
-def forward_kernel(valid_ref, tok, mem, tch, la, lu, ld, ls, idk, idq,
+def row_ids(ids, y, half, idk, idq):
+    length = ids.shape[1]
+    idq[:, pl.ds(0, length)] = ids[pl.ds(y, 1), :].astype(F32)
+    i = lax.broadcasted_iota(jnp.int32, (1, 128), 1)
+    idq[:, pl.ds(length, 128)] = jnp.where(i < half, -1.0, jnp.where(i < 2 * half, 1.0 * length, 2.0 * length))
+    for j in range(length // 128 + 1):
+        idk[pl.ds(128 * j, 128), :] = jnp.broadcast_to(idq[:, pl.ds(128 * j, 128)], (128, 128)).T
+
+def pack_inputs(w3, wo, la, vecs, bias_up, bias_qv, scale, ls, memory, mtmp, mem):
+    b = w3.shape[1]
+    f = lambda r: r.astype(F32)
+    lo = lax.broadcasted_iota(jnp.int32, (b, 128), 1) < 64
+    t0, t1 = f(w3[0, :, pl.ds(0, 128)]), f(w3[1, :, pl.ds(0, 128)])
+    la[:, pl.ds(0, 128)] = jnp.where(lo, t0, pltpu.roll(t1, 64, 1)).astype(BF)
+    la[:, pl.ds(128, 128)] = jnp.where(lo, pltpu.roll(t0, 64, 1), t1).astype(BF)
+    v = [f(w3[j, :, pl.ds(128, 64)]) for j in range(3)]
+    la[:, pl.ds(256, 128)] = jnp.concatenate([v[0], v[1]], axis=1).astype(BF)
+    la[:, pl.ds(384, 128)] = w3[2, :, pl.ds(0, 128)]
+    wot = f(wo[...]).T
+    la[:, pl.ds(512, 128)] = jnp.concatenate([v[2], wot[:, 128:]], axis=1).astype(BF)
+    la[:, pl.ds(640, 128)] = wot[:, :128].astype(BF)
+    ls[...] = jnp.zeros_like(ls)
+    for j, r in enumerate(vecs):
+        ls[pl.ds(j, 1), pl.ds(0, b)] = r[...]
+    ls[pl.ds(6, 1), :] = scale
+    for j in range(3):
+        ls[pl.ds(8 + j, 1), :] = bias_up[:, pl.ds(256 * j, 256)]
+    ls[pl.ds(11, 1), pl.ds(0, 128)] = bias_qv[0:1, :]
+    ls[pl.ds(11, 1), pl.ds(128, 128)] = bias_qv[1:2, :]
+    ls[pl.ds(12, 1), pl.ds(0, 128)] = bias_qv[2:3, :]
+    mtmp[...] = jnp.zeros_like(mtmp)
+    for s in range(2):
+        mtmp[pl.ds(0, memory.shape[1]), :] = f(memory[s])
+        mem[s] = mtmp[...].T.astype(BF)
+
+def forward_kernel(valid_ref, tok, memory, tch, w3, wo, lu, ld, v0, v1, v2, v3, v4, v5, bias_up, bias_qv, ids,
                    xt_o, q_o, k_o, v_o, mixed_o, wa_o, ga_o, hu_o, hd_o, lse, g_one, vgrad, bupgrad, out4,
                    xt, x, wa, wu, wd, sm, tt, tr, wp, qt, kt, vt, vtt, ot, mixed, mrows, bias, vec, wt,
-                   h1, h2, rs1, low, lowt, br, brt, hid, dgl, gdz, guz, hu, hd, ru, rd, ga, o4, ss, rs, lsem, zsem, zrem):
+                   h1, h2, rs1, low, lowt, br, brt, hid, dgl, gdz, guz, hu, hd, ru, rd, ga, o4, la, ls, mem, mtmp, idk, idq, ss, rs, lsem, zsem, zrem):
     n = Net(ss, rs, lsem)
+    total = lax.fori_loop(0, valid_ref.shape[0], lambda i, t: t + valid_ref[i], jnp.int32(0))
+    count = valid_ref[(n.d * n.nz + n.z) * 2 + n.y]
+    scale_row = (valid_ref.shape[0] * tok.shape[2]) / jnp.full((1, 256), total, jnp.int32).astype(F32)
+    pack_inputs(w3, wo, la, (v0, v1, v2, v3, v4, v5), bias_up, bias_qv, scale_row, ls, memory, mtmp, mem)
     n.barrier(n.zp[1:] + [n.yp, n.ykp, n.kp, n.xp])
     nz, y, k, c, z, oc = n.nz, n.y, n.k, n.c, n.z, n.oc
     b = la.shape[0]; hb = b // 2
@@ -464,59 +503,71 @@
     tail = pl.ds(length, 128); body = pl.ds(0, length)
     fz = n.from_row
     R = range(1, nz)
+    e1 = z + 1 - 2 * lax.rem(z, 2)
+    e2 = lax.rem(z + 2, nz)
+    e3 = lax.rem(e1 + 2, nz)
+    dev1, dev2 = (n.d, e1, c), (n.d, e2, c)
+    order = [z, e2, e1, e3]
+    s_blk = lambda zz, cc: (lambda: sm.at[zz, cc])
+    fwd = lambda u, dev: n.move(u, u, dev)
     local = [n.local(lambda: tok.at[y], lambda: xt.at[row(c), body]), n.local(lambda: mem.at[y], lambda: xt.at[row(c), tail])]
-    s_blk = lambda zz, cc: (lambda: sm.at[zz, cc])
-    a_z = [n.send(part(la), hlf(wa, z, c, mine), n.zp[i]) for i in R]
+    au = lambda zz, cc: hlf(wa, zz, cc, mine)
+    a2 = n.send(part(la), au(z, c), dev2)
+    a1 = n.send(part(la), au(z, c), dev1)
+    a_y = [n.send(part(la), au(z, c), n.yp)]
+    a_k = [n.send(all_of(la), blk(wa, z, c), n.kp)]
     s_z = [n.send(all_of(ls), s_blk(z, c), n.zp[i]) for i in R]
-    a_y = [n.send(part(la), hlf(wa, z, c, mine), n.yp)]
-    t_y = [n.send(lambda: tok.at[1 - y], lambda: xt.at[row(c), body], n.yp), n.send(lambda: mem.at[1 - y], lambda: xt.at[row(c), tail], n.yp)]
     s_y = [n.send(all_of(ls), s_blk(z, c), n.yp)]
-    u_y = n.send(part(lu), hlf(wu, z, c, mine), n.yp)
     s_k = [n.send(all_of(ls), s_blk(z, c), n.kp)]
     t_k = [n.send(lambda: tok.at[y], lambda: xt.at[row(c), body], n.kp), n.send(lambda: mem.at[y], lambda: xt.at[row(c), tail], n.kp)]
-    a_k = [n.send(all_of(la), blk(wa, z, c), n.kp)]
     for w, l in ((wa, la), (wu, lu), (wd, ld)):
         local.append(n.local(all_of(l), blk(w, z, c)))
     local.append(n.local(all_of(ls), s_blk(z, c)))
-    fwd = lambda u, dev: n.move(u, u, dev)
-    a_x = []
+    a_x, a_xu = [], []
+    def pass_on(u, lists):
+        for lst, dev in lists:
+            lst.append(fwd(u, dev)); lst[-1].start()
+    def a_own(zz):
+        a_xu.append((zz, c))
+        pass_on(au(zz, c), ((a_x, n.xp), (a_y, n.yp), (a_k, n.kp)))
+    def a_far(i):
+        a_y[i].wait_recv()
+        a_xu.append((order[i], oc))
+        pass_on(au(order[i], oc), ((a_x, n.xp), (a_k, n.kp)))
+    def a_home(i):
+        a_x[i].wait_recv()
+        pass_on(hlf(wa, *a_xu[i], theirs), ((a_k, n.kp),))
+    a_far(0)
+    a2.wait_recv()
+    a3 = fwd(au(e2, c), dev1); a3.start()
+    a_own(e2)
+    t_y = [n.send(lambda: tok.at[1 - y], lambda: xt.at[row(c), body], n.yp), n.send(lambda: mem.at[1 - y], lambda: xt.at[row(c), tail], n.yp)]
+    a1.wait_recv()
+    a_own(e1)
+    a_far(1)
     for i in R:
-        a_z[i - 1].wait_recv()
-        u = hlf(wa, fz(i), c, mine)
-        for lst, dev in ((a_y, n.yp), (a_x, n.xp), (a_k, n.kp)):
-            lst.append(fwd(u, dev)); lst[-1].start()
         s_z[i - 1].wait_recv()
-        u = s_blk(fz(i), c)
-        for lst, dev in ((s_y, n.yp), (s_k, n.kp)):
-            lst.append(fwd(u, dev)); lst[-1].start()
-    u_z = [n.send(part(lu), hlf(wu, z, c, mine), n.zp[i]) for i in R]
-    u_k = [n.send(all_of(lu), blk(wu, z, c), n.kp)]
-    u_y.wait_recv()
-    uo = hlf(wu, z, oc, mine)
-    u_z2 = [fwd(uo, n.zp[i]) for i in R]
-    for m in u_z2:
-        m.start()
-    u_x = [fwd(uo, n.xp)]
-    u_k.append(fwd(uo, n.kp)); u_k[-1].start()
-    for m, w_ in zip(t_y, (body, tail)):
-        m.wait_recv()
-        t_k.append(fwd((lambda w_=w_: xt.at[row(oc), w_]), n.kp)); t_k[-1].start()
-    for i in range(nz):
-        a_y[i].wait_recv()
-        u = hlf(wa, fz(i), oc, mine)
-        for lst, dev in ((a_x, n.xp), (a_k, n.kp)):
-            lst.append(fwd(u, dev)); lst[-1].start()
-        s_y[i].wait_recv()
-        u = s_blk(fz(i), oc)
-        s_k.append(fwd(u, n.kp)); s_k[-1].start()
-    u_x[0].start()
-    d_z = [n.send(all_of(ld), blk(wd, z, c), n.zp[i]) for i in R]
-    d_y = [n.send(all_of(ld), blk(wd, z, c), n.yp)]
+        pass_on(s_blk(fz(i), c), ((s_y, n.yp), (s_k, n.kp)))
+    a3.wait_recv()
+    a_own(e3)
+    uu = lambda zz, cc: blk(wu, zz, cc)
+    du = lambda zz, cc: hlf(wd, zz, cc, mine)
+    u2 = n.send(all_of(lu), uu(z, c), dev2)
+    u1 = n.send(all_of(lu), uu(z, c), dev1)
+    d_y = n.send(part(ld), du(z, c), n.yp)
+    u_y = [n.send(all_of(lu), uu(z, c), n.yp)]
+    u_k = {0: n.send(all_of(lu), uu(z, c), n.kp)}
     d_k = [n.send(all_of(ld), blk(wd, z, c), n.kp)]
     tsl = lambda s, kk: (lambda: tch.at[s, :, pl.ds(pl.multiple_of(kk * main, 128), main)])
     th = lambda: tt.at[row(c)]
     h_y = [n.send(tsl(y, 1 - k), th, n.kp)]
     local.append(n.local(tsl(y, k), th))
+    row_ids(ids, y, memory.shape[1] // 2, idk, idq)
+    for m, w_ in zip(t_y, (body, tail)):
+        m.wait_recv()
+        t_k.append(fwd((lambda w_=w_: xt.at[row(oc), w_]), n.kp)); t_k[-1].start()
+    for i in range(3):
+        a_home(i)
     local[0].wait(); local[1].wait()
     for m in t_k:
         m.wait_recv()
@@ -527,38 +578,74 @@
     lax.fori_loop(0, length // 128, turn, 0)
     x[pl.ds(length, rows - length), :] = xt[:, tail].T[: rows - length, :]
     o_x = n.local(all_of(xt), all_of(xt_o))
-    order = [(i, c) for i in R] + [(i, oc) for i in range(nz)]
-    for m, (i, cc) in zip(a_x, order):
-        m.wait_recv()
-        a_k.append(fwd(hlf(wa, fz(i), cc, theirs), n.kp)); a_k[-1].start()
-    h_y += [n.send(tsl(1 - y, k), th, n.yp), n.send(tsl(1 - y, 1 - k), th, n.ykp)]
-    events = []
-    def relay(wait, u, pairs):
-        ms = []
-        for lst, dev in pairs:
-            m = fwd(u, dev)
-            lst.append(m)
-            ms.append(m)
+    for i in range(nz):
+        s_y[i].wait_recv()
+        pass_on(s_blk(fz(i), oc), ((s_k, n.kp),))
+    a_far(2)
+    a_far(3)
+    for i in range(3, 5):
+        a_home(i)
+    u2.wait_recv()
+    u3 = fwd(uu(e2, c), dev1); u3.start()
+    d2 = n.send(part(ld), du(z, c), dev2)
+    d1 = n.send(part(ld), du(z, c), dev1)
+    def u_put(i, cc, y_too=True):
+        m = fwd(uu(order[i], cc), n.kp)
+        u_k[(i, cc is oc)] = m
+        if y_too:
+            u_y.append(fwd(uu(order[i], cc), n.yp))
+            u_y[-1].start()
+        m.start()
+    u_put(1, c)
+    d_y.wait_recv()
+    d_x, d_xu = [], []
+    def d_put(zz, cc):
+        d_xu.append((zz, cc))
+        d_x.append(fwd(du(zz, cc), n.xp)); d_k.append(fwd(du(zz, cc), n.kp))
+        return [d_x[-1], d_k[-1]]
+    for m in d_put(z, oc):
+        m.start()
+    for i in range(5, 7):
+        a_home(i)
+    def step(wait, moves):
         def run():
-            wait()
-            for m in ms:
+            wait.wait_recv()
+            for m in moves:
                 m.start()
-        events.append(run)
-    for i in R:
-        relay(u_z[i - 1].wait_recv, hlf(wu, fz(i), c, mine), ((u_x, n.xp), (u_k, n.kp)))
-    for i in R:
-        relay(u_z2[i - 1].wait_recv, hlf(wu, fz(i), oc, mine), ((u_x, n.xp), (u_k, n.kp)))
-    u_order = [(0, oc)] + [(i, c) for i in R] + [(i, oc) for i in R]
-    u_units = list(zip(u_x, u_order))
-    for i in R:
-        relay(d_z[i - 1].wait_recv, blk(wd, fz(i), c), ((d_y, n.yp), (d_k, n.kp)))
-    for m, (i, cc) in u_units:
-        relay(m.wait_recv, hlf(wu, fz(i), cc, theirs), ((u_k, n.kp),))
-    u_events, d_events = events, []
-    events = []
-    for i in range(nz):
-        relay(d_y[i].wait_recv, blk(wd, fz(i), oc), ((d_k, n.kp),))
-    d_events = events
+        return run
+    def u_step(wait, i):
+        u_y.append(fwd(uu(order[i], c), n.yp))
+        u_w.append(fwd(uu(order[i], c), n.kp))
+        return step(wait, [u_y[-1], u_w[-1]])
+    u_w = list(u_k.values())
+    def u_far(i):
+        u_w.append(fwd(uu(order[i], oc), n.kp))
+        return step(u_y[i], [u_w[-1]])
+    d3, d2o, d1o, d3o = fwd(du(e2, c), dev1), fwd(du(z, oc), dev2), fwd(du(z, oc), dev1), fwd(du(e2, oc), dev1)
+    E_u1 = u_step(u1, 2)
+    E_u3 = u_step(u3, 3)
+    h_m = [n.move(tsl(1 - y, k), th, n.yp), n.move(tsl(1 - y, 1 - k), th, n.ykp)]
+    def E_h():
+        for m in h_m:
+            m.start()
+    h_y += h_m
+    E_uy = [u_far(i) for i in range(4)]
+    E_d2 = step(d2, [d3] + d_put(e2, c))
+    def E_do():
+        d2o.start(); d1o.start()
+    E_d1 = step(d1, d_put(e1, c))
+    E_d3 = step(d3, d_put(e3, c))
+    E_d2o = step(d2o, [d3o] + d_put(e2, oc))
+    E_d1o = step(d1o, d_put(e1, oc))
+    E_d3o = step(d3o, d_put(e3, oc))
+    E_dx = []
+    for m, (zz, cc) in zip(d_x, d_xu):
+        d_k.append(fwd(hlf(wd, zz, cc, theirs), n.kp))
+        E_dx.append(step(m, [d_k[-1]]))
+    proj_events = {1: [E_u1], 8: [E_u3, E_h]}
+    head_events = {2: [E_do, E_dx[0]], 4: [E_uy[0]], 6: [E_d2], 8: [E_d1], 10: [E_d3, E_uy[1]], 12: [E_dx[1], E_dx[2]], 14: [E_d2o, E_uy[2]], 16: [E_d1o, E_dx[3]]}
+    out_events = [E_d3o]
+    gate_events = {0: [], 3: [], 6: [E_dx[4], E_dx[5]], 9: [E_dx[6]]}
     for m in s_k:
         m.wait_recv()
     for m in local[2:6]:
@@ -568,11 +655,11 @@
     sw = lambda a: pltpu.roll(a, 64, 1)
     bias[...] = jnp.zeros_like(bias)
     hv = [[sm[2 * k + j, 0, 11:12, pl.ds(0, 128)], sm[2 * k + j, 0, 11:12, pl.ds(128, 128)], sm[2 * k + j, 0, 12:13, pl.ds(0, 128)]] for j in range(2)]
-    for p, (e0, e1) in enumerate(((hv[0][0], hv[0][1]), (hv[1][0], hv[1][1]), (hv[0][2], hv[1][2]))):
+    for p, (ea, eb) in enumerate(((hv[0][0], hv[0][1]), (hv[1][0], hv[1][1]), (hv[0][2], hv[1][2]))):
         w8 = lambda a: jnp.broadcast_to(a, (8, 128))
         lo8 = lax.broadcasted_iota(jnp.int32, (8, 128), 1) < 64
-        bias[p, :, pl.ds(0, 128)] = jnp.where(lo8, w8(e0), sw(w8(e1)))
-        bias[p, :, pl.ds(256, 128)] = jnp.where(lo8, sw(w8(e0)), w8(e1))
+        bias[p, :, pl.ds(0, 128)] = jnp.where(lo8, w8(ea), sw(w8(eb)))
+        bias[p, :, pl.ds(256, 128)] = jnp.where(lo8, sw(w8(ea)), w8(eb))
     for m in a_k:
         m.wait_recv()
     own = pl.ds(2 * k, 2)
@@ -580,7 +667,6 @@
     w = wa.at[own]
     assemble_pairs(w, wp, feats)
     rc = rows // 3
-    ev = spread_events(u_events[:6], 9)
 
     def project(i, _):
         p = i // 3
@@ -589,7 +675,7 @@
         qt[p, r, :] = (v[:, :128].astype(BF).astype(F32) * 0.125).astype(BF)
         kt[p, r, :] = v[:, 128:256].astype(BF)
         vt[p, r, :] = v[:, 256:].astype(BF)
-        at(i, ev)
+        at(i, proj_events)
         return 0
     lax.fori_loop(0, 9, project, 0)
     o_q = [n.local(all_of(a), all_of(o)) for a, o in ((qt, q_o), (kt, k_o), (vt, v_o))]
@@ -597,7 +683,7 @@
             n.move((lambda p=p: mixed.at[p, pl.ds(pl.multiple_of(length + (1 - k) * 16, 16), 16)]), (lambda p=p: mrows.at[k * 3 + p, pl.ds(main, 16)]), n.kp)) for p in range(3)]
     m_l = [(n.copy((lambda p=p: mixed.at[p, pl.ds(pl.multiple_of(k * main, 16), main)]), (lambda p=p: mrows.at[k * 3 + p, pl.ds(0, main)])),
             n.copy((lambda p=p: mixed.at[p, pl.ds(pl.multiple_of(length + k * 16, 16), 16)]), (lambda p=p: mrows.at[k * 3 + p, pl.ds(main, 16)]))) for p in range(3)]
-    ev = spread_events(u_events[6:], 6)
+    cuts = {1: 0, 3: 1, 4: 2}
 
     def head(i, _):
         p = i // 2
@@ -608,7 +694,7 @@
         def _():
             vtt[...] = vt[p].T
         lanes = (lax.broadcasted_iota(jnp.int32, (1, 128), 1) // 64) == e
-        for q0, qn, spans in tiles(rows, length):
+        for t_, (q0, qn, spans) in enumerate(tiles(rows, length)):
             q = qt[p, pl.ds(q0, qn), :]
             qm = jnp.where(lanes, q, jnp.zeros_like(q))
             sc = scores_of(kt, qm, idk, idq[0:1, pl.ds(q0, qn)], p, spans)
@@ -624,11 +710,12 @@
                 acc = o if acc is None else acc + o
             ot[he, pl.ds(q0, qn)] = acc / tot
             lse[i, :, pl.ds(q0, qn)] = m + jnp.log(tot)
+            if t_ in cuts:
+                at(3 * i + cuts[t_], head_events)
 
         @pl.when(e == 1)
         def _():
             mixed[p] = ot[...].T.astype(BF)
-        at(i, ev)
         at(i, {2 * p + 1: [m.start for m in m_k[p] + m_l[p]] for p in range(3)})
         return 0
     lax.fori_loop(0, 6, head, 0)
@@ -648,8 +735,6 @@
             m.wait()
     nb = feats // 256
     CHS = own_rows // CH
-    for e in d_events[:0]:
-        e()
 
     def own_slice(i, num):
         start = jnp.where(i < main, k * main + i, length + k * 16)
@@ -661,6 +746,8 @@
         for j in range(1, 6):
             acc = acc + nt(mrows[j], wt[f, pl.ds(128 * j, 128)])
         h1[:, f] = acc + vec[0:1, f]
+    for e in out_events:
+        e()
     inv = 1.0 / feats
     vgrad[...] = jnp.zeros_like(vgrad)
     bupgrad[...] = jnp.zeros_like(bupgrad)
@@ -678,11 +765,12 @@
         return 0
     lax.fori_loop(0, own_rows // 16, norm1, 0, unroll=3)
     lowt[...] = low[...].T
-    for m in u_k:
+    E_uy[3]()
+    for m in u_w:
         m.wait_recv()
-    ev = spread_events(d_events, 12)
 
     def gate(i, _):
+        at(i, gate_events)
         zz = i // nb
         j = i % nb
         f = pl.ds(pl.multiple_of(j * 256, 256), 256)
@@ -690,7 +778,6 @@
         a, g = gelu_pair(v)
         hid[zz, :, f] = a.astype(BF)
         dgl[zz, :, f] = g.astype(BF)
-        at(i, ev)
         return 0
     lax.fori_loop(0, nz * nb, gate, 0)
     for m in h_y:
@@ -714,6 +801,7 @@
         return 0
     lax.fori_loop(0, nb, down, 0)
     scale = vec[6:7, 0:1]
+    o4[:, :, pl.ds(b, o4.shape[2] - b)] = jnp.zeros((4, own_rows, o4.shape[2] - b), BF)
 
     def norm2(i, _):
         r = pl.ds(pl.multiple_of(i * CH, 16), CH)
@@ -724,10 +812,10 @@
         xhat = (h - m) * rstd
         o = xhat * vec[4:5, :] + vec[5:6, :]
         for cc in range(4):
-            o4[cc, r, :] = o[:, cc * b:(cc + 1) * b].astype(BF)
+            o4[cc, r, pl.ds(0, b)] = o[:, cc * b:(cc + 1) * b].astype(BF)
         place = lax.broadcasted_iota(jnp.int32, (CH, 1), 0) + i * CH
-        place = jnp.where(place < main, place + k * main, valid_ref[0])
-        go = jnp.where(place < valid_ref[0], scale * (o - tr[r, :].astype(F32)), 0.0)
+        place = jnp.where(place < main, place + k * main, count)
+        go = jnp.where(place < count, scale * (o - tr[r, :].astype(F32)), 0.0)
         a = go * vec[4:5, :]
         m1 = jnp.sum(a, axis=1, keepdims=True) * inv
         m2 = jnp.sum(a * xhat, axis=1, keepdims=True) * inv
@@ -832,25 +920,25 @@
 def add_to(dst, src):
     dst[...] = (dst[...].astype(F32) + src[...].astype(F32)).astype(BF)
 
-def forward(valid, tok, mem, tch, la, lu, ld, ls, idk, idq, nz):
+def forward(valid, tok, memory, tch, w3, wo, lu, ld, vecs, bias_up, bias_qv, ids, nz):
     b, width = lu.shape
-    feats = 4 * b; length = tok.shape[2]; rows = idk.shape[0]; main = length // 2; own = main + 16
+    feats = 4 * b; length = tok.shape[2]; rows = length + 32; main = length // 2; own = main + 16
     V = lambda *s, d=BF: pltpu.VMEM(s, d)
     vm = pl.BlockSpec(memory_space=pltpu.VMEM); sm = pl.BlockSpec(memory_space=pltpu.SMEM); an = pl.BlockSpec(memory_space=pl.ANY)
     S = jax.ShapeDtypeStruct
     t3 = S((3, rows, 128), BF); h = S((2, nz, b, width), BF)
     outs = [(S((feats, length + 128), BF), an), (t3, an), (t3, an), (t3, an), (t3, an), (S((2, feats, width), BF), an), (S((rows, feats), BF), an), (h, an), (h, an),
-            (S((6, 1, rows), F32), vm), (S((own, feats), F32), vm), (S((6, 8, feats), F32), vm), (S((nz, 8, width), F32), vm), (S((2, 2, own, b), BF), vm)]
+            (S((6, 1, rows), F32), vm), (S((own, feats), F32), vm), (S((6, 8, feats), F32), vm), (S((nz, 8, width), F32), vm), (S((2, 2, own, 256), BF), vm)]
     w = V(nz, feats, width)
-    scratch = [V(feats, length + 128), V(rows, feats), w, w, w, V(nz, 4, *ls.shape, d=F32), V(feats, main), V(own, feats), V(3, feats, 384),
+    scratch = [V(feats, length + 128), V(rows, feats), w, w, w, V(nz, 4, 16, 256, d=F32), V(feats, main), V(own, feats), V(3, feats, 384),
                V(3, rows, 128), V(3, rows, 128), V(3, rows, 128), V(128, rows), V(128, rows, d=F32), V(3, rows, 128), V(6, own, 128), V(3, 8, 384, d=F32), V(8, feats, d=F32), V(feats, feats),
                V(own, feats, d=F32), V(own, feats, d=F32), V(own, 128, d=F32), V(own, feats), V(feats, own), V(own, feats), V(feats, own),
-               V(nz, own, width), V(nz, own, width), V(2, 4, b, width), V(2, 4, b, width)] + [V(2, nz, b, width)] * 4 + [V(rows, feats), V(4, own, b),
+               V(nz, own, width), V(nz, own, width), V(2, 4, b, width), V(2, 4, b, width)] + [V(2, nz, b, width)] * 4 + [V(rows, feats), V(4, own, 256), V(b, width), V(16, 256, d=F32), V(2, b, 128), V(128, b, d=F32), V(length + 128, 128, d=F32), V(1, length + 128, d=F32),
                pltpu.SemaphoreType.DMA((136,)), pltpu.SemaphoreType.DMA((136,)), pltpu.SemaphoreType.DMA((32,)),
                pltpu.SemaphoreType.DMA((2, 2, nz)), pltpu.SemaphoreType.DMA((2, 2, nz))]
     return pl.pallas_call(forward_kernel, out_shape=[o for o, _ in outs], out_specs=[s for _, s in outs],
-        in_specs=[sm, an, an, an, an, an, an, an, vm, vm], scratch_shapes=scratch,
-        compiler_params=pltpu.CompilerParams(collective_id=1, has_side_effects=True, vmem_limit_bytes=67043328))(valid, tok, mem, tch, la, lu, ld, ls, idk, idq)
+        in_specs=[sm, an, vm, an, vm, vm, an, an] + [vm] * 9, scratch_shapes=scratch,
+        compiler_params=pltpu.CompilerParams(collective_id=1, has_side_effects=True, vmem_limit_bytes=67043328))(valid, tok, memory, tch, w3, wo, lu, ld, *vecs, bias_up, bias_qv, ids)
 def total_of(refs):
     acc = refs[0][...].astype(F32)
     for r in refs[1:]:
@@ -908,16 +996,17 @@
     def end(self):
         self.b.wait_recv(); self.c.wait_recv()
 
-def backward_kernel(hu_h, hd_h, ga_h, mixed_h, xt_h, q_h, k_h, v_h, w_h, o4_h, g1_h, lse, vgrad, bupgrad, idk, idq,
+def backward_kernel(hu_h, hd_h, ga_h, mixed_h, xt_h, q_h, k_h, v_h, w_h, o4_h, g1_h, lse, vgrad, bupgrad, ids,
                     grad4, lout, gmem, g3, gwo, fu, fd, fvec, bup, bqv,
                     hu, hd, ux, uz1, uz2, ut, uy, fub, pu, dy, dz1, dz2, df, dx, pd,
                     ha, ax, ay, ayf, axf, az1, az2, fa, pa, gown,
                     ga, mixed, xt, qt, kt, vt, w, o4, g1, wp, wt, gat, gm, gp, dv, dk, dqt, ktt, dd, g4, gs, gr, lo32,
-                    sv, svk, svt, svy, svo, svx, ps, svz, ss, rs, lsem):
+                    sv, svk, svt, svy, svo, svx, ps, svz, idk, idq, ss, rs, lsem):
     n = Net(ss, rs, lsem)
     nz, y, k, c, z, x, d, nd = n.nz, n.y, n.k, n.c, n.z, n.x, n.d, n.nd
     b = fu.shape[0]; hb = b // 2
     rows, feats = ga.shape
+    fb = pl.ds(0, b)
     own_rows = g1.shape[0]; main = own_rows - 16; length = 2 * main
     mine = pl.ds(pl.multiple_of(x * hb, 16), hb)
     theirs = pl.ds(pl.multiple_of((1 - x) * hb, 16), hb)
@@ -933,7 +1022,7 @@
     e2 = lax.rem(z + 2, nz)
     e3 = lax.rem(e1 + 2, nz)
     e = (e1, e2, e3)
-    order = [e3, e1, e2, z]
+    order = [e3, e2, e1, z]
     dev1, dev2 = (d, e1, c), (d, e2, c)
     d_y = [n.send((lambda q=q: hd_h.at[1 - y, q]), (lambda q=q: dy.at[q]), n.yp) for q in order]
     u_x = [n.send((lambda q=q: hu_h.at[:, q, theirs]), (lambda q=q: ux.at[:, q]), n.xp) for q in order]
@@ -964,8 +1053,8 @@
             if j == 0:
                 l_d.wait()
             add_to(hd.at[order[j]], dy.at[order[j]])
-            if j == 1:
-                dz.start()
+            if j == 0:
+                dz.a.start()
         return run
     def ev_ux(j):
         def run():
@@ -973,8 +1062,8 @@
             if j == 0:
                 l_u.wait()
             add2(hu.at[:, order[j]], ux.at[:, order[j]])
-            if j == 1:
-                uz.start()
+            if j == 0:
+                uz.a.start()
         return run
     def ev_df():
         dz.end()
@@ -1007,6 +1096,7 @@
             fa[mine, C] = pairs_sum(total_of([ha.at[y, z, mine, C], az1.at[0, :, C], az2.at[:, C]]), pa, lambda s, i: s.at[i, :, C]).astype(BF)
             self.f.start()
     ZO, Z01, Z2, Z3 = Cols(640, 128), Cols(0, 384), Cols(384, 128), Cols(512, 128)
+    row_ids(ids, y, gmem.shape[1] // 2, idk, idq)
     l_w.wait(); l_ga.wait()
     gat[...] = ga[...].T
     assemble_pairs(w, wp, feats)
@@ -1032,8 +1122,10 @@
     for m in l_q:
         m.wait()
     l_x.wait()
-    table = {0: [ev_dy(0), ev_ux(0)], 1: [PO.ev1], 3: [ev_dy(1), ev_ux(1)], 6: [ev_dy(2), P0.ev1], 7: [dz.middle, ev_ux(2)],
-             9: [ev_dy(3)], 10: [ev_ux(3), uz.middle], 12: [P1.ev1, PO.ev2], 13: [ev_df], 14: [P0.ev2], 15: [ev_ut, PO.ev3, ZO.z.start], 16: [P1.ev2], 17: [P0.ev3, ev_uf]}
+    def ev_b():
+        dz.b.start(); uz.b.start()
+    table = {0: [ev_dy(0), ev_ux(0)], 1: [PO.ev1], 4: [ev_dy(1), ev_ux(1), dz.middle], 7: [ev_dy(2), ev_ux(2), P0.ev1], 8: [uz.middle], 9: [ev_b],
+             11: [ev_dy(3), ev_ux(3)], 13: [PO.ev2, P1.ev1], 16: [PO.ev3, ZO.z.start, P0.ev2]}
     cuts = {1: 0, 3: 1, 4: 2}
 
     def head(i, _):
@@ -1087,6 +1179,16 @@
         at(i, {1: [P0.start], 3: [P1.start]})
         return 0
     lax.fori_loop(0, 6, head, 0)
+    sv[...] = jnp.zeros_like(sv)
+    for i in range(6):
+        sv[pl.ds(i, 1), :] = jnp.sum(vgrad[i], axis=0, keepdims=True)
+    for i in range(nz):
+        sv[pl.ds(6 + i, 1), :] = jnp.sum(bupgrad[i], axis=0, keepdims=True)
+    for p in range(3):
+        t = jnp.sum(group_sum(gp[p].astype(F32)), axis=0, keepdims=True)
+        sv[pl.ds(6 + nz + p, 1), pl.ds(0, 384)] = jnp.where(k == 0, t, 0.0)
+        sv[pl.ds(6 + nz + p, 1), pl.ds(384, 384)] = jnp.where(k == 1, t, 0.0)
+    s_k = n.send(all_of(sv), all_of(svk), n.kp)
     sw = lambda a: pltpu.roll(a, 64, 1)
 
     def last(cc, _):
@@ -1115,60 +1217,53 @@
         gs[r, :] = v.astype(BF)
     half_rows(1 - k, put_other)
     g_k = n.send(all_of(gs), all_of(gr), n.kp)
+    s_k.wait_recv()
+    svt[...] = sv[...] + svk[...]
+    s_y = n.send(all_of(svt), all_of(svy), n.yp)
     P2.ev1(); P3.ev1()
-    sv[...] = jnp.zeros_like(sv)
-    for i in range(6):
-        sv[pl.ds(i, 1), :] = jnp.sum(vgrad[i], axis=0, keepdims=True)
-    for i in range(nz):
-        sv[pl.ds(6 + i, 1), :] = jnp.sum(bupgrad[i], axis=0, keepdims=True)
-    for p in range(3):
-        t = jnp.sum(group_sum(gp[p].astype(F32)), axis=0, keepdims=True)
-        sv[pl.ds(6 + nz + p, 1), pl.ds(0, 384)] = jnp.where(k == 0, t, 0.0)
-        sv[pl.ds(6 + nz + p, 1), pl.ds(384, 384)] = jnp.where(k == 1, t, 0.0)
-    s_k = n.send(all_of(sv), all_of(svk), n.kp)
-    P1.ev3()
-    Z01.z.start()
-    ZO.z.middle()
+    P1.ev2(); P0.ev3()
+    ev_ut()
+    ev_df()
     for m in l_o:
         m.wait()
+    g4[:, :, pl.ds(b, g4.shape[2] - b)] = jnp.zeros((4, own_rows, g4.shape[2] - b), BF)
     def put_own(r, v):
         g1[r, :] = g1[r, :] + v
     half_rows(k, put_own)
-    P2.ev2(); P3.ev2()
-    s_k.wait_recv()
-    svt[...] = sv[...] + svk[...]
-    s_y = n.send(all_of(svt), all_of(svy), n.yp)
+    s_y.wait_recv()
+    svo[...] = svt[...] + svy[...]
+    s_x = n.send(all_of(svo), all_of(svx), n.xp)
+    P1.ev3(); Z01.z.start(); ZO.z.middle()
+    P2.ev2()
     g_k.wait_recv()
 
     def own(i, _):
         r = pl.ds(pl.multiple_of(i * 48, 16), 48)
         v = g1[r, :] + gr[r, :].astype(F32)
         for cc in range(4):
-            g4[cc, r, :] = v[:, cc * b:(cc + 1) * b].astype(BF)
+            g4[cc, r, fb] = v[:, cc * b:(cc + 1) * b].astype(BF)
         return 0
     lax.fori_loop(0, own_rows // 48, own, 0)
     g_l = n.local(lambda: g4.at[c], lambda: grad4.at[y, k])
     dst = lambda: grad4.at[y, k]
     g_s = [n.send(lambda: g4.at[n.oc], dst, n.yp), n.send(lambda: g4.at[3 - c], dst, n.ykp), n.send(lambda: g4.at[c + 1 - 2 * k], dst, n.kp)]
-    P2.ev3(); Z2.z.start()
-    P3.ev3(); Z3.z.start()
-    s_y.wait_recv()
-    svo[...] = svt[...] + svy[...]
-    s_x = n.send(all_of(svo), all_of(svx), n.xp)
-    Z01.z.middle(); ZO.end()
-    half = (lout.shape[1] - length) // 2
-    for s in range(2):
-        lo32[pl.ds(0, half), :] = o4[s, 0, pl.ds(main, 16), :].astype(F32)[:half]
-        lo32[pl.ds(half, main), :] = o4[s, 0, pl.ds(0, main), :].astype(F32)
-        lo32[pl.ds(half + main, main), :] = o4[s, 1, pl.ds(0, main), :].astype(F32)
-        lo32[pl.ds(half + length, 16 - half), :] = o4[s, 0, pl.ds(main, 16), :].astype(F32)[half:]
-        lo32[pl.ds(length + 16, 2 * half - 16), :] = o4[s, 1, pl.ds(main, 16), :].astype(F32)[:2 * half - 16]
-        lout[s] = lo32[pl.ds(0, length + 2 * half), :].astype(BF)
-    Z2.z.middle(); Z3.z.middle()
+    P3.ev2()
     s_x.wait_recv()
     svz[z] = pairs_sum(svo[...] + svx[...], ps, lambda s, i: s.at[i])
     s_z = [n.send(lambda: svz.at[z], lambda: svz.at[z], n.zp[i]) for i in range(1, nz)]
-    Z01.end()
+    P2.ev3(); Z2.z.start()
+    ev_uf()
+    Z01.z.middle(); ZO.end()
+    P3.ev3(); Z3.z.start()
+    half = (lout.shape[1] - length) // 2
+    for s in range(2):
+        lo32[pl.ds(0, half), :] = o4[s, 0, pl.ds(main, 16), fb].astype(F32)[:half]
+        lo32[pl.ds(half, main), :] = o4[s, 0, pl.ds(0, main), fb].astype(F32)
+        lo32[pl.ds(half + main, main), :] = o4[s, 1, pl.ds(0, main), fb].astype(F32)
+        lo32[pl.ds(half + length, 16 - half), :] = o4[s, 0, pl.ds(main, 16), fb].astype(F32)[half:]
+        lo32[pl.ds(length + 16, 2 * half - 16), :] = o4[s, 1, pl.ds(main, 16), fb].astype(F32)[:2 * half - 16]
+        lout[s] = lo32[pl.ds(0, length + 2 * half), :].astype(BF)
+    Z2.z.middle(); Z01.end(); Z3.z.middle()
     d_x.wait_recv()
     fd[...] = pairs_sum(total_of([df, dx]), pd, lambda s, i: s.at[i])
     u_f.wait_recv()
@@ -1216,11 +1311,11 @@
         m.wait_recv()
     g_l.wait()
     for s in range(2):
-        gmem[s, pl.ds(0, 16), :] = grad4[s, 0, pl.ds(main, 16), :].astype(F32)
-        gmem[s, pl.ds(16, 2 * half - 16), :] = grad4[s, 1, pl.ds(main, 16), :].astype(F32)[:2 * half - 16]
+        gmem[s, pl.ds(0, 16), :] = grad4[s, 0, pl.ds(main, 16), fb].astype(F32)
+        gmem[s, pl.ds(16, 2 * half - 16), :] = grad4[s, 1, pl.ds(main, 16), fb].astype(F32)[:2 * half - 16]
     n.finish()
 
-def backward(hu, hd, ga, mixed, xt, qt, kt, vt, w, o4, g1, lse, vgrad, bupgrad, idk, idq, half, nz, nd):
+def backward(hu, hd, ga, mixed, xt, qt, kt, vt, w, o4, g1, lse, vgrad, bupgrad, ids, half, nz, nd):
     b, width = hu.shape[2:]
     feats = 4 * b; hb = b // 2; rows = ga.shape[0]; own = g1.shape[0]; length = 2 * (own - 16)
     V = lambda *s, d=BF: pltpu.VMEM(s, d)
@@ -1230,16 +1325,16 @@
     pw = (hb, width) if nd > 2 else (16, 128)
     t3 = V(3, rows, 128); f3 = lambda *s: V(*s, d=F32)
     sm = f3(16, feats)
-    outs = (S((2, 2, own, b), BF), S((2, length + 2 * half, b), BF), S((2, 2 * half, b), F32), S((3, b, b), F32), S((b, b), F32), S((b, width), F32), S((b, width), F32), S((8, b), F32), S((1, feats), F32), S((3, 128), F32))
+    outs = (S((2, 2, own, 256), BF), S((2, length + 2 * half, b), BF), S((2, 2 * half, b), F32), S((3, b, b), F32), S((b, b), F32), S((b, width), F32), S((b, width), F32), S((8, b), F32), S((1, feats), F32), S((3, 128), F32))
     scratch = [V(2, nz, hb, width), V(nz, b, width), V(2, nz, hb, width), V(2, 2, hb, width), V(2, hb, width), V(2, hb, width), V(hb, width), V(b, width), V(np_, *pw),
                V(nz, b, width), V(2, b, width), V(b, width), V(b, width), V(b, width), V(np_, b, width) if nd > 2 else V(1, 16, 128),
                V(2, nz, b, width), V(2, nz, hb, width), V(nz, hb, width), V(nz, b, width), V(nz, hb, width), V(2, hb, width), V(hb, width), V(b, width), V(np_, *pw), V(2, 4, b, width),
                V(rows, feats), t3, V(*xt.shape), t3, t3, t3, V(*w.shape), V(*o4.shape), f3(*g1.shape), V(3, feats, 384), V(feats, 384), V(feats, rows), t3, V(3, rows, 384),
-               f3(rows, 128), f3(rows, 128), f3(128, rows), V(128, rows), f3(2, 1, rows), V(4, own, b), V(own, feats), V(own, feats), f3(rows, b),
-               sm, sm, sm, sm, sm, sm, f3(np_, 16, feats), f3(nz, 16, feats),
+               f3(rows, 128), f3(rows, 128), f3(128, rows), V(128, rows), f3(2, 1, rows), V(4, own, 256), V(own, feats), V(own, feats), f3(rows, b),
+               sm, sm, sm, sm, sm, sm, f3(np_, 16, feats), f3(nz, 16, feats), f3(length + 128, 128), f3(1, length + 128),
                pltpu.SemaphoreType.DMA((128 + 5 * nd,)), pltpu.SemaphoreType.DMA((128 + 5 * nd,)), pltpu.SemaphoreType.DMA((40,))]
-    return pl.pallas_call(backward_kernel, out_shape=outs, in_specs=[an] * 11 + [vm] * 5, out_specs=(vm,) * len(outs), scratch_shapes=scratch,
-        compiler_params=pltpu.CompilerParams(collective_id=2, has_side_effects=True, vmem_limit_bytes=67043328))(hu, hd, ga, mixed, xt, qt, kt, vt, w, o4, g1, lse, vgrad, bupgrad, idk, idq)
+    return pl.pallas_call(backward_kernel, out_shape=outs, in_specs=[an] * 11 + [vm] * 4, out_specs=(vm,) * len(outs), scratch_shapes=scratch,
+        compiler_params=pltpu.CompilerParams(collective_id=2, has_side_effects=True, vmem_limit_bytes=67043328))(hu, hd, ga, mixed, xt, qt, kt, vt, w, o4, g1, lse, vgrad, bupgrad, ids)
 
 def per_device(tokens, memory, block_ids, valid, teacher, w_qkv, bias_qv, w_out, bias_out, ln1_gain, ln1_bias, w_up, bias_up, w_down, bias_down, ln2_gain, ln2_bias):
     _, b, length = tokens.shape
@@ -1250,20 +1345,10 @@
     half = memory.shape[1] // 2
     main = length // 2
     rows = length + 32
-    wq = w_qkv.reshape(3, b, 192)
-    wo = jnp.transpose(w_out)
-    la = jnp.concatenate([wq[0, :, :64], wq[1, :, :64], wq[0, :, 64:128], wq[1, :, 64:128], wq[0, :, 128:], wq[1, :, 128:], wq[2], wo[:, 128:], wo[:, :128]], axis=1)
-    mem = jnp.pad(jnp.swapaxes(memory, 1, 2), ((0, 0), (0, 0), (0, 128 - 2 * half)))
-    scale = (valid.shape[0] * length) / jnp.sum(valid).astype(F32)
-    fv = jnp.stack([bias_out, ln1_gain, ln1_bias, bias_down, ln2_gain, ln2_bias, jnp.full((b,), scale, F32), jnp.zeros((b,), F32)])
-    ls = jnp.concatenate([jnp.pad(fv, ((0, 0), (0, 256 - b))), bias_up.reshape(3, 256), jnp.pad(bias_qv.reshape(1, 384), ((0, 0), (0, 128))).reshape(2, 256), jnp.zeros((3, 256), F32)])
-    ids = lax.dynamic_index_in_dim(block_ids, y, 0, keepdims=False)
-    ids = jnp.concatenate([ids, jnp.full((half,), -1, jnp.int32), jnp.full((half,), length, jnp.int32), jnp.full((32 - 2 * half,), 2 * length, jnp.int32)])
-    idk = jnp.broadcast_to(ids[:, None], (rows, 128))
-    count = lax.dynamic_index_in_dim(valid, (d * nz + z) * 2 + y, 0)
-    xt, qt, kt, vt, mixed, wown, ga, hu, hd, lse, g_one, vgrad, bupgrad, out4 = forward(count, tokens, mem, teacher, la, w_up, w_down, ls, idk, ids[None], nz)
-    grad4, lout, gmem, g3, gwo, fu, fd, fvec, bup, bqv = backward(hu, hd, ga, mixed, xt, qt, kt, vt, wown, out4, g_one, lse, vgrad, bupgrad, idk, ids[None], half, nz, nd)
-    grad_tokens = grad4[:, :, :main].reshape(2, length, b).astype(F32)
+    one = lambda a: a.reshape(1, -1)
+    xt, qt, kt, vt, mixed, wown, ga, hu, hd, lse, g_one, vgrad, bupgrad, out4 = forward(valid, tokens, memory, teacher, w_qkv.reshape(3, b, 192), w_out, w_up, w_down, [one(a) for a in (bias_out, ln1_gain, ln1_bias, bias_down, ln2_gain, ln2_bias)], one(bias_up), bias_qv, block_ids, nz)
+    grad4, lout, gmem, g3, gwo, fu, fd, fvec, bup, bqv = backward(hu, hd, ga, mixed, xt, qt, kt, vt, wown, out4, g_one, lse, vgrad, bupgrad, block_ids, half, nz, nd)
+    grad_tokens = grad4[:, :, :main, :b].reshape(2, length, b).astype(F32)
     return (lout, grad_tokens, gmem, g3.reshape(3, b * b), bqv, gwo, fvec[5], fvec[3], fvec[4], fu, bup[0], fd, fvec[2], fvec[0], fvec[1])
 
 def solution(mesh):

time: 267 us -> 226 us (0.85)
  Pallas kernels: 240 us -> 210 us
  local copies, waits for them, and re-layouts: 21.8 us -> 14.1 us
    pallas_call x1, Pallas kernels: 107 us -> 87.7 us  [backward(): pl.pallas_call(backward_kernel, out_shape=outs, in_specs=[an] * 11 + [vm]...]
    pallas_call x1, Pallas kernels: 133 us -> 123 us  [forward(): pl.pallas_call(forward_kernel, out_shape=[o for o, _ in outs], out_specs=...]
    unnamed x28 -> x26, local copies, waits for them, and re-layouts: 10.2 us -> 8.99 us
where the time goes in v4:
time: 226 us
  Pallas kernels  210 us (93%)
  local copies, waits for them, and re-layouts  14.1 us (6%)
    pallas_call x1, Pallas kernels, forward(): pl.pallas_call(forward_kernel, out_shape=[o for o, _ in outs], out_specs=...  123 us
    pallas_call x1, Pallas kernels, backward(): pl.pallas_call(backward_kernel, out_shape=outs, in_specs=[an] * 11 + [vm]...  87.7 us
    unnamed x26, local copies, waits for them, and re-layouts  8.99 us

profile of v4, /device:TPU:0, one launch (start us, length us, event | category | flops | bytes accessed | tf_op | source)
XLA Modules:
  0.0 226.0 jit_solution(5883146881918938239)
XLA Ops:
  0.6 1.3 reshape.67.bias_up
  1.9 1.3 copy.32.memory
  3.3 2.0 reshape.60.w3
  5.3 122.6 %shard_map.280 = (bf16[768,1152]{1,0:T(8,128)(2,1)}, bf16[3,1056,128]{2,1,0:T(8,128)(2,1)}, bf16[3,1056,128]{2,1,0:T(8,128)(2,1)}, bf16[3,1056,128]{2,1,0:T(8,12...) custom-call(s32[16]{0:T(128)} %valid_ref.1, ...), custom_call_target="tpu_custom_call" | custom-call | tf_op jit(solution)/shard_map/pallas_call | solution.py:939
  127.9 87.7 %shard_map.281 = (bf16[2,2,528,256]{3,2,1,0:T(8,128)(2,1)}, bf16[2,1044,192]{2,1,0:T(8,128)(2,1)}, f32[2,20,192]{2,1,0:T(8,128)}, f32[3,192,192]{2,1,0:T(8,128)}...) custom-call(bf16[2,4,192,768]{3,2,1,0:T(8,128)(2,1)} %get-tuple-elem, ...), custom_call_target="tpu_custom_call" | custom-call | tf_op jit(solution)/shard_map/pallas_call | solution.py:1336
  215.6 0.0 copy-start.7
  215.6 0.0 copy-start.6
  215.6 0.0 copy-start.5
  215.6 0.0 copy-start.3
  215.6 0.0 copy-start
  215.6 2.4 %copy.33 = bf16[2,1044,192]{1,2,0:T(8,128)(2,1)} copy(bf16[2,1044,192]{2,1,0:T(8,128)(2,1)} %get-tuple-element.63) | data formatting | bytes 1603584
  218.0 0.0 copy-done.7
  218.0 0.6 reduce
  218.6 0.0 copy-done.6
  218.6 0.6 fusion
  219.2 0.0 copy-done.5
  219.2 0.6 copy.35
  219.9 0.0 copy-done.3
  219.9 1.2 reshape.68
  221.1 0.0 copy-done
  221.1 0.1 slice.21
  221.2 0.2 bitcast_convert_fusion
  221.4 0.0 copy-start.8
  221.4 0.0 copy-start.4
  221.4 0.0 copy-start.2
  221.4 0.0 copy-start.1
  221.4 1.7 copy.34
  223.1 0.0 copy-done.8
  223.1 0.6 copy.40
  223.7 0.0 copy-done.4
  223.7 0.7 copy.41
  224.4 0.0 copy-done.2
  224.4 0.8 copy.42
  225.2 0.0 copy-done.1
  225.2 0.8 copy.43
Async XLA Ops:
  215.6 2.4 %copy-start.7 = (f32[1,768]{1,0:T(1,128)S(1)}, f32[1,768]{1,0:T(1,128)}, u32[]{:S(2)}) copy-start(f32[1,768]{1,0:T(1,128)} %get-tuple-element.61) | copy-start | bytes 9220
  215.6 3.0 %copy-start.6 = (f32[8,192]{1,0:T(8,128)S(1)}, f32[8,192]{1,0:T(8,128)}, u32[]{:S(2)}) copy-start(f32[8,192]{1,0:T(8,128)} %get-tuple-element.59) | copy-start | bytes 18436
  215.6 3.6 %copy-start.5 = (f32[2,20,192]{2,1,0:T(8,128)S(1)}, f32[2,20,192]{2,1,0:T(8,128)}, u32[]{:S(2)}) copy-start(f32[2,20,192]{2,1,0:T(8,128)} %get-tuple-element.65) | copy-start | bytes 92164
  215.6 4.3 %copy-start.3 = (f32[3,192,192]{2,1,0:T(8,128)S(1)}, f32[3,192,192]{2,1,0:T(8,128)}, u32[]{:S(2)}) copy-start(f32[3,192,192]{2,1,0:T(8,128)} %get-tuple-element.56) | copy-start | bytes 1327108
  215.6 5.5 %copy-start = (bf16[2,2,528,256]{3,2,1,0:T(8,128)(2,1)S(1)}, bf16[2,2,528,256]{3,2,1,0:T(8,128)(2,1)}, u32[]{:S(2)}) copy-start(bf16[2,2,528,256]{3,2,1,0:T(8,128)(2,1)} %get-tuple-element.54) | copy-start | bytes 3244036
  221.4 1.7 copy-start.8
  221.4 2.3 %copy-start.4 = (f32[192,192]{1,0:T(8,128)S(1)}, f32[192,192]{1,0:T(8,128)}, u32[]{:S(2)}) copy-start(f32[192,192]{1,0:T(8,128)} %get-tuple-element.104) | copy-start | bytes 442372
  221.4 3.0 %copy-start.2 = (f32[192,768]{1,0:T(8,128)S(1)}, f32[192,768]{1,0:T(8,128)}, u32[]{:S(2)}) copy-start(f32[192,768]{1,0:T(8,128)} %get-tuple-element.108) | copy-start | bytes 1769476
  221.4 3.8 %copy-start.1 = (f32[192,768]{1,0:T(8,128)S(1)}, f32[192,768]{1,0:T(8,128)}, u32[]{:S(2)}) copy-start(f32[192,768]{1,0:T(8,128)} %get-tuple-element.110) | copy-start | bytes 1769476

commit v5 on v4

--- a/solution.py
+++ b/solution.py
@@ -395,11 +395,15 @@
         self.others = [(lax.rem(self.d + 2 * i, self.nd), self.z, self.c) for i in range(1, self.nd // 2)]
     def from_row(self, i):
         return self.zs[(self.nz - i) % self.nz]
-    def barrier(self, peers):
+    def hello(self, peers):
         b = pltpu.get_barrier_semaphore()
         for p in peers:
             pl.semaphore_signal(b, inc=1, device_id=p, device_id_type=MESH)
-        pl.semaphore_wait(b, len(peers))
+    def await_hello(self, peers):
+        pl.semaphore_wait(pltpu.get_barrier_semaphore(), len(peers))
+    def barrier(self, peers):
+        self.hello(peers)
+        self.await_hello(peers)
     def move(self, src, dst, dev):
         m = Move(self, src, dst, dev, self.count)
         self.count += 1
@@ -485,11 +489,13 @@
                    xt, x, wa, wu, wd, sm, tt, tr, wp, qt, kt, vt, vtt, ot, mixed, mrows, bias, vec, wt,
                    h1, h2, rs1, low, lowt, br, brt, hid, dgl, gdz, guz, hu, hd, ru, rd, ga, o4, la, ls, mem, mtmp, idk, idq, ss, rs, lsem, zsem, zrem):
     n = Net(ss, rs, lsem)
+    peers = n.zp[1:] + [n.yp, n.ykp, n.kp, n.xp]
+    n.hello(peers)
     total = lax.fori_loop(0, valid_ref.shape[0], lambda i, t: t + valid_ref[i], jnp.int32(0))
     count = valid_ref[(n.d * n.nz + n.z) * 2 + n.y]
     scale_row = (valid_ref.shape[0] * tok.shape[2]) / jnp.full((1, 256), total, jnp.int32).astype(F32)
     pack_inputs(w3, wo, la, (v0, v1, v2, v3, v4, v5), bias_up, bias_qv, scale_row, ls, memory, mtmp, mem)
-    n.barrier(n.zp[1:] + [n.yp, n.ykp, n.kp, n.xp])
+    n.await_hello(peers)
     nz, y, k, c, z, oc = n.nz, n.y, n.k, n.c, n.z, n.oc
     b = la.shape[0]; hb = b // 2
     feats = x.shape[1]; rows = x.shape[0]; length = tok.shape[2]; main = length // 2
@@ -541,7 +547,6 @@
     a2.wait_recv()
     a3 = fwd(au(e2, c), dev1); a3.start()
     a_own(e2)
-    t_y = [n.send(lambda: tok.at[1 - y], lambda: xt.at[row(c), body], n.yp), n.send(lambda: mem.at[1 - y], lambda: xt.at[row(c), tail], n.yp)]
     a1.wait_recv()
     a_own(e1)
     a_far(1)
@@ -550,6 +555,7 @@
         pass_on(s_blk(fz(i), c), ((s_y, n.yp), (s_k, n.kp)))
     a3.wait_recv()
     a_own(e3)
+    t_y = [n.send(lambda: tok.at[1 - y], lambda: xt.at[row(c), body], n.yp), n.send(lambda: mem.at[1 - y], lambda: xt.at[row(c), tail], n.yp)]
     uu = lambda zz, cc: blk(wu, zz, cc)
     du = lambda zz, cc: hlf(wd, zz, cc, mine)
     u2 = n.send(all_of(lu), uu(z, c), dev2)
@@ -562,13 +568,20 @@
     th = lambda: tt.at[row(c)]
     h_y = [n.send(tsl(y, 1 - k), th, n.kp)]
     local.append(n.local(tsl(y, k), th))
+    a_far(2)
+    a_far(3)
     row_ids(ids, y, memory.shape[1] // 2, idk, idq)
+    for i in range(3):
+        a_home(i)
+    for i in range(nz):
+        s_y[i].wait_recv()
+        pass_on(s_blk(fz(i), oc), ((s_k, n.kp),))
+    local[0].wait(); local[1].wait()
+    a_home(3)
     for m, w_ in zip(t_y, (body, tail)):
         m.wait_recv()
         t_k.append(fwd((lambda w_=w_: xt.at[row(oc), w_]), n.kp)); t_k[-1].start()
-    for i in range(3):
-        a_home(i)
-    local[0].wait(); local[1].wait()
+    a_home(4)
     for m in t_k:
         m.wait_recv()
     def turn(i, _):
@@ -578,13 +591,6 @@
     lax.fori_loop(0, length // 128, turn, 0)
     x[pl.ds(length, rows - length), :] = xt[:, tail].T[: rows - length, :]
     o_x = n.local(all_of(xt), all_of(xt_o))
-    for i in range(nz):
-        s_y[i].wait_recv()
-        pass_on(s_blk(fz(i), oc), ((s_k, n.kp),))
-    a_far(2)
-    a_far(3)
-    for i in range(3, 5):
-        a_home(i)
     u2.wait_recv()
     u3 = fwd(uu(e2, c), dev1); u3.start()
     d2 = n.send(part(ld), du(z, c), dev2)
@@ -597,14 +603,12 @@
             u_y[-1].start()
         m.start()
     u_put(1, c)
-    d_y.wait_recv()
     d_x, d_xu = [], []
     def d_put(zz, cc):
         d_xu.append((zz, cc))
         d_x.append(fwd(du(zz, cc), n.xp)); d_k.append(fwd(du(zz, cc), n.kp))
         return [d_x[-1], d_k[-1]]
-    for m in d_put(z, oc):
-        m.start()
+    d_own = d_put(z, oc)
     for i in range(5, 7):
         a_home(i)
     def step(wait, moves):
@@ -621,6 +625,7 @@
     def u_far(i):
         u_w.append(fwd(uu(order[i], oc), n.kp))
         return step(u_y[i], [u_w[-1]])
+    E_dy = step(d_y, d_own)
     d3, d2o, d1o, d3o = fwd(du(e2, c), dev1), fwd(du(z, oc), dev2), fwd(du(z, oc), dev1), fwd(du(e2, oc), dev1)
     E_u1 = u_step(u1, 2)
     E_u3 = u_step(u3, 3)
@@ -642,8 +647,8 @@
     for m, (zz, cc) in zip(d_x, d_xu):
         d_k.append(fwd(hlf(wd, zz, cc, theirs), n.kp))
         E_dx.append(step(m, [d_k[-1]]))
-    proj_events = {1: [E_u1], 8: [E_u3, E_h]}
-    head_events = {2: [E_do, E_dx[0]], 4: [E_uy[0]], 6: [E_d2], 8: [E_d1], 10: [E_d3, E_uy[1]], 12: [E_dx[1], E_dx[2]], 14: [E_d2o, E_uy[2]], 16: [E_d1o, E_dx[3]]}
+    proj_events = {0: [E_dy], 1: [E_u1]}
+    head_events = {2: [E_do, E_dx[0]], 4: [E_uy[0], E_u3, E_h], 6: [E_d2], 8: [E_d1], 10: [E_uy[1]], 12: [E_dx[1], E_dx[2]], 13: [E_d3], 14: [E_d2o], 15: [E_uy[2]], 17: [E_d1o, E_dx[3]]}
     out_events = [E_d3o]
     gate_events = {0: [], 3: [], 6: [E_dx[4], E_dx[5]], 9: [E_dx[6]]}
     for m in s_k:
@@ -1124,8 +1129,8 @@
     l_x.wait()
     def ev_b():
         dz.b.start(); uz.b.start()
-    table = {0: [ev_dy(0), ev_ux(0)], 1: [PO.ev1], 4: [ev_dy(1), ev_ux(1), dz.middle], 7: [ev_dy(2), ev_ux(2), P0.ev1], 8: [uz.middle], 9: [ev_b],
-             11: [ev_dy(3), ev_ux(3)], 13: [PO.ev2, P1.ev1], 16: [PO.ev3, ZO.z.start, P0.ev2]}
+    table = {0: [ev_dy(0), ev_ux(0)], 1: [PO.ev1], 4: [ev_dy(1), ev_ux(1)], 6: [dz.middle], 7: [ev_dy(2), ev_ux(2), P0.ev1], 9: [uz.middle], 10: [ev_b],
+             11: [ev_dy(3), ev_ux(3)], 13: [PO.ev2], 15: [P1.ev1], 16: [PO.ev3, ZO.z.start, P0.ev2]}
     cuts = {1: 0, 3: 1, 4: 2}
 
     def head(i, _):
@@ -1220,10 +1225,9 @@
     s_k.wait_recv()
     svt[...] = sv[...] + svk[...]
     s_y = n.send(all_of(svt), all_of(svy), n.yp)
+    P1.ev2(); P0.ev3()
     P2.ev1(); P3.ev1()
-    P1.ev2(); P0.ev3()
     ev_ut()
-    ev_df()
     for m in l_o:
         m.wait()
     g4[:, :, pl.ds(b, g4.shape[2] - b)] = jnp.zeros((4, own_rows, g4.shape[2] - b), BF)
@@ -1233,6 +1237,7 @@
     s_y.wait_recv()
     svo[...] = svt[...] + svy[...]
     s_x = n.send(all_of(svo), all_of(svx), n.xp)
+    ev_df()
     P1.ev3(); Z01.z.start(); ZO.z.middle()
     P2.ev2()
     g_k.wait_recv()

time: 226 us -> 220 us (0.973)
  Pallas kernels: 210 us -> 203 us
    pallas_call x1, Pallas kernels: 87.7 us -> 82.3 us  [backward(): pl.pallas_call(backward_kernel, out_shape=outs, in_specs=[an] * 11 + [vm]...]
where the time goes in v5:
time: 220 us; the launch traced here: 219 us
  Pallas kernels  203 us (92%)
  local copies, waits for them, and re-layouts  14.1 us (6%)
    pallas_call x1, Pallas kernels, forward(): pl.pallas_call(forward_kernel, out_shape=[o for o, _ in outs], out_specs=...  121 us
    pallas_call x1, Pallas kernels, backward(): pl.pallas_call(backward_kernel, out_shape=outs, in_specs=[an] * 11 + [vm]...  82.3 us
    unnamed x26, local copies, waits for them, and re-layouts  8.99 us

profile of v5, /device:TPU:0, one launch (start us, length us, event | category | flops | bytes accessed | tf_op | source)
XLA Modules:
  0.0 219.2 jit_solution(8553759279733727763)
XLA Ops:
  0.6 1.3 reshape.67.bias_up
  1.9 1.3 copy.32.memory
  3.3 2.0 reshape.60.w3
  5.3 121.2 %shard_map.280 = (bf16[768,1152]{1,0:T(8,128)(2,1)}, bf16[3,1056,128]{2,1,0:T(8,128)(2,1)}, bf16[3,1056,128]{2,1,0:T(8,128)(2,1)}, bf16[3,1056,128]{2,1,0:T(8,12...) custom-call(s32[16]{0:T(128)} %valid_ref.1, ...), custom_call_target="tpu_custom_call" | custom-call | tf_op jit(solution)/shard_map/pallas_call | solution.py:944
  126.5 82.3 %shard_map.281 = (bf16[2,2,528,256]{3,2,1,0:T(8,128)(2,1)}, bf16[2,1044,192]{2,1,0:T(8,128)(2,1)}, f32[2,20,192]{2,1,0:T(8,128)}, f32[3,192,192]{2,1,0:T(8,128)}...) custom-call(bf16[2,4,192,768]{3,2,1,0:T(8,128)(2,1)} %get-tuple-elem, ...), custom_call_target="tpu_custom_call" | custom-call | tf_op jit(solution)/shard_map/pallas_call | solution.py:1341
  208.8 0.0 copy-start.7
  208.8 0.0 copy-start.6
  208.8 0.0 copy-start.5
  208.8 0.0 copy-start.3
  208.8 0.0 copy-start
  208.8 2.4 %copy.33 = bf16[2,1044,192]{1,2,0:T(8,128)(2,1)} copy(bf16[2,1044,192]{2,1,0:T(8,128)(2,1)} %get-tuple-element.63) | data formatting | bytes 1603584
  211.2 0.0 copy-done.7
  211.2 0.6 reduce
  211.8 0.0 copy-done.6
  211.8 0.6 fusion
  212.4 0.0 copy-done.5
  212.4 0.6 copy.35
  213.1 0.0 copy-done.3
  213.1 1.2 reshape.68
  214.3 0.0 copy-done
  214.3 0.1 slice.21
  214.3 0.2 bitcast_convert_fusion
  214.6 0.0 copy-start.8
  214.6 0.0 copy-start.4
  214.6 0.0 copy-start.2
  214.6 0.0 copy-start.1
  214.6 1.7 copy.34
  216.3 0.0 copy-done.8
  216.3 0.6 copy.40
  216.9 0.0 copy-done.4
  216.9 0.7 copy.41
  217.6 0.0 copy-done.2
  217.6 0.8 copy.42
  218.4 0.0 copy-done.1
  218.4 0.8 copy.43
Async XLA Ops:
  208.8 2.4 %copy-start.7 = (f32[1,768]{1,0:T(1,128)S(1)}, f32[1,768]{1,0:T(1,128)}, u32[]{:S(2)}) copy-start(f32[1,768]{1,0:T(1,128)} %get-tuple-element.61) | copy-start | bytes 9220
  208.8 3.0 %copy-start.6 = (f32[8,192]{1,0:T(8,128)S(1)}, f32[8,192]{1,0:T(8,128)}, u32[]{:S(2)}) copy-start(f32[8,192]{1,0:T(8,128)} %get-tuple-element.59) | copy-start | bytes 18436
  208.8 3.6 %copy-start.5 = (f32[2,20,192]{2,1,0:T(8,128)S(1)}, f32[2,20,192]{2,1,0:T(8,128)}, u32[]{:S(2)}) copy-start(f32[2,20,192]{2,1,0:T(8,128)} %get-tuple-element.65) | copy-start | bytes 92164
  208.8 4.3 %copy-start.3 = (f32[3,192,192]{2,1,0:T(8,128)S(1)}, f32[3,192,192]{2,1,0:T(8,128)}, u32[]{:S(2)}) copy-start(f32[3,192,192]{2,1,0:T(8,128)} %get-tuple-element.56) | copy-start | bytes 1327108
  208.8 5.5 %copy-start = (bf16[2,2,528,256]{3,2,1,0:T(8,128)(2,1)S(1)}, bf16[2,2,528,256]{3,2,1,0:T(8,128)(2,1)}, u32[]{:S(2)}) copy-start(bf16[2,2,528,256]{3,2,1,0:T(8,128)(2,1)} %get-tuple-element.54) | copy-start | bytes 3244036
  214.6 1.7 copy-start.8
  214.6 2.3 %copy-start.4 = (f32[192,192]{1,0:T(8,128)S(1)}, f32[192,192]{1,0:T(8,128)}, u32[]{:S(2)}) copy-start(f32[192,192]{1,0:T(8,128)} %get-tuple-element.104) | copy-start | bytes 442372
  214.6 3.0 %copy-start.2 = (f32[192,768]{1,0:T(8,128)S(1)}, f32[192,768]{1,0:T(8,128)}, u32[]{:S(2)}) copy-start(f32[192,768]{1,0:T(8,128)} %get-tuple-element.108) | copy-start | bytes 1769476
  214.6 3.8 %copy-start.1 = (f32[192,768]{1,0:T(8,128)S(1)}, f32[192,768]{1,0:T(8,128)}, u32[]{:S(2)}) copy-start(f32[192,768]{1,0:T(8,128)} %get-tuple-element.110) | copy-start | bytes 1769476

commit v6 on v5

--- a/solution.py
+++ b/solution.py
@@ -543,6 +543,11 @@
     def a_home(i):
         a_x[i].wait_recv()
         pass_on(hlf(wa, *a_xu[i], theirs), ((a_k, n.kp),))
+    first, second = pl.ds(0, main), pl.ds(main, main)
+    t_y = [n.send(lambda: tok.at[1 - y, :, first], lambda: xt.at[row(c), first], n.yp), n.send(lambda: mem.at[1 - y], lambda: xt.at[row(c), tail], n.yp)]
+    def t_pass(i, w_):
+        t_y[i].wait_recv()
+        t_k.append(fwd(lambda: xt.at[row(oc), w_], n.kp)); t_k[-1].start()
     a_far(0)
     a2.wait_recv()
     a3 = fwd(au(e2, c), dev1); a3.start()
@@ -555,7 +560,9 @@
         pass_on(s_blk(fz(i), c), ((s_y, n.yp), (s_k, n.kp)))
     a3.wait_recv()
     a_own(e3)
-    t_y = [n.send(lambda: tok.at[1 - y], lambda: xt.at[row(c), body], n.yp), n.send(lambda: mem.at[1 - y], lambda: xt.at[row(c), tail], n.yp)]
+    t_y.append(n.send(lambda: tok.at[1 - y, :, second], lambda: xt.at[row(c), second], n.yp))
+    t_pass(0, first)
+    t_pass(1, tail)
     uu = lambda zz, cc: blk(wu, zz, cc)
     du = lambda zz, cc: hlf(wd, zz, cc, mine)
     u2 = n.send(all_of(lu), uu(z, c), dev2)
@@ -578,9 +585,7 @@
         pass_on(s_blk(fz(i), oc), ((s_k, n.kp),))
     local[0].wait(); local[1].wait()
     a_home(3)
-    for m, w_ in zip(t_y, (body, tail)):
-        m.wait_recv()
-        t_k.append(fwd((lambda w_=w_: xt.at[row(oc), w_]), n.kp)); t_k[-1].start()
+    t_pass(2, second)
     a_home(4)
     for m in t_k:
         m.wait_recv()
@@ -648,8 +653,8 @@
         d_k.append(fwd(hlf(wd, zz, cc, theirs), n.kp))
         E_dx.append(step(m, [d_k[-1]]))
     proj_events = {0: [E_dy], 1: [E_u1]}
-    head_events = {2: [E_do, E_dx[0]], 4: [E_uy[0], E_u3, E_h], 6: [E_d2], 8: [E_d1], 10: [E_uy[1]], 12: [E_dx[1], E_dx[2]], 13: [E_d3], 14: [E_d2o], 15: [E_uy[2]], 17: [E_d1o, E_dx[3]]}
-    out_events = [E_d3o]
+    head_events = {2: [E_do, E_dx[0]], 4: [E_uy[0], E_u3, E_h], 6: [E_d2], 8: [E_d1], 10: [E_uy[1]], 14: [E_d3, E_d2o], 15: [E_uy[2], E_dx[1], E_dx[2]], 17: [E_d1o]}
+    out_events = [E_d3o, E_dx[3]]
     gate_events = {0: [], 3: [], 6: [E_dx[4], E_dx[5]], 9: [E_dx[6]]}
     for m in s_k:
         m.wait_recv()
@@ -1225,9 +1230,8 @@
     s_k.wait_recv()
     svt[...] = sv[...] + svk[...]
     s_y = n.send(all_of(svt), all_of(svy), n.yp)
-    P1.ev2(); P0.ev3()
+    P1.ev2()
     P2.ev1(); P3.ev1()
-    ev_ut()
     for m in l_o:
         m.wait()
     g4[:, :, pl.ds(b, g4.shape[2] - b)] = jnp.zeros((4, own_rows, g4.shape[2] - b), BF)
@@ -1237,6 +1241,8 @@
     s_y.wait_recv()
     svo[...] = svt[...] + svy[...]
     s_x = n.send(all_of(svo), all_of(svx), n.xp)
+    ev_ut()
+    P0.ev3()
     ev_df()
     P1.ev3(); Z01.z.start(); ZO.z.middle()
     P2.ev2()

time: 220 us -> 213 us (0.968)
  Pallas kernels: 203 us -> 197 us
    pallas_call x1, Pallas kernels: 121 us -> 116 us  [forward(): pl.pallas_call(forward_kernel, out_shape=[o for o, _ in outs], out_specs=...]
where the time goes in v6:
time: 213 us
  Pallas kernels  197 us (92%)
  local copies, waits for them, and re-layouts  14.1 us (7%)
    pallas_call x1, Pallas kernels, forward(): pl.pallas_call(forward_kernel, out_shape=[o for o, _ in outs], out_specs=...  116 us
    pallas_call x1, Pallas kernels, backward(): pl.pallas_call(backward_kernel, out_shape=outs, in_specs=[an] * 11 + [vm]...  80.9 us
    unnamed x26, local copies, waits for them, and re-layouts  8.99 us

profile of v6, /device:TPU:0, one launch (start us, length us, event | category | flops | bytes accessed | tf_op | source)
XLA Modules:
  0.0 212.6 jit_solution(11528077681925432929)
XLA Ops:
  0.6 1.3 reshape.67.bias_up
  1.9 1.3 copy.32.memory
  3.3 2.0 reshape.60.w3
  5.3 116.0 %shard_map.280 = (bf16[768,1152]{1,0:T(8,128)(2,1)}, bf16[3,1056,128]{2,1,0:T(8,128)(2,1)}, bf16[3,1056,128]{2,1,0:T(8,128)(2,1)}, bf16[3,1056,128]{2,1,0:T(8,12...) custom-call(s32[16]{0:T(128)} %valid_ref.1, ...), custom_call_target="tpu_custom_call" | custom-call | tf_op jit(solution)/shard_map/pallas_call | solution.py:949
  121.2 80.9 %shard_map.281 = (bf16[2,2,528,256]{3,2,1,0:T(8,128)(2,1)}, bf16[2,1044,192]{2,1,0:T(8,128)(2,1)}, f32[2,20,192]{2,1,0:T(8,128)}, f32[3,192,192]{2,1,0:T(8,128)}...) custom-call(bf16[2,4,192,768]{3,2,1,0:T(8,128)(2,1)} %get-tuple-elem, ...), custom_call_target="tpu_custom_call" | custom-call | tf_op jit(solution)/shard_map/pallas_call | solution.py:1347
  202.2 0.0 copy-start.7
  202.2 0.0 copy-start.6
  202.2 0.0 copy-start.5
  202.2 0.0 copy-start.3
  202.2 0.0 copy-start
  202.2 2.4 %copy.33 = bf16[2,1044,192]{1,2,0:T(8,128)(2,1)} copy(bf16[2,1044,192]{2,1,0:T(8,128)(2,1)} %get-tuple-element.63) | data formatting | bytes 1603584
  204.6 0.0 copy-done.7
  204.6 0.6 reduce
  205.2 0.0 copy-done.6
  205.2 0.6 fusion
  205.8 0.0 copy-done.5
  205.8 0.6 copy.35
  206.4 0.0 copy-done.3
  206.4 1.2 reshape.68
  207.7 0.0 copy-done
  207.7 0.1 slice.21
  207.7 0.2 bitcast_convert_fusion
  208.0 0.0 copy-start.8
  208.0 0.0 copy-start.4
  208.0 0.0 copy-start.2
  208.0 0.0 copy-start.1
  208.0 1.7 copy.34
  209.7 0.0 copy-done.8
  209.7 0.6 copy.40
  210.3 0.0 copy-done.4
  210.3 0.7 copy.41
  211.0 0.0 copy-done.2
  211.0 0.8 copy.42
  211.8 0.0 copy-done.1
  211.8 0.8 copy.43
Async XLA Ops:
  202.2 2.4 %copy-start.7 = (f32[1,768]{1,0:T(1,128)S(1)}, f32[1,768]{1,0:T(1,128)}, u32[]{:S(2)}) copy-start(f32[1,768]{1,0:T(1,128)} %get-tuple-element.61) | copy-start | bytes 9220
  202.2 3.0 %copy-start.6 = (f32[8,192]{1,0:T(8,128)S(1)}, f32[8,192]{1,0:T(8,128)}, u32[]{:S(2)}) copy-start(f32[8,192]{1,0:T(8,128)} %get-tuple-element.59) | copy-start | bytes 18436
  202.2 3.6 %copy-start.5 = (f32[2,20,192]{2,1,0:T(8,128)S(1)}, f32[2,20,192]{2,1,0:T(8,128)}, u32[]{:S(2)}) copy-start(f32[2,20,192]{2,1,0:T(8,128)} %get-tuple-element.65) | copy-start | bytes 92164
  202.2 4.3 %copy-start.3 = (f32[3,192,192]{2,1,0:T(8,128)S(1)}, f32[3,192,192]{2,1,0:T(8,128)}, u32[]{:S(2)}) copy-start(f32[3,192,192]{2,1,0:T(8,128)} %get-tuple-element.56) | copy-start | bytes 1327108
  202.2 5.5 %copy-start = (bf16[2,2,528,256]{3,2,1,0:T(8,128)(2,1)S(1)}, bf16[2,2,528,256]{3,2,1,0:T(8,128)(2,1)}, u32[]{:S(2)}) copy-start(bf16[2,2,528,256]{3,2,1,0:T(8,128)(2,1)} %get-tuple-element.54) | copy-start | bytes 3244036
  208.0 1.7 copy-start.8
  208.0 2.3 %copy-start.4 = (f32[192,192]{1,0:T(8,128)S(1)}, f32[192,192]{1,0:T(8,128)}, u32[]{:S(2)}) copy-start(f32[192,192]{1,0:T(8,128)} %get-tuple-element.104) | copy-start | bytes 442372
  208.0 3.0 %copy-start.2 = (f32[192,768]{1,0:T(8,128)S(1)}, f32[192,768]{1,0:T(8,128)}, u32[]{:S(2)}) copy-start(f32[192,768]{1,0:T(8,128)} %get-tuple-element.108) | copy-start | bytes 1769476
  208.0 3.8 %copy-start.1 = (f32[192,768]{1,0:T(8,128)S(1)}, f32[192,768]{1,0:T(8,128)}, u32[]{:S(2)}) copy-start(f32[192,768]{1,0:T(8,128)} %get-tuple-element.110) | copy-start | bytes 1769476

commit v7 on v6

--- a/solution.py
+++ b/solution.py
@@ -912,10 +912,14 @@
         vgrad[4] += group_sum(g)
         vgrad[5] += group_sum(gb.astype(F32))
         return 0
-    lax.fori_loop(0, own_rows // 16, norm1_back, 0, unroll=3)
-    g_main = lambda: ga.at[pl.ds(pl.multiple_of(k * main, 16), main)]
+    early = main // 16 // 6 * 3
+    g_rows = lambda start, num: (lambda: ga.at[pl.ds(pl.multiple_of(k * main + start, 16), num)])
     g_tail = lambda: ga.at[pl.ds(pl.multiple_of(length + k * 16, 16), 16)]
-    g_k = [n.send(g_main, g_main, n.kp), n.send(g_tail, g_tail, n.kp)]
+    g_first, g_rest = g_rows(0, early * 16), g_rows(early * 16, main - early * 16)
+    lax.fori_loop(0, early, norm1_back, 0, unroll=3)
+    g_k = [n.send(g_first, g_first, n.kp)]
+    lax.fori_loop(early, own_rows // 16, norm1_back, 0, unroll=3)
+    g_k += [n.send(g_rest, g_rest, n.kp), n.send(g_tail, g_tail, n.kp)]
     for m in g_k:
         m.wait_recv()
     o_g = n.local(all_of(ga), all_of(ga_o))

time: 213 us -> 212 us (level)
  no operation moved by 1% of the time
where the time goes in v7:
time: 212 us
  Pallas kernels  196 us (92%)
  local copies, waits for them, and re-layouts  14.1 us (7%)
    pallas_call x1, Pallas kernels, forward(): pl.pallas_call(forward_kernel, out_shape=[o for o, _ in outs], out_specs=...  115 us
    pallas_call x1, Pallas kernels, backward(): pl.pallas_call(backward_kernel, out_shape=outs, in_specs=[an] * 11 + [vm]...  80.9 us
    unnamed x26, local copies, waits for them, and re-layouts  8.99 us

profile of v7, /device:TPU:0, one launch (start us, length us, event | category | flops | bytes accessed | tf_op | source)
XLA Modules:
  0.0 212.1 jit_solution(13938725806758652903)
XLA Ops:
  0.6 1.3 reshape.67.bias_up
  1.9 1.3 copy.32.memory
  3.3 2.0 reshape.60.w3
  5.3 115.4 %shard_map.280 = (bf16[768,1152]{1,0:T(8,128)(2,1)}, bf16[3,1056,128]{2,1,0:T(8,128)(2,1)}, bf16[3,1056,128]{2,1,0:T(8,128)(2,1)}, bf16[3,1056,128]{2,1,0:T(8,12...) custom-call(s32[16]{0:T(128)} %valid_ref.1, ...), custom_call_target="tpu_custom_call" | custom-call | tf_op jit(solution)/shard_map/pallas_call | solution.py:953
  120.7 80.9 %shard_map.281 = (bf16[2,2,528,256]{3,2,1,0:T(8,128)(2,1)}, bf16[2,1044,192]{2,1,0:T(8,128)(2,1)}, f32[2,20,192]{2,1,0:T(8,128)}, f32[3,192,192]{2,1,0:T(8,128)}...) custom-call(bf16[2,4,192,768]{3,2,1,0:T(8,128)(2,1)} %get-tuple-elem, ...), custom_call_target="tpu_custom_call" | custom-call | tf_op jit(solution)/shard_map/pallas_call | solution.py:1351
  201.6 0.0 copy-start.7
  201.6 0.0 copy-start.6
  201.6 0.0 copy-start.5
  201.6 0.0 copy-start.3
  201.7 0.0 copy-start
  201.7 2.4 %copy.33 = bf16[2,1044,192]{1,2,0:T(8,128)(2,1)} copy(bf16[2,1044,192]{2,1,0:T(8,128)(2,1)} %get-tuple-element.63) | data formatting | bytes 1603584
  204.1 0.0 copy-done.7
  204.1 0.6 reduce
  204.7 0.0 copy-done.6
  204.7 0.6 fusion
  205.3 0.0 copy-done.5
  205.3 0.6 copy.35
  205.9 0.0 copy-done.3
  205.9 1.2 reshape.68
  207.1 0.0 copy-done
  207.1 0.1 slice.21
  207.2 0.2 bitcast_convert_fusion
  207.4 0.0 copy-start.8
  207.4 0.0 copy-start.4
  207.4 0.0 copy-start.2
  207.5 0.0 copy-start.1
  207.5 1.7 copy.34
  209.2 0.0 copy-done.8
  209.2 0.6 copy.40
  209.7 0.0 copy-done.4
  209.7 0.7 copy.41
  210.4 0.0 copy-done.2
  210.4 0.8 copy.42
  211.2 0.0 copy-done.1
  211.2 0.8 copy.43
Async XLA Ops:
  201.6 2.4 %copy-start.7 = (f32[1,768]{1,0:T(1,128)S(1)}, f32[1,768]{1,0:T(1,128)}, u32[]{:S(2)}) copy-start(f32[1,768]{1,0:T(1,128)} %get-tuple-element.61) | copy-start | bytes 9220
  201.6 3.0 %copy-start.6 = (f32[8,192]{1,0:T(8,128)S(1)}, f32[8,192]{1,0:T(8,128)}, u32[]{:S(2)}) copy-start(f32[8,192]{1,0:T(8,128)} %get-tuple-element.59) | copy-start | bytes 18436
  201.6 3.6 %copy-start.5 = (f32[2,20,192]{2,1,0:T(8,128)S(1)}, f32[2,20,192]{2,1,0:T(8,128)}, u32[]{:S(2)}) copy-start(f32[2,20,192]{2,1,0:T(8,128)} %get-tuple-element.65) | copy-start | bytes 92164
  201.6 4.3 %copy-start.3 = (f32[3,192,192]{2,1,0:T(8,128)S(1)}, f32[3,192,192]{2,1,0:T(8,128)}, u32[]{:S(2)}) copy-start(f32[3,192,192]{2,1,0:T(8,128)} %get-tuple-element.56) | copy-start | bytes 1327108
  201.7 5.5 %copy-start = (bf16[2,2,528,256]{3,2,1,0:T(8,128)(2,1)S(1)}, bf16[2,2,528,256]{3,2,1,0:T(8,128)(2,1)}, u32[]{:S(2)}) copy-start(bf16[2,2,528,256]{3,2,1,0:T(8,128)(2,1)} %get-tuple-element.54) | copy-start | bytes 3244036
  207.4 1.7 copy-start.8
  207.4 2.3 %copy-start.4 = (f32[192,192]{1,0:T(8,128)S(1)}, f32[192,192]{1,0:T(8,128)}, u32[]{:S(2)}) copy-start(f32[192,192]{1,0:T(8,128)} %get-tuple-element.104) | copy-start | bytes 442372
  207.4 3.0 %copy-start.2 = (f32[192,768]{1,0:T(8,128)S(1)}, f32[192,768]{1,0:T(8,128)}, u32[]{:S(2)}) copy-start(f32[192,768]{1,0:T(8,128)} %get-tuple-element.108) | copy-start | bytes 1769476
  207.5 3.8 %copy-start.1 = (f32[192,768]{1,0:T(8,128)S(1)}, f32[192,768]{1,0:T(8,128)}, u32[]{:S(2)}) copy-start(f32[192,768]{1,0:T(8,128)} %get-tuple-element.110) | copy-start | bytes 1769476
